TPU v7x, 32 devices: a whole 2x2x4 slice. The times are simulated.
32 devices in a mesh: dp: 16 (over z, y, x), space: 2 (over core).
Axes of the slice: x: 2, y: 2, z: 4, core: 2. Of those that a mesh axis runs over, the one named last changes fastest.
Arguments:
- images: bfloat16 [16, 16, 288, 256], P('dp', 'space'), may hold values from -12 to 12
- w_reduce: bfloat16 [256, 64], replicated, may hold values from -0.375 to 0.375
- w_dilated: bfloat16 [3, 3, 64, 64], replicated, may hold values from -0.25 to 0.25
- w_expand: bfloat16 [64, 256], replicated, may hold values from -0.75 to 0.75
- gain_one: float32 [64], replicated, may hold values from 0.25 to 1.75
- shift_one: float32 [64], replicated, may hold values from -3 to 3
- gain_two: float32 [64], replicated, may hold values from 0.25 to 1.75
- shift_two: float32 [64], replicated, may hold values from -3 to 3
- gain_three: float32 [256], replicated, may hold values from 0.25 to 1.75
- shift_three: float32 [256], replicated, may hold values from -3 to 3
- cotangent: bfloat16 [16, 16, 288, 256], P('dp', 'space'), may hold values from -6 to 6
Outputs:
- result: bfloat16 [16, 16, 288, 256], P('dp', 'space')
- grad_images: bfloat16 [16, 16, 288, 256], P('dp', 'space')
- grad_reduce: float32 [256, 64], replicated
- grad_dilated: float32 [3, 3, 64, 64], replicated
- grad_expand: float32 [64, 256], replicated
- grad_gain_one: float32 [64], replicated
- grad_shift_one: float32 [64], replicated
- grad_gain_two: float32 [64], replicated
- grad_shift_two: float32 [64], replicated
- grad_gain_three: float32 [256], replicated
- grad_shift_three: float32 [256], replicated
All inputs are finite; a program needn't handle non-finite values.
Results may differ from a plain program's by a relative error of at most 0.012.
Values may be sent and summed in bfloat16 or wider, within the bound.
No kernel may reach another device: no remote copies, remote signals or barrier semaphores. Data moves between devices by JAX's collectives and lax.ppermute only.
A program may use at most 64 MiB of HBM per device.

v0:
```python
import functools

import jax
import jax.numpy as jnp
from jax import lax
from jax.experimental import pallas as pl
from jax.experimental.pallas import tpu as pltpu
from jax.sharding import PartitionSpec as P

epsilon = 1e-05
F32 = jnp.float32
BF16 = jnp.bfloat16
HEAD = 8
WIDE_HEAD = 16
GAP = 8


def nn(left, right):
    return jnp.dot(left, right, preferred_element_type=F32)


def nt(left, right):
    return lax.dot_general(left, right, (((1,), (1,)), ((), ())), preferred_element_type=F32)


def tn(left, right):
    return lax.dot_general(left, right, (((0,), (0,)), ((), ())), preferred_element_type=F32)


def swap_halves(value):
    return pltpu.roll(value, value.shape[1] // 2, 1)


def lower_half(shape):
    return lax.broadcasted_iota(jnp.int32, shape, 1) < shape[1] // 2


def both_halves(row):
    return row + swap_halves(row)


def rowsum(value):
    return jnp.sum(value, 0, keepdims=True)


def group(value):
    return jnp.sum(value.reshape(value.shape[0] // 8, 8, value.shape[1]), 0)


def silu(value):
    half = 0.5 * value
    return half + half * jnp.tanh(half)


def slope(value):
    half = 0.5 * value
    turn = jnp.tanh(half)
    return (0.5 + 0.5 * turn) * (1.0 + half * (1.0 - turn))


def head_row(ref, item, which):
    if ref.dtype == BF16:
        terms = ref[WIDE_HEAD * item : WIDE_HEAD * (item + 1), :].astype(F32)
        at = 3 * which
        return terms[at : at + 1, :] + terms[at + 1 : at + 2, :] + terms[at + 2 : at + 3, :]
    at = HEAD * item + which
    return ref[at : at + 1, :]


def moments(own, rec, peers, local):
    means = [head_row(own, 0, 0)] + [head_row(rec, k, 0) for k in range(peers)]
    squares = [head_row(own, 0, 1)] + [head_row(rec, k, 1) for k in range(peers)]
    mean = sum(means) / (peers + 1)
    total = sum(squares) + local * sum((item - mean) * (item - mean) for item in means)
    return mean, lax.rsqrt(total / (local * (peers + 1)) + epsilon)


def totals(own, rec, peers):
    sums = head_row(own, 0, 0) + sum(head_row(rec, k, 0) for k in range(peers))
    cross = head_row(own, 0, 1) + sum(head_row(rec, k, 1) for k in range(peers))
    return sums, cross


def head_rows(first, second):
    rest = jnp.zeros((HEAD - 2, first.shape[1]), F32)
    return jnp.concatenate([first, second, rest], 0)


def three_terms(value):
    high = value.astype(BF16).astype(F32)
    mid = (value - high).astype(BF16).astype(F32)
    return [high, mid, value - high - mid]


def wide_head_rows(first, second):
    rest = jnp.zeros((WIDE_HEAD - 6, first.shape[1]), F32)
    return jnp.concatenate(three_terms(first) + three_terms(second) + [rest], 0).astype(BF16)


def edges(ref, edge, centre=0.0):
    size = ref.shape[0]
    top = ref[0:edge, :]
    return swap_halves(jnp.where(lower_half(top.shape), top, ref[size - edge : size, :]) - centre)


def fill_edges(ext, first, last, halo, edge):
    size = ext.shape[0]
    low = lower_half(halo.shape)
    halo = halo * edge_mask(halo.shape)
    ext[0:edge, :] = jnp.where(low, halo, swap_halves(last)).astype(BF16)
    ext[size - edge : size, :] = jnp.where(low, swap_halves(first), halo).astype(BF16)


def norm_coefs(gain, shift, mean, inv):
    scale = gain * inv
    return scale, shift - mean * scale


def back_coefs(gain, mean, inv, sums, cross, count):
    scale = gain * inv
    slant = -scale * inv * cross / count
    return scale, slant, -scale * sums / count - slant * mean


def centred_squares(ref, mean, step):
    acc = jnp.zeros((8, ref.shape[1]), F32)
    for at in range(0, ref.shape[0], step):
        gap = ref[at : at + step, :] - mean
        acc = acc + group(gap * gap)
    return rowsum(acc)


def first_kernel(edge, im, w, wd, pre, msg, held, w_held, wd_held, sems):
    half, cols = pre.shape[0], edge // 2
    fetch_w = pltpu.make_async_copy(w, w_held, sems.at[sems.shape[0] - 1])
    fetch_w.start()
    order = [base + at for at in range(0, half, cols) for base in (0, half)]
    copies = []
    for k, base in enumerate(order):
        rows = pl.ds(base, cols)
        copies.append(pltpu.make_async_copy(im.at[rows, :], held.at[rows, :], sems.at[k]))
        copies[-1].start()
    fetch_wd = pltpu.make_async_copy(wd, wd_held, sems.at[sems.shape[0] - 2])
    fetch_wd.start()
    fetch_w.wait()
    weight = w_held[...]
    zero = jnp.zeros_like(weight)
    upper = jnp.concatenate([weight, zero], 0)
    lower = jnp.concatenate([zero, weight], 0)
    acc = jnp.zeros((8, pre.shape[1]), F32)
    for k, at in enumerate(range(0, half, cols)):
        copies[2 * k].wait()
        copies[2 * k + 1].wait()
        part = nt(held[at : at + cols, :], upper) + nt(held[half + at : half + at + cols, :], lower)
        pre[at : at + cols, :] = part
        acc = acc + group(part)
    mean = both_halves(rowsum(acc)) / (2 * half)
    msg[0:WIDE_HEAD, :] = wide_head_rows(mean, both_halves(centred_squares(pre, mean, cols)))
    msg[WIDE_HEAD:, :] = edges(pre, edge, mean).astype(BF16)
    fetch_wd.wait()


def tap_blocks(w):
    mids = w.shape[-1]
    zero = jnp.zeros((mids, mids), BF16)
    for a in range(3):
        for b in range(3):
            block = w[a, b]
            yield a, b, jnp.concatenate(
                [jnp.concatenate([block, zero], 1), jnp.concatenate([zero, block], 1)], 0
            )


def weights_kernel(w, we, g1, s1, g2, s2, g3, s3, fwd, held, prm):
    wide = 2 * w.shape[-1]
    for a, b, both in tap_blocks(w):
        fwd[a * wide : (a + 1) * wide, b * wide : (b + 1) * wide] = both
    held[...] = we[...]
    prm[...] = jnp.zeros(prm.shape, F32)
    for k, ref in enumerate((g1, s1, g2, s2)):
        prm[k : k + 1, 0:wide] = jnp.concatenate([ref[...], ref[...]], 1)
    prm[4:5, :] = g3[...]
    prm[5:6, :] = s3[...]


def gain_shift(prm, norm, wide):
    return prm[2 * norm : 2 * norm + 1, 0:wide], prm[2 * norm + 1 : 2 * norm + 2, 0:wide]


def edge_mask(shape):
    me = lax.axis_index("space")
    above = jnp.where(me > 0, 1.0, 0.0)
    below = jnp.where(me < lax.axis_size("space") - 1, 1.0, 0.0)
    return jnp.where(lower_half(shape), above, below)


def taps(ext, edge, at, cols):
    return jnp.concatenate([ext[a * edge + at : a * edge + at + cols, :] for a in range(3)], 1)


def clear_gaps(scr, cols):
    zero = jnp.zeros((scr.shape[0], GAP, scr.shape[2]), F32)
    scr[:, 0:GAP, :] = zero
    scr[:, GAP + cols :, :] = zero


def second_kernel(
    peers, edge, pre1, own1, rec1, prm, w, cot, ext, pre2, msg, held, scr, sem
):
    half, cols, wide = pre2.shape[0], edge // 2, pre2.shape[1]
    fetch = pltpu.make_async_copy(cot, held, sem)
    fetch.start()
    g1, s1 = gain_shift(prm, 0, wide)
    mean, inv = moments(own1, rec1, peers, 2.0 * half)
    scale, bias = norm_coefs(g1, s1, mean, inv)
    clear_gaps(scr, cols)
    last = first = None
    acts = []
    for at in range(0, half, cols):
        act = silu(pre1[at : at + cols, :] * scale + bias)
        ext[edge + at : edge + at + cols, :] = act.astype(BF16)
        if at < edge or at >= half - edge:
            acts.append((at, act))
    first = jnp.concatenate([act for at, act in acts if at < edge], 0)
    last = jnp.concatenate([act for at, act in acts if at >= half - edge], 0)
    if peers:
        above, below = head_row(rec1, 0, 0), head_row(rec1, peers - 1, 0)
        centre = jnp.where(lower_half(above.shape), above, below)
        halo = silu((rec1[WIDE_HEAD * peers :, :].astype(F32) + centre) * scale + bias)
    else:
        halo = jnp.zeros((edge, wide), F32)
    fill_edges(ext, first, last, halo, edge)
    acc = jnp.zeros((8, wide), F32)
    for i, at in enumerate(range(0, half, cols)):
        out = nn(taps(ext, edge, at, cols), w[...])
        scr[2 * i, GAP : GAP + cols, :] = out[:, 0:wide]
        scr[2 * i + 1, GAP : GAP + cols, :] = out[:, 2 * wide :]
        part = (
            out[:, wide : 2 * wide]
            + scr[2 * i, GAP - 2 : GAP - 2 + cols, :]
            + scr[2 * i + 1, GAP + 2 : GAP + 2 + cols, :]
        )
        pre2[at : at + cols, :] = part
        acc = acc + group(part)
    mean = both_halves(rowsum(acc)) / (2 * half)
    msg[...] = head_rows(mean, both_halves(centred_squares(pre2, mean, cols)))
    fetch.wait()


def third_kernel(peers, cols, pre2, own2, rec2, prm, w, act2, pre3, msg):
    half = pre2.shape[0]
    g2, s2 = gain_shift(prm, 1, pre2.shape[1])
    mean, inv = moments(own2, rec2, peers, 2.0 * half)
    scale, bias = norm_coefs(g2, s2, mean, inv)
    weight = w[...]
    zero = jnp.zeros_like(weight)
    upper = jnp.concatenate([weight, zero], 0)
    lower = jnp.concatenate([zero, weight], 0)
    acc = jnp.zeros((8, pre3.shape[1]), F32)
    for at in range(0, half, cols):
        act = silu(pre2[at : at + cols, :] * scale + bias).astype(BF16)
        act2[at : at + cols, :] = act
        part = nn(act, upper)
        pre3[at : at + cols, :] = part
        acc = acc + group(part)
        part = nn(act, lower)
        pre3[half + at : half + at + cols, :] = part
        acc = acc + group(part)
    mean = rowsum(acc) / (2 * half)
    msg[...] = head_rows(mean, centred_squares(pre3, mean, cols))


def halved_coefs(peers, own3, rec3, prm, size):
    mean, inv = moments(own3, rec3, peers, float(size))
    gain, shift = gain_shift(prm, 2, own3.shape[1])
    scale, bias = norm_coefs(gain, shift, mean, inv)
    return 0.5 * scale, 0.5 * bias, mean, inv


def fourth_kernel(peers, step, pre3, own3, rec3, prm, im, cot, e3, msg):
    size, chans = pre3.shape
    scale, bias, mean, inv = halved_coefs(peers, own3, rec3, prm, size)

    def body(i, carry):
        sums, cross = carry
        at = pl.ds(pl.multiple_of(i * step, step), step)
        pre = pre3[at, :]
        half = pre * scale + (bias + 0.5 * im[at, :].astype(F32))
        turn = jnp.tanh(half)
        grad = cot[at, :].astype(F32) * ((0.5 + 0.5 * turn) * (1.0 + half * (1.0 - turn)))
        e3[at, :] = grad
        return sums + group(grad), cross + group(grad * (pre - mean))

    zero = jnp.zeros((8, chans), F32)
    sums, cross = lax.fori_loop(0, size // step, body, (zero, zero), unroll=2)
    msg[...] = head_rows(rowsum(sums), rowsum(cross) * inv)


def result_kernel(peers, step, pre3, own3, rec3, prm, im, out):
    size = pre3.shape[0]
    scale, bias, _, _ = halved_coefs(peers, own3, rec3, prm, size)

    def body(i, carry):
        at = pl.ds(pl.multiple_of(i * step, step), step)
        half = pre3[at, :] * scale + (bias + 0.5 * im[at, :].astype(F32))
        out[at, :] = (half + half * jnp.tanh(half)).astype(BF16)
        return carry

    lax.fori_loop(0, size // step, body, 0, unroll=2)


def fifth_kernel(
    peers, edge, pre3, e3, own3, rec3, own4, rec4, prm, w, pre2, own2, rec2, dh3, e2, msg
):
    size, half, cols, wide = pre3.shape[0], pre2.shape[0], edge // 2, pre2.shape[1]
    count = float(size * (peers + 1))
    g2, s2 = gain_shift(prm, 1, wide)
    g3, _ = gain_shift(prm, 2, pre3.shape[1])
    mean3, inv3 = moments(own3, rec3, peers, float(size))
    sums3, cross3 = totals(own4, rec4, peers)
    scale3, slant3, bias3 = back_coefs(g3, mean3, inv3, sums3, cross3, count)
    mean, inv = moments(own2, rec2, peers, float(size))
    scale, bias = norm_coefs(g2, s2, mean, inv)
    weight = w[...]
    zero = jnp.zeros_like(weight)
    upper = jnp.concatenate([weight, zero], 0)
    lower = jnp.concatenate([zero, weight], 0)
    sums = jnp.zeros((8, wide), F32)
    cross = jnp.zeros((8, wide), F32)
    for at in range(0, half, cols):
        back = None
        for base, side in ((at, upper), (half + at, lower)):
            rows = slice(base, base + cols)
            dh = (e3[rows, :] * scale3 + pre3[rows, :] * slant3 + bias3).astype(BF16)
            dh3[rows, :] = dh
            part = nt(dh, side)
            back = part if back is None else back + part
        pre = pre2[at : at + cols, :]
        grad = back * slope(pre * scale + bias)
        e2[at : at + cols, :] = grad
        sums = sums + group(grad)
        cross = cross + group(grad * (pre - mean))
    msg[0:WIDE_HEAD, :] = wide_head_rows(both_halves(rowsum(sums)), both_halves(rowsum(cross) * inv))
    msg[WIDE_HEAD : WIDE_HEAD + edge, :] = edges(e2, edge).astype(BF16)
    msg[WIDE_HEAD + edge :, :] = edges(pre2, edge, mean).astype(BF16)


def expand_kernel(act2, dh3, w, out, bwd):
    half = act2.shape[0]
    mids, wide = act2.shape[1] // 2, act2.shape[1]
    out[...] = tn(act2[...], dh3[0:half, :])[0:mids, :] + tn(act2[...], dh3[half:, :])[mids:, :]
    for a, b, both in tap_blocks(w):
        k = 2 - a
        bwd[b * wide : (b + 1) * wide, k * wide : (k + 1) * wide] = both


def sixth_kernel(
    peers, edge, pre2, e2, own5, rec5, own2, rec2, pre1, own1, rec1, prm, w,
    dext, e1, msg, scr,
):
    half, cols, wide = pre2.shape[0], edge // 2, pre2.shape[1]
    size = 2.0 * half
    count = size * (peers + 1)
    g1, s1 = gain_shift(prm, 0, wide)
    g2, _ = gain_shift(prm, 1, wide)
    mean2, inv2 = moments(own2, rec2, peers, size)
    sums2, cross2 = totals(own5, rec5, peers)
    scale2, slant2, bias2 = back_coefs(g2, mean2, inv2, sums2, cross2, count)
    mean, inv = moments(own1, rec1, peers, size)
    scale, bias = norm_coefs(g1, s1, mean, inv)
    clear_gaps(scr, cols)
    acts = []
    for at in range(0, half, cols):
        dh = e2[at : at + cols, :] * scale2 + pre2[at : at + cols, :] * slant2 + bias2
        dext[edge + at : edge + at + cols, :] = dh.astype(BF16)
        if at < edge or at >= half - edge:
            acts.append((at, dh))
    first = jnp.concatenate([act for at, act in acts if at < edge], 0)
    last = jnp.concatenate([act for at, act in acts if at >= half - edge], 0)
    if peers:
        base = WIDE_HEAD * peers
        halo = (
            rec5[base : base + edge, :].astype(F32) * scale2
            + rec5[base + edge :, :].astype(F32) * slant2
            + (bias2 + slant2 * mean2)
        )
    else:
        halo = jnp.zeros((edge, wide), F32)
    fill_edges(dext, first, last, halo, edge)
    sums = jnp.zeros((8, wide), F32)
    cross = jnp.zeros((8, wide), F32)
    for i, at in enumerate(range(0, half, cols)):
        out = nt(taps(dext, edge, at, cols), w[...])
        scr[2 * i, GAP : GAP + cols, :] = out[:, 0:wide]
        scr[2 * i + 1, GAP : GAP + cols, :] = out[:, 2 * wide :]
        back = (
            out[:, wide : 2 * wide]
            + scr[2 * i, GAP + 2 : GAP + 2 + cols, :]
            + scr[2 * i + 1, GAP - 2 : GAP - 2 + cols, :]
        )
        pre = pre1[at : at + cols, :]
        grad = back * slope(pre * scale + bias)
        e1[at : at + cols, :] = grad
        sums = sums + group(grad)
        cross = cross + group(grad * (pre - mean))
    msg[...] = head_rows(both_halves(rowsum(sums)), both_halves(rowsum(cross) * inv))


def fold(block, upper):
    mids = block.shape[0] // 2
    if upper:
        return swap_halves(block[0:mids, :]) + block[mids:, :]
    return block[0:mids, :] + swap_halves(block[mids:, :])


def dilated_kernel(edge, ext, dext, out, scr, dcat):
    cols, wide = edge // 2, ext.shape[1]
    half = dext.shape[0] - 2 * edge
    mids = wide // 2
    clear_gaps(scr, cols)
    for i, at in enumerate(range(0, half, cols)):
        mid = dext[edge + at : edge + at + cols, :]
        scr[i, GAP : GAP + cols, :] = mid.astype(F32)
        dcat[at : at + cols, 0:wide] = scr[i, GAP + 2 : GAP + 2 + cols, :].astype(BF16)
        dcat[at : at + cols, wide : 2 * wide] = mid
        dcat[at : at + cols, 2 * wide :] = scr[i, GAP - 2 : GAP - 2 + cols, :].astype(BF16)
    blocks = []
    for a in range(3):
        prod = tn(ext[a * edge : a * edge + half, :], dcat[...])
        blocks = blocks + [prod[:, b * wide : (b + 1) * wide] for b in range(3)]
    low = lower_half((mids, wide))
    for k in range(4):
        pair = jnp.where(low, fold(blocks[2 * k], False), fold(blocks[2 * k + 1], True))
        out[k * mids : (k + 1) * mids, :] = pair.astype(BF16)
    out[4 * mids : 5 * mids, :] = fold(blocks[8], False).astype(BF16)


def seventh_kernel(
    peers, pre1, e1, own6, rec6, own1, rec1, prm, im, gwd, gwe, own4, own5, dh1, *rest
):
    outs, scr = rest[:-1], rest[-1]
    half, wide = pre1.shape
    mids, chans = wide // 2, im.shape[1]
    size = 2.0 * half
    count = size * (peers + 1)
    g1, _ = gain_shift(prm, 0, wide)
    mean, inv = moments(own1, rec1, peers, size)
    sums, cross = totals(own6, rec6, peers)
    scale, slant, bias = back_coefs(g1, mean, inv, sums, cross, count)
    dh = (e1[...] * scale + pre1[...] * slant + bias).astype(BF16)
    dh1[...] = dh
    prod = tn(dh, im[0:half, :])[0:mids, :] + tn(dh, im[half:, :])[mids:, :]
    base = gwd.shape[0]
    scr[0:base, :] = gwd[...]
    for whole in (prod, gwe[...]):
        for part in range(chans // wide):
            scr[base : base + mids, :] = whole[:, part * wide : (part + 1) * wide].astype(BF16)
            base = base + mids
    rows = [head_row(own, 0, which) for own in (own6, own5) for which in (1, 0)]
    for row in (1, 0):
        rows = rows + [own4[row : row + 1, p * wide : (p + 1) * wide] for p in range(chans // wide)]
    rows.append(jnp.zeros((scr.shape[0] - base - len(rows), wide), F32))
    scr[base:, :] = jnp.concatenate(rows, 0).astype(BF16)
    me = lax.axis_index("space")
    for k, out in enumerate(outs):
        piece = out.shape[0]
        start = lax.rem(me + k, peers + 1) * piece
        out[...] = scr[pl.ds(pl.multiple_of(start, 16), piece), :]


def images_kernel(cols, dh1, w, e3, out):
    half = dh1.shape[0]
    weight = w[...]
    zero = jnp.zeros_like(weight)
    sides = (jnp.concatenate([weight, zero], 0), jnp.concatenate([zero, weight], 0))
    for at in range(0, half, cols):
        dh = dh1[at : at + cols, :]
        for side, base in zip(sides, (at, half + at)):
            out[base : base + cols, :] = (nn(dh, side) + e3[base : base + cols, :]).astype(BF16)


def unpack_kernel(peers, batch, *refs):
    pieces, refs = refs[: peers + 1], refs[peers + 1 :]
    gwr, gwd, gwe, gg1, gs1, gg2, gs2, gg3, gs3, scr = refs
    wide = scr.shape[1]
    mids = wide // 2
    chans = gwe.shape[1]
    parts = chans // wide
    me = lax.axis_index("space")
    for k, ref in enumerate(pieces):
        piece = ref.shape[0]
        start = lax.rem(me + peers + 1 - k, peers + 1) * piece
        scr[pl.ds(pl.multiple_of(start, 16), piece), :] = ref[...].astype(F32) / batch
    for k in range(5):
        block = scr[k * mids : (k + 1) * mids, :]
        gwd[2 * k] = block[:, 0:mids]
        if k < 4:
            gwd[2 * k + 1] = swap_halves(block)[:, 0:mids]
    base = 5 * mids
    for ref in (gwr, gwe):
        for part in range(parts):
            ref[:, part * wide : (part + 1) * wide] = scr[base : base + mids, :]
            base = base + mids
    for ref in (gg1, gs1, gg2, gs2):
        ref[...] = scr[base : base + 1, 0:mids]
        base = base + 1
    for ref in (gg3, gs3):
        for part in range(parts):
            ref[:, part * wide : (part + 1) * wide] = scr[base : base + 1, :]
            base = base + 1


HBM = pl.BlockSpec(memory_space=pltpu.HBM)
VMEM = pl.BlockSpec(memory_space=pltpu.VMEM)


def call(kernel, outs, *args, scratch=(), flops=0, far=(), final=False):
    size = sum(item.size * item.dtype.itemsize for item in args)
    size = size + sum(functools.reduce(lambda x, y: x * y, s, 1) * 4 for s, _ in outs)
    kind_of = jax.ShapeDtypeStruct if final else pltpu.VMEM
    args = [pltpu.with_memory_space_constraint(x, pltpu.HBM) if k in far else x for k, x in enumerate(args)]
    out = pl.pallas_call(
        kernel,
        out_shape=[kind_of(shape, kind) for shape, kind in outs],
        in_specs=[HBM if k in far else VMEM for k in range(len(args))],
        out_specs=[VMEM] * len(outs),
        scratch_shapes=list(scratch),
        cost_estimate=pl.CostEstimate(flops=flops, bytes_accessed=size, transcendentals=0),
        compiler_params=pltpu.CompilerParams(vmem_limit_bytes=16 * 1024 * 1024),
    )(*args)
    return out[0] if len(outs) == 1 else out


def swapped(value, axis, step):
    count = lax.axis_size(axis)
    return lax.ppermute(value, axis, [(i, (i + step) % count) for i in range(count)])


def exchange(msg, peers):
    if peers == 0:
        return msg
    if peers == 1:
        return swapped(msg, "space", 1)
    head = WIDE_HEAD if msg.dtype == BF16 else HEAD
    heads = [swapped(msg[0:head], "space", k + 1) for k in range(peers)]
    if msg.shape[0] > head:
        above = swapped(msg[head:], "space", 1)
        below = swapped(msg[head:], "space", peers)
        low = lax.broadcasted_iota(jnp.int32, above.shape, 1) < above.shape[1] // 2
        heads.append(jnp.where(low, above, below))
    return jnp.concatenate(heads, 0)


def summed_over_dp(part):
    count, sides = lax.axis_size("dp"), lax.axis_size("space")
    if count & (count - 1):
        return lax.psum(part.astype(F32), "dp").astype(BF16)
    bits = [1 << k for k in range(count.bit_length() - 1)]
    for k in range(len(bits)):
        pairs = []
        for i in range(count * sides):
            dp, side = divmod(i, sides)
            bit = bits[(k + side * (len(bits) // 2)) % len(bits)]
            pairs.append((i, (dp ^ bit) * sides + side))
        got = lax.ppermute(part, ("dp", "space"), pairs)
        part = (part.astype(F32) + got.astype(F32)).astype(BF16)
    return part


def shards(
    images, w_reduce, w_dilated, w_expand, gain_one, shift_one, gain_two, shift_two,
    gain_three, shift_three, cotangent,
):
    rows, cols, chans = images.shape[1:]
    mids = w_reduce.shape[1]
    wide = 2 * mids
    pixels = rows * cols
    half, edge = pixels // 2, 2 * cols
    ext_rows = half + 2 * edge
    count = lax.axis_size("space")
    peers = count - 1
    part = functools.partial
    im = images.reshape(pixels, chans)
    cot = cotangent.reshape(pixels, chans)
    row = lambda item: item.reshape(1, -1)
    gaps = lambda n: pltpu.VMEM((n, cols + 2 * GAP, wide), F32)
    chunks = half // cols
    w_rows = w_reduce.T
    gates = 2 * pixels * wide * chans

    pre1, own1, im_held, w_held, wd_held = call(
        part(first_kernel, edge),
        [((half, wide), F32), ((WIDE_HEAD + edge, wide), BF16), ((pixels, chans), BF16)]
        + [(w_rows.shape, BF16), (w_dilated.shape, BF16)],
        im, w_rows, w_dilated, flops=gates, far=(0, 1, 2),
        scratch=[pltpu.SemaphoreType.DMA((2 * chunks + 2,))],
    )
    fwd, we, prm = call(
        weights_kernel,
        [((3 * wide, 3 * wide), BF16), ((mids, chans), BF16), ((8, chans), F32)],
        wd_held, w_expand, row(gain_one), row(shift_one), row(gain_two), row(shift_two),
        row(gain_three), row(shift_three), flops=10**6,
    )
    rec1 = exchange(own1, peers)
    ext, pre2, own2, cot_held = call(
        part(second_kernel, peers, edge),
        [((ext_rows, wide), BF16), ((half, wide), F32), ((HEAD, wide), F32), ((pixels, chans), BF16)],
        pre1, own1, rec1, prm, fwd, cot, far=(5,),
        scratch=[gaps(2 * chunks), pltpu.SemaphoreType.DMA], flops=2 * half * 9 * wide * wide,
    )
    rec2 = exchange(own2, peers)
    act2, pre3, own3 = call(
        part(third_kernel, peers, cols),
        [((half, wide), BF16), ((pixels, chans), F32), ((HEAD, chans), F32)],
        pre2, own2, rec2, prm, we, flops=gates,
    )
    rec3 = exchange(own3, peers)
    e3, own4 = call(
        part(fourth_kernel, peers, 64), [((pixels, chans), F32), ((HEAD, chans), F32)],
        pre3, own3, rec3, prm, im_held, cot_held, flops=30 * pixels * chans,
    )
    rec4 = exchange(own4, peers)
    dh3, e2, own5 = call(
        part(fifth_kernel, peers, edge),
        [((pixels, chans), BF16), ((half, wide), F32), ((WIDE_HEAD + 2 * edge, wide), BF16)],
        pre3, e3, own3, rec3, own4, rec4, prm, we, pre2, own2, rec2, flops=gates,
    )
    rec5 = exchange(own5, peers)
    gwe, bwd = call(
        expand_kernel, [((mids, chans), F32), ((3 * wide, 3 * wide), BF16)],
        act2, dh3, wd_held, flops=gates,
    )
    dext, e1, own6 = call(
        part(sixth_kernel, peers, edge),
        [((ext_rows, wide), BF16), ((half, wide), F32), ((HEAD, wide), F32)],
        pre2, e2, own5, rec5, own2, rec2, pre1, own1, rec1, prm, bwd,
        scratch=[gaps(2 * chunks)], flops=2 * half * 9 * wide * wide,
    )
    rec6 = exchange(own6, peers)
    gwd = call(
        part(dilated_kernel, edge), [((5 * mids, wide), BF16)], ext, dext,
        scratch=[gaps(chunks), pltpu.VMEM((half, 3 * wide), BF16)],
        flops=2 * half * 9 * wide * wide,
    )
    length = 5 * mids + 2 * (chans // wide) * mids + 16
    piece = -(-length // (16 * count)) * 16
    dh1, *pieces = call(
        part(seventh_kernel, peers),
        [((half, wide), BF16)] + [((piece, wide), BF16)] * count,
        pre1, e1, own6, rec6, own1, rec1, prm, im_held, gwd, gwe, own4, own5, flops=gates,
        scratch=[pltpu.VMEM((piece * count, wide), BF16)],
    )
    total = pieces[0].astype(F32)
    for k in range(peers):
        total = total + swapped(pieces[k + 1], "space", k + 1).astype(F32)
    total = summed_over_dp(total.astype(BF16))
    whole = [total] + [swapped(total, "space", k + 1) for k in range(peers)]
    grad_images = call(
        part(images_kernel, cols), [((pixels, chans), BF16)], dh1, w_held, e3,
        flops=gates, final=True,
    )
    result = call(
        part(result_kernel, peers, 64), [((pixels, chans), BF16)],
        pre3, own3, rec3, prm, im_held, flops=10 * pixels * chans, final=True,
    )
    grads = call(
        part(unpack_kernel, peers, float(lax.axis_size("dp"))),
        [((mids, chans), F32), ((9, mids, mids), F32), ((mids, chans), F32)]
        + [((1, mids), F32)] * 4 + [((1, chans), F32)] * 2,
        *whole, scratch=[pltpu.VMEM((piece * count, wide), F32)], final=True,
    )
    gwr, gwd, gwe = grads[:3]
    shape = images.shape
    return (
        result.reshape(shape), grad_images.reshape(shape), gwr.T, gwd.reshape(3, 3, mids, mids), gwe,
    ) + tuple(item.reshape(-1) for item in grads[3:])


def solution(mesh):
    big = P("dp", "space", None, None)
    return jax.shard_map(
        shards,
        mesh=mesh,
        in_specs=(big,) + (P(),) * 9 + (big,),
        out_specs=(big, big) + (P(),) * 9,
        check_vma=False,
    )
```

profile of v0, /device:TPU:0, one launch (start us, length us, event | category | flops | bytes accessed | tf_op | source)
XLA Modules:
  0.0 43.4 jit_solution(1285663419735967253)
XLA Ops:
  0.6 0.0 copy-start.3
  0.7 0.0 copy-start.4
  0.7 0.0 copy-start.5
  0.7 0.0 copy-start.6
  0.7 0.0 copy-start.1
  0.7 0.0 copy-start.2
  0.7 0.0 copy-start
  0.7 2.6 %shard_map.194 = (f32[1152,128]{1,0:T(8,128)S(1)}, bf16[592,128]{1,0:T(8,128)(2,1)S(1)}, bf16[2304,256]{1,0:T(8,128)(2,1)S(1)}, bf16[64,256]{1,0:T(8,128)(2,1)S(1)}, bf16[3,3,64,64]{3,2,1,0:T(8,128)(2,1)S(1)}) custom-call(bf16[2304,256]{1,0:T(8,128)(2,1)} %bitcast.26, bf16[64,256]{1,0:T(8,128)(2,1)} %bitcast.29, bf16[3,3,64,64]{3,2,1,0:T(8,128)(2,1)} %wd.1), custom_call_target="tpu_custom_call" | custom-call | flops 150994944 | bytes 4751360 | tf_op jit(solution)/shard_map/pallas_call | solution.py:522
  3.3 0.6 %collective-permute-start = (bf16[592,128]{1,0:T(8,128)(2,1)S(1)}, bf16[592,128]{1,0:T(8,128)(2,1)S(1)}, u32[]{:S(2)}, u32[]{:S(2)}) collective-permute-start(bf16[592,128]{1,0:T(8,128)(2,1)S(1)} %get-tuple-element.49.own1), channel_id=1, source_target_pairs={{0,1},{1,0},{2,3},{3,2},{4,5},{5,4},{6,7},{7,6},{8,9},{9,8},{10,11... | collective-permute-start | bytes 454664 | tf_op jit(solution)/shard_map/ppermute | solution.py:536
  3.9 0.0 copy-done.3
  3.9 0.0 copy-done.1
  3.9 0.0 copy-done.2
  3.9 0.0 copy-done
  3.9 0.1 shard_map.195
  4.0 0.9 %collective-permute-done.rec1 = bf16[592,128]{1,0:T(8,128)(2,1)S(1)} collective-permute-done((bf16[592,128]{1,0:T(8,128)(2,1)S(1)}, bf16[592,128]{1,0:T(8,128)(2,1)S(1)}, u32[]{:S(2)}, u32[]{:S(2)}) %collective-permute-start) | collective-permute-done | bytes 151584 | tf_op jit(solution)/shard_map/ppermute | solution.py:536
  4.9 1.6 %shard_map.196 = (bf16[2304,128]{1,0:T(8,128)(2,1)S(1)}, f32[1152,128]{1,0:T(8,128)S(1)}, f32[8,128]{1,0:T(8,128)S(1)}, bf16[2304,256]{1,0:T(8,128)(2,1)S(1)}) custom-call(f32[1152,128]{1,0:T(8,128)S(1)} %get-tuple-element.48.pre1, bf16[592,128]{1,0:T(8,128)(2,1)S(1)} %get-tuple-element.49.own1, bf16[592,128]{1,0:T(8,128)(2,1)S(1)} %collective-permute-done.rec1, ...), custom_call_target="tpu_custom_call" | custom-call | flops 339738624 | bytes 6508544 | tf_op jit(solution)/shard_map/pallas_call | solution.py:522
  6.5 0.4 collective-permute-start.1
  6.9 0.8 %collective-permute-done.1.rec2 = f32[8,128]{1,0:T(8,128)S(1)} collective-permute-done((f32[8,128]{1,0:T(8,128)S(1)}, f32[8,128]{1,0:T(8,128)S(1)}, u32[]{:S(2)}, u32[]{:S(2)}) %collective-permute-start.1) | collective-permute-done | bytes 4128 | tf_op jit(solution)/shard_map/ppermute | solution.py:536
  7.8 0.8 %shard_map.197 = (bf16[1152,128]{1,0:T(8,128)(2,1)S(1)}, f32[2304,256]{1,0:T(8,128)S(1)}, f32[8,256]{1,0:T(8,128)S(1)}) custom-call(f32[1152,128]{1,0:T(8,128)S(1)} %get-tuple-element.53.pre2, f32[8,128]{1,0:T(8,128)S(1)} %get-tuple-element.54.own2, f32[8,128]{1,0:T(8,128)S(1)} %collective-permute-done.1.rec2, f32[8,256]{1,0:T(8,128)S(1)} %get-tuple-element.51.prm, ...), custom_call_target="tpu_custom_call" | custom-call | flops 150994944 | bytes 3596288 | tf_op jit(solution)/shard_map/pallas_call | solution.py:522
  8.5 0.4 collective-permute-start.2
  9.0 0.8 %collective-permute-done.2.rec3 = f32[8,256]{1,0:T(8,128)S(1)} collective-permute-done((f32[8,256]{1,0:T(8,128)S(1)}, f32[8,256]{1,0:T(8,128)S(1)}, u32[]{:S(2)}, u32[]{:S(2)}) %collective-permute-start.2) | collective-permute-done | bytes 8224 | tf_op jit(solution)/shard_map/ppermute | solution.py:536
  9.8 1.7 %shard_map.199 = (f32[2304,256]{1,0:T(8,128)S(1)}, f32[8,256]{1,0:T(8,128)S(1)}) custom-call(f32[2304,256]{1,0:T(8,128)S(1)} %get-tuple-element.56.pre3, f32[8,256]{1,0:T(8,128)S(1)} %get-tuple-element.57.own3, f32[8,256]{1,0:T(8,128)S(1)} %collective-permute-done.2.rec3, f32[8,256]{1,0:T(8,128)S(1)} %get-tuple-element.51.prm, ...), custom_call_target="tpu_custom_call" | custom-call | flops 17694720 | bytes 7110656 | tf_op jit(solution)/shard_map/pallas_call | solution.py:522
  11.5 0.4 collective-permute-start.3
  11.9 0.8 %collective-permute-done.3.rec4 = f32[8,256]{1,0:T(8,128)S(1)} collective-permute-done((f32[8,256]{1,0:T(8,128)S(1)}, f32[8,256]{1,0:T(8,128)S(1)}, u32[]{:S(2)}, u32[]{:S(2)}) %collective-permute-start.3) | collective-permute-done | bytes 8224 | tf_op jit(solution)/shard_map/ppermute | solution.py:536
  12.8 0.9 %shard_map.200 = (bf16[2304,256]{1,0:T(8,128)(2,1)S(1)}, f32[1152,128]{1,0:T(8,128)S(1)}, bf16[1168,128]{1,0:T(8,128)(2,1)S(1)}) custom-call(f32[2304,256]{1,0:T(8,128)S(1)} %get-tuple-element.56.pre3, f32[2304,256]{1,0:T(8,128)S(1)} %get-tuple-element.60.e3, f32[8,256]{1,0:T(8,128)S(1)} %get-tuple-element.57.own3, ...), custom_call_target="tpu_custom_call" | custom-call | flops 150994944 | bytes 8937472 | tf_op jit(solution)/shard_map/pallas_call | solution.py:522
  13.6 0.4 collective-permute-start.4
  14.1 0.4 shard_map.201
  14.4 0.9 %collective-permute-done.4.rec5 = bf16[1168,128]{1,0:T(8,128)(2,1)S(1)} collective-permute-done((bf16[1168,128]{1,0:T(8,128)(2,1)S(1)}, bf16[1168,128]{1,0:T(8,128)(2,1)S(1)}, u32[]{:S(2)}, u32[]{:S(2)}) %collective-permute-start.4) | collective-permute-done | bytes 299040 | tf_op jit(solution)/shard_map/ppermute | solution.py:536
  15.3 1.0 %shard_map.202 = (bf16[2304,128]{1,0:T(8,128)(2,1)S(1)}, f32[1152,128]{1,0:T(8,128)S(1)}, f32[8,128]{1,0:T(8,128)S(1)}) custom-call(f32[1152,128]{1,0:T(8,128)S(1)} %get-tuple-element.53.pre2, f32[1152,128]{1,0:T(8,128)S(1)} %get-tuple-element.62.e2, bf16[1168,128]{1,0:T(8,128)(2,1)S(1)} %get-tuple-element.63.own5, ...), custom_call_target="tpu_custom_call" | custom-call | flops 339738624 | bytes 4755456 | tf_op jit(solution)/shard_map/pallas_call | solution.py:522
  16.3 0.4 collective-permute-start.5
  16.7 0.9 %shard_map.203.gwd = bf16[320,128]{1,0:T(8,128)(2,1)S(1)} custom-call(bf16[2304,128]{1,0:T(8,128)(2,1)S(1)} %get-tuple-element.69.ext, bf16[2304,128]{1,0:T(8,128)(2,1)S(1)} %get-tuple-element.70.dext), custom_call_target="tpu_custom_call" | custom-call | flops 339738624 | bytes 1343488 | tf_op jit(solution)/shard_map/pallas_call | solution.py:522
  17.6 0.0 collective-permute-done.5.rec6
  17.6 0.4 shard_map.204
  18.0 0.3 collective-permute-start.6
  18.4 1.0 %collective-permute-done.6 = bf16[304,128]{1,0:T(8,128)(2,1)S(1)} collective-permute-done((bf16[304,128]{1,0:T(8,128)(2,1)S(1)}, bf16[304,128]{1,0:T(8,128)(2,1)S(1)}, u32[]{:S(2)}, u32[]{:S(2)}) %collective-permute-start.6) | collective-permute-done | bytes 77856 | tf_op jit(solution)/shard_map/ppermute | solution.py:536
  19.4 2.8 %collective-permute-start.7 = (bf16[304,128]{1,0:T(8,128)(2,1)S(1)}, bf16[304,128]{1,0:T(8,128)(2,1)S(1)}, u32[]{:S(2)}, u32[]{:S(2)}) collective-permute-start(bf16[304,128]{1,0:T(8,128)(2,1)S(1)} %add_convert_fusion.4), channel_id=1, source_target_pairs={{0,2},{1,9},{2,0},{3,11},{4,6},{5,13},{6,4},{7,15},{8,10},{9,1},{1... | collective-permute-start | bytes 233480 | tf_op jit(solution)/shard_map/ppermute | solution.py:565
  22.2 2.4 %collective-permute-done.7 = bf16[304,128]{1,0:T(8,128)(2,1)S(1)} collective-permute-done((bf16[304,128]{1,0:T(8,128)(2,1)S(1)}, bf16[304,128]{1,0:T(8,128)(2,1)S(1)}, u32[]{:S(2)}, u32[]{:S(2)}) %collective-permute-start.7) | collective-permute-done | bytes 77856 | tf_op jit(solution)/shard_map/ppermute | solution.py:565
  24.6 2.1 %collective-permute-start.8 = (bf16[304,128]{1,0:T(8,128)(2,1)S(1)}, bf16[304,128]{1,0:T(8,128)(2,1)S(1)}, u32[]{:S(2)}, u32[]{:S(2)}) collective-permute-start(bf16[304,128]{1,0:T(8,128)(2,1)S(1)} %add_convert_fusion.3), channel_id=1, source_target_pairs={{0,4},{1,17},{2,6},{3,19},{4,0},{5,21},{6,2},{7,23},{8,12},{9,25},... | collective-permute-start | bytes 233480 | tf_op jit(solution)/shard_map/ppermute | solution.py:565
  26.7 2.4 %collective-permute-done.8 = bf16[304,128]{1,0:T(8,128)(2,1)S(1)} collective-permute-done((bf16[304,128]{1,0:T(8,128)(2,1)S(1)}, bf16[304,128]{1,0:T(8,128)(2,1)S(1)}, u32[]{:S(2)}, u32[]{:S(2)}) %collective-permute-start.8) | collective-permute-done | bytes 77856 | tf_op jit(solution)/shard_map/ppermute | solution.py:565
  29.1 2.1 %collective-permute-start.9 = (bf16[304,128]{1,0:T(8,128)(2,1)S(1)}, bf16[304,128]{1,0:T(8,128)(2,1)S(1)}, u32[]{:S(2)}, u32[]{:S(2)}) collective-permute-start(bf16[304,128]{1,0:T(8,128)(2,1)S(1)} %add_convert_fusion.2), channel_id=1, source_target_pairs={{0,8},{1,3},{2,10},{3,1},{4,12},{5,7},{6,14},{7,5},{8,0},{9,11},{1... | collective-permute-start | bytes 233480 | tf_op jit(solution)/shard_map/ppermute | solution.py:565
  31.2 2.4 %collective-permute-done.9 = bf16[304,128]{1,0:T(8,128)(2,1)S(1)} collective-permute-done((bf16[304,128]{1,0:T(8,128)(2,1)S(1)}, bf16[304,128]{1,0:T(8,128)(2,1)S(1)}, u32[]{:S(2)}, u32[]{:S(2)}) %collective-permute-start.9) | collective-permute-done | bytes 77856 | tf_op jit(solution)/shard_map/ppermute | solution.py:565
  33.7 3.1 %collective-permute-start.10 = (bf16[304,128]{1,0:T(8,128)(2,1)S(1)}, bf16[304,128]{1,0:T(8,128)(2,1)S(1)}, u32[]{:S(2)}, u32[]{:S(2)}) collective-permute-start(bf16[304,128]{1,0:T(8,128)(2,1)S(1)} %add_convert_fusion.1), channel_id=1, source_target_pairs={{0,16},{1,5},{2,18},{3,7},{4,20},{5,1},{6,22},{7,3},{8,24},{9,13},... | collective-permute-start | bytes 233480 | tf_op jit(solution)/shard_map/ppermute | solution.py:565
  36.8 2.4 %collective-permute-done.10 = bf16[304,128]{1,0:T(8,128)(2,1)S(1)} collective-permute-done((bf16[304,128]{1,0:T(8,128)(2,1)S(1)}, bf16[304,128]{1,0:T(8,128)(2,1)S(1)}, u32[]{:S(2)}, u32[]{:S(2)}) %collective-permute-start.10) | collective-permute-done | bytes 77856 | tf_op jit(solution)/shard_map/ppermute | solution.py:565
  39.2 0.1 collective-permute-start.11
  39.2 1.8 %shard_map.198 = bf16[2304,256]{1,0:T(8,128)(2,1)} custom-call(f32[2304,256]{1,0:T(8,128)S(1)} %get-tuple-element.56.pre3, f32[8,256]{1,0:T(8,128)S(1)} %get-tuple-element.57.own3, f32[8,256]{1,0:T(8,128)S(1)} %collective-permute-done.2.rec3, f32[8,256]{1,0:T(8,128)S(1)} %get-tuple-element.51.prm, bf16[2304,256]{1,0:T(8,128)(2,1)S(1)} %get-tuple-element.58.im), custom_call_target="tpu_custom_call" | custom-call | flops 5898240 | bytes 5922816 | tf_op jit(solution)/shard_map/pallas_call | solution.py:522
  41.0 1.5 %shard_map.205 = bf16[2304,256]{1,0:T(8,128)(2,1)} custom-call(bf16[1152,128]{1,0:T(8,128)(2,1)S(1)} %get-tuple-element.72.dh1, bf16[64,256]{1,0:T(8,128)(2,1)S(1)} %get-tuple-element.73.w, f32[2304,256]{1,0:T(8,128)S(1)} %get-tuple-element.60.e3), custom_call_target="tpu_custom_call" | custom-call | flops 150994944 | bytes 5046272 | tf_op jit(solution)/shard_map/pallas_call | solution.py:522
  42.5 0.0 collective-permute-done.11.refs_1_
  42.5 0.9 %shard_map.206 = (f32[64,256]{1,0:T(8,128)}, f32[9,64,64]{2,1,0:T(8,128)}, f32[64,256]{1,0:T(8,128)}, f32[1,64]{1,0:T(1,128)}, f32[1,64]{1,0:T(1,128)}, /*index=...) custom-call(bf16[304,128]{1,0:T(8,128)(2,1)S(1)} %add_convert_fusion.refs_0_, ...), custom_call_target="tpu_custom_call" | custom-call | bytes 437248 | tf_op jit(solution)/shard_map/pallas_call | solution.py:522
  (8 shorter events, 0.1 us)
Async XLA Ops:
  0.6 3.2 %copy-start.3 = (f32[64]{0:T(128)S(1)}, f32[64]{0:T(128)}, u32[]{:S(2)}) copy-start(f32[64]{0:T(128)} %param.15) | copy-start | bytes 772
  0.7 3.2 %copy-start.4 = (f32[64]{0:T(128)S(1)}, f32[64]{0:T(128)}, u32[]{:S(2)}) copy-start(f32[64]{0:T(128)} %param.16) | copy-start | bytes 772
  0.7 3.2 %copy-start.5 = (f32[64]{0:T(128)S(1)}, f32[64]{0:T(128)}, u32[]{:S(2)}) copy-start(f32[64]{0:T(128)} %param.17) | copy-start | bytes 772
  0.7 3.2 %copy-start.6 = (f32[64]{0:T(128)S(1)}, f32[64]{0:T(128)}, u32[]{:S(2)}) copy-start(f32[64]{0:T(128)} %param.18) | copy-start | bytes 772
  0.7 3.2 %copy-start.1 = (f32[256]{0:T(256)S(1)}, f32[256]{0:T(256)}, u32[]{:S(2)}) copy-start(f32[256]{0:T(256)} %param.19) | copy-start | bytes 3076
  0.7 3.2 %copy-start.2 = (f32[256]{0:T(256)S(1)}, f32[256]{0:T(256)}, u32[]{:S(2)}) copy-start(f32[256]{0:T(256)} %param.20) | copy-start | bytes 3076
  0.7 3.2 %copy-start = (bf16[64,256]{1,0:T(8,128)(2,1)S(1)}, bf16[64,256]{1,0:T(8,128)(2,1)}, u32[]{:S(2)}) copy-start(bf16[64,256]{1,0:T(8,128)(2,1)} %we.1) | copy-start | bytes 98308
  3.3 1.6 %collective-permute-start = (bf16[592,128]{1,0:T(8,128)(2,1)S(1)}, bf16[592,128]{1,0:T(8,128)(2,1)S(1)}, u32[]{:S(2)}, u32[]{:S(2)}) collective-permute-start(bf16[592,128]{1,0:T(8,128)(2,1)S(1)} %get-tuple-element.49.own1), channel_id=1, source_target_pairs={{0,1},{1,0},{2,3},{3,2},{4,5},{5,4},{6,7},{7,6},{8,9},{9,8},{10,11... | collective-permute-start | bytes 454664 | tf_op jit(solution)/shard_map/ppermute | solution.py:536
  6.5 1.2 %collective-permute-start.1 = (f32[8,128]{1,0:T(8,128)S(1)}, f32[8,128]{1,0:T(8,128)S(1)}, u32[]{:S(2)}, u32[]{:S(2)}) collective-permute-start(f32[8,128]{1,0:T(8,128)S(1)} %get-tuple-element.54.own2), channel_id=1, source_target_pairs={{0,1},{1,0},{2,3},{3,2},{4,5},{5,4},{6,7},{7,6},{8,9},{9,8},{10,11... | collective-permute-start | bytes 12296 | tf_op jit(solution)/shard_map/ppermute | solution.py:536
  8.5 1.2 %collective-permute-start.2 = (f32[8,256]{1,0:T(8,128)S(1)}, f32[8,256]{1,0:T(8,128)S(1)}, u32[]{:S(2)}, u32[]{:S(2)}) collective-permute-start(f32[8,256]{1,0:T(8,128)S(1)} %get-tuple-element.57.own3), channel_id=1, source_target_pairs={{0,1},{1,0},{2,3},{3,2},{4,5},{5,4},{6,7},{7,6},{8,9},{9,8},{10,11... | collective-permute-start | bytes 24584 | tf_op jit(solution)/shard_map/ppermute | solution.py:536
  11.5 1.2 %collective-permute-start.3 = (f32[8,256]{1,0:T(8,128)S(1)}, f32[8,256]{1,0:T(8,128)S(1)}, u32[]{:S(2)}, u32[]{:S(2)}) collective-permute-start(f32[8,256]{1,0:T(8,128)S(1)} %get-tuple-element.61.own4), channel_id=1, source_target_pairs={{0,1},{1,0},{2,3},{3,2},{4,5},{5,4},{6,7},{7,6},{8,9},{9,8},{10,11... | collective-permute-start | bytes 24584 | tf_op jit(solution)/shard_map/ppermute | solution.py:536
  13.6 1.7 %collective-permute-start.4 = (bf16[1168,128]{1,0:T(8,128)(2,1)S(1)}, bf16[1168,128]{1,0:T(8,128)(2,1)S(1)}, u32[]{:S(2)}, u32[]{:S(2)}) collective-permute-start(bf16[1168,128]{1,0:T(8,128)(2,1)S(1)} %get-tuple-element.63.own5), channel_id=1, source_target_pairs={{0,1},{1,0},{2,3},{3,2},{4,5},{5,4},{6,7},{7,6},{8,9},{9,8},{10,11... | collective-permute-start | bytes 897032 | tf_op jit(solution)/shard_map/ppermute | solution.py:536
  16.3 1.3 %collective-permute-start.5 = (f32[8,128]{1,0:T(8,128)S(1)}, f32[8,128]{1,0:T(8,128)S(1)}, u32[]{:S(2)}, u32[]{:S(2)}) collective-permute-start(f32[8,128]{1,0:T(8,128)S(1)} %get-tuple-element.68.own6), channel_id=1, source_target_pairs={{0,1},{1,0},{2,3},{3,2},{4,5},{5,4},{6,7},{7,6},{8,9},{9,8},{10,11... | collective-permute-start | bytes 12296 | tf_op jit(solution)/shard_map/ppermute | solution.py:536
  18.0 1.3 %collective-permute-start.6 = (bf16[304,128]{1,0:T(8,128)(2,1)S(1)}, bf16[304,128]{1,0:T(8,128)(2,1)S(1)}, u32[]{:S(2)}, u32[]{:S(2)}) collective-permute-start(bf16[304,128]{1,0:T(8,128)(2,1)S(1)} %get-tuple-element.75), channel_id=1, source_target_pairs={{0,1},{1,0},{2,3},{3,2},{4,5},{5,4},{6,7},{7,6},{8,9},{9,8},{10,11... | collective-permute-start | bytes 233480 | tf_op jit(solution)/shard_map/ppermute | solution.py:536
  19.4 5.2 %collective-permute-start.7 = (bf16[304,128]{1,0:T(8,128)(2,1)S(1)}, bf16[304,128]{1,0:T(8,128)(2,1)S(1)}, u32[]{:S(2)}, u32[]{:S(2)}) collective-permute-start(bf16[304,128]{1,0:T(8,128)(2,1)S(1)} %add_convert_fusion.4), channel_id=1, source_target_pairs={{0,2},{1,9},{2,0},{3,11},{4,6},{5,13},{6,4},{7,15},{8,10},{9,1},{1... | collective-permute-start | bytes 233480 | tf_op jit(solution)/shard_map/ppermute | solution.py:565
  24.6 4.5 %collective-permute-start.8 = (bf16[304,128]{1,0:T(8,128)(2,1)S(1)}, bf16[304,128]{1,0:T(8,128)(2,1)S(1)}, u32[]{:S(2)}, u32[]{:S(2)}) collective-permute-start(bf16[304,128]{1,0:T(8,128)(2,1)S(1)} %add_convert_fusion.3), channel_id=1, source_target_pairs={{0,4},{1,17},{2,6},{3,19},{4,0},{5,21},{6,2},{7,23},{8,12},{9,25},... | collective-permute-start | bytes 233480 | tf_op jit(solution)/shard_map/ppermute | solution.py:565
  29.1 4.5 %collective-permute-start.9 = (bf16[304,128]{1,0:T(8,128)(2,1)S(1)}, bf16[304,128]{1,0:T(8,128)(2,1)S(1)}, u32[]{:S(2)}, u32[]{:S(2)}) collective-permute-start(bf16[304,128]{1,0:T(8,128)(2,1)S(1)} %add_convert_fusion.2), channel_id=1, source_target_pairs={{0,8},{1,3},{2,10},{3,1},{4,12},{5,7},{6,14},{7,5},{8,0},{9,11},{1... | collective-permute-start | bytes 233480 | tf_op jit(solution)/shard_map/ppermute | solution.py:565
  33.7 5.5 %collective-permute-start.10 = (bf16[304,128]{1,0:T(8,128)(2,1)S(1)}, bf16[304,128]{1,0:T(8,128)(2,1)S(1)}, u32[]{:S(2)}, u32[]{:S(2)}) collective-permute-start(bf16[304,128]{1,0:T(8,128)(2,1)S(1)} %add_convert_fusion.1), channel_id=1, source_target_pairs={{0,16},{1,5},{2,18},{3,7},{4,20},{5,1},{6,22},{7,3},{8,24},{9,13},... | collective-permute-start | bytes 233480 | tf_op jit(solution)/shard_map/ppermute | solution.py:565
  39.2 3.3 %collective-permute-start.11 = (bf16[304,128]{1,0:T(8,128)(2,1)S(1)}, bf16[304,128]{1,0:T(8,128)(2,1)S(1)}, u32[]{:S(2)}, u32[]{:S(2)}) collective-permute-start(bf16[304,128]{1,0:T(8,128)(2,1)S(1)} %add_convert_fusion.refs_0_), channel_id=1, source_target_pairs={{0,1},{1,0},{2,3},{3,2},{4,5},{5,4},{6,7},{7,6},{8,9},{9,8},{10,11... | collective-permute-start | bytes 233480 | tf_op jit(solution)/shard_map/ppermute | solution.py:536
where the time goes:
time: 43.8 us; the launch traced here: 43.4 us
  waiting for transfers between devices  14.7 us (34%)
  Pallas kernels  14.6 us (33%)
  starting transfers between devices  13.1 us (30%)
  between operations  0.83 us (2%)
    pallas_call x13, Pallas kernels, call(): pl.pallas_call(kernel, out_shape=[kind_of(shape, kind) for shape, kind in...  14.6 us
    ppermute x4, starting transfers between devices, summed_over_dp(): got = lax.ppermute(part, ('dp', 'space'), pairs)  10.1 us
    ppermute x4, waiting for transfers between devices, summed_over_dp(): got = lax.ppermute(part, ('dp', 'space'), pairs)  9.51 us
    ppermute x8, waiting for transfers between devices, swapped(): lax.ppermute(value, axis, [(i, (i + step) % count) for i in range(count)])  5.23 us
    ppermute x8, starting transfers between devices, swapped(): lax.ppermute(value, axis, [(i, (i + step) % count) for i in range(count)])  2.95 us
  transfers between devices with their start and end apart: 12, of which 10 were waited for; matrix products, arithmetic and copies ran while one was open for 0% of the time, Pallas kernels for 11%

commit v1 on v0

--- a/solution.py
+++ b/solution.py
@@ -130,34 +130,37 @@
     return rowsum(acc)
 
 
-def first_kernel(edge, im, w, wd, pre, msg, held, w_held, wd_held, sems):
+def first_kernel(edge, im, w, pre, msg, im_held, w_held, im_near, w_near, sems):
     half, cols = pre.shape[0], edge // 2
-    fetch_w = pltpu.make_async_copy(w, w_held, sems.at[sems.shape[0] - 1])
+    fetch_w = pltpu.make_async_copy(w, w_near, sems.at[0])
     fetch_w.start()
-    order = [base + at for at in range(0, half, cols) for base in (0, half)]
     copies = []
-    for k, base in enumerate(order):
-        rows = pl.ds(base, cols)
-        copies.append(pltpu.make_async_copy(im.at[rows, :], held.at[rows, :], sems.at[k]))
-        copies[-1].start()
-    fetch_wd = pltpu.make_async_copy(wd, wd_held, sems.at[sems.shape[0] - 2])
-    fetch_wd.start()
+    for at in range(0, half, cols):
+        for base in (at, half + at):
+            rows = pl.ds(base, cols)
+            sem = sems.at[1 + len(copies)]
+            copies.append(pltpu.make_async_copy(im.at[rows, :], im_near.at[rows, :], sem))
+            copies[-1].start()
     fetch_w.wait()
-    weight = w_held[...]
+    weight = w_near[...]
+    w_held[...] = weight
     zero = jnp.zeros_like(weight)
     upper = jnp.concatenate([weight, zero], 0)
     lower = jnp.concatenate([zero, weight], 0)
     acc = jnp.zeros((8, pre.shape[1]), F32)
     for k, at in enumerate(range(0, half, cols)):
-        copies[2 * k].wait()
-        copies[2 * k + 1].wait()
-        part = nt(held[at : at + cols, :], upper) + nt(held[half + at : half + at + cols, :], lower)
+        part = None
+        for copy, base, side in ((2 * k, at, upper), (2 * k + 1, half + at, lower)):
+            copies[copy].wait()
+            block = im_near[base : base + cols, :]
+            im_held[base : base + cols, :] = block
+            prod = nt(block, side)
+            part = prod if part is None else part + prod
         pre[at : at + cols, :] = part
         acc = acc + group(part)
     mean = both_halves(rowsum(acc)) / (2 * half)
     msg[0:WIDE_HEAD, :] = wide_head_rows(mean, both_halves(centred_squares(pre, mean, cols)))
     msg[WIDE_HEAD:, :] = edges(pre, edge, mean).astype(BF16)
-    fetch_wd.wait()
 
 
 def tap_blocks(w):
@@ -171,16 +174,24 @@
             )
 
 
-def weights_kernel(w, we, g1, s1, g2, s2, g3, s3, fwd, held, prm):
-    wide = 2 * w.shape[-1]
-    for a, b, both in tap_blocks(w):
+def weights_kernel(*refs):
+    far, (we_held, fwd, bwd, prm), near, sems = refs[:8], refs[8:12], refs[12:-1], refs[-1]
+    copies = [pltpu.make_async_copy(a, b, sems.at[k]) for k, (a, b) in enumerate(zip(far, near))]
+    for item in copies:
+        item.start()
+    for item in copies:
+        item.wait()
+    wide = 2 * near[0].shape[-1]
+    for a, b, both in tap_blocks(near[0]):
+        k = 2 - a
         fwd[a * wide : (a + 1) * wide, b * wide : (b + 1) * wide] = both
-    held[...] = we[...]
+        bwd[b * wide : (b + 1) * wide, k * wide : (k + 1) * wide] = both
     prm[...] = jnp.zeros(prm.shape, F32)
-    for k, ref in enumerate((g1, s1, g2, s2)):
+    we_held[...] = near[7][...]
+    for k, ref in enumerate(near[1:5]):
         prm[k : k + 1, 0:wide] = jnp.concatenate([ref[...], ref[...]], 1)
-    prm[4:5, :] = g3[...]
-    prm[5:6, :] = s3[...]
+    prm[4:5, :] = near[5][...]
+    prm[5:6, :] = near[6][...]
 
 
 def gain_shift(prm, norm, wide):
@@ -205,11 +216,9 @@
 
 
 def second_kernel(
-    peers, edge, pre1, own1, rec1, prm, w, cot, ext, pre2, msg, held, scr, sem
+    peers, edge, pre1, own1, rec1, prm, w, ext, pre2, msg, scr
 ):
     half, cols, wide = pre2.shape[0], edge // 2, pre2.shape[1]
-    fetch = pltpu.make_async_copy(cot, held, sem)
-    fetch.start()
     g1, s1 = gain_shift(prm, 0, wide)
     mean, inv = moments(own1, rec1, peers, 2.0 * half)
     scale, bias = norm_coefs(g1, s1, mean, inv)
@@ -244,7 +253,6 @@
         acc = acc + group(part)
     mean = both_halves(rowsum(acc)) / (2 * half)
     msg[...] = head_rows(mean, both_halves(centred_squares(pre2, mean, cols)))
-    fetch.wait()
 
 
 def third_kernel(peers, cols, pre2, own2, rec2, prm, w, act2, pre3, msg):
@@ -270,39 +278,59 @@
     msg[...] = head_rows(mean, centred_squares(pre3, mean, cols))
 
 
+def halves_kernel(step, im, cot, im_half, cot_half):
+    def body(i, carry):
+        at = pl.ds(pl.multiple_of(i * step, step), step)
+        im_half[at, :] = 0.5 * im[at, :].astype(F32)
+        cot_half[at, :] = 0.5 * cot[at, :].astype(F32)
+        return carry
+
+    lax.fori_loop(0, im.shape[0] // step, body, 0, unroll=2)
+
+
+def slopes_kernel(peers, step, pre1, own1, rec1, pre2, own2, rec2, prm, slope1, slope2):
+    half, wide = pre1.shape
+    for norm, pre, own, rec, out in ((0, pre1, own1, rec1, slope1), (1, pre2, own2, rec2, slope2)):
+        mean, inv = moments(own, rec, peers, 2.0 * half)
+        scale, bias = norm_coefs(*gain_shift(prm, norm, wide), mean, inv)
+        for at in range(0, half, step):
+            out[at : at + step, :] = slope(pre[at : at + step, :] * scale + bias)
+
+
 def halved_coefs(peers, own3, rec3, prm, size):
     mean, inv = moments(own3, rec3, peers, float(size))
     gain, shift = gain_shift(prm, 2, own3.shape[1])
     scale, bias = norm_coefs(gain, shift, mean, inv)
-    return 0.5 * scale, 0.5 * bias, mean, inv
-
-
-def fourth_kernel(peers, step, pre3, own3, rec3, prm, im, cot, e3, msg):
+    return 0.5 * scale, 0.5 * bias, gain, shift
+
+
+def fourth_kernel(peers, step, pre3, own3, rec3, prm, im_half, cot_half, e3, msg):
     size, chans = pre3.shape
-    scale, bias, mean, inv = halved_coefs(peers, own3, rec3, prm, size)
+    scale, bias, gain, shift = halved_coefs(peers, own3, rec3, prm, size)
 
     def body(i, carry):
         sums, cross = carry
         at = pl.ds(pl.multiple_of(i * step, step), step)
-        pre = pre3[at, :]
-        half = pre * scale + (bias + 0.5 * im[at, :].astype(F32))
+        out = pre3[at, :] * scale + bias
+        half = out + im_half[at, :]
         turn = jnp.tanh(half)
-        grad = cot[at, :].astype(F32) * ((0.5 + 0.5 * turn) * (1.0 + half * (1.0 - turn)))
+        grad = cot_half[at, :] * ((1.0 + turn) * (1.0 + half * (1.0 - turn)))
         e3[at, :] = grad
-        return sums + group(grad), cross + group(grad * (pre - mean))
+        return sums + group(grad), cross + group(grad * out)
 
     zero = jnp.zeros((8, chans), F32)
     sums, cross = lax.fori_loop(0, size // step, body, (zero, zero), unroll=2)
-    msg[...] = head_rows(rowsum(sums), rowsum(cross) * inv)
-
-
-def result_kernel(peers, step, pre3, own3, rec3, prm, im, out):
+    sums = rowsum(sums)
+    msg[...] = head_rows(sums, (2.0 * rowsum(cross) - shift * sums) / gain)
+
+
+def result_kernel(peers, step, pre3, own3, rec3, prm, im_half, out):
     size = pre3.shape[0]
     scale, bias, _, _ = halved_coefs(peers, own3, rec3, prm, size)
 
     def body(i, carry):
         at = pl.ds(pl.multiple_of(i * step, step), step)
-        half = pre3[at, :] * scale + (bias + 0.5 * im[at, :].astype(F32))
+        half = pre3[at, :] * scale + bias + im_half[at, :]
         out[at, :] = (half + half * jnp.tanh(half)).astype(BF16)
         return carry
 
@@ -310,17 +338,15 @@
 
 
 def fifth_kernel(
-    peers, edge, pre3, e3, own3, rec3, own4, rec4, prm, w, pre2, own2, rec2, dh3, e2, msg
+    peers, edge, pre3, e3, own3, rec3, own4, rec4, prm, w, pre2, own2, rec2, slope2, dh3, e2, msg
 ):
     size, half, cols, wide = pre3.shape[0], pre2.shape[0], edge // 2, pre2.shape[1]
     count = float(size * (peers + 1))
-    g2, s2 = gain_shift(prm, 1, wide)
     g3, _ = gain_shift(prm, 2, pre3.shape[1])
     mean3, inv3 = moments(own3, rec3, peers, float(size))
     sums3, cross3 = totals(own4, rec4, peers)
     scale3, slant3, bias3 = back_coefs(g3, mean3, inv3, sums3, cross3, count)
     mean, inv = moments(own2, rec2, peers, float(size))
-    scale, bias = norm_coefs(g2, s2, mean, inv)
     weight = w[...]
     zero = jnp.zeros_like(weight)
     upper = jnp.concatenate([weight, zero], 0)
@@ -336,7 +362,7 @@
             part = nt(dh, side)
             back = part if back is None else back + part
         pre = pre2[at : at + cols, :]
-        grad = back * slope(pre * scale + bias)
+        grad = back * slope2[at : at + cols, :]
         e2[at : at + cols, :] = grad
         sums = sums + group(grad)
         cross = cross + group(grad * (pre - mean))
@@ -345,29 +371,24 @@
     msg[WIDE_HEAD + edge :, :] = edges(pre2, edge, mean).astype(BF16)
 
 
-def expand_kernel(act2, dh3, w, out, bwd):
+def expand_kernel(act2, dh3, out):
     half = act2.shape[0]
-    mids, wide = act2.shape[1] // 2, act2.shape[1]
+    mids = act2.shape[1] // 2
     out[...] = tn(act2[...], dh3[0:half, :])[0:mids, :] + tn(act2[...], dh3[half:, :])[mids:, :]
-    for a, b, both in tap_blocks(w):
-        k = 2 - a
-        bwd[b * wide : (b + 1) * wide, k * wide : (k + 1) * wide] = both
 
 
 def sixth_kernel(
-    peers, edge, pre2, e2, own5, rec5, own2, rec2, pre1, own1, rec1, prm, w,
+    peers, edge, pre2, e2, own5, rec5, own2, rec2, pre1, own1, rec1, prm, w, slope1,
     dext, e1, msg, scr,
 ):
     half, cols, wide = pre2.shape[0], edge // 2, pre2.shape[1]
     size = 2.0 * half
     count = size * (peers + 1)
-    g1, s1 = gain_shift(prm, 0, wide)
     g2, _ = gain_shift(prm, 1, wide)
     mean2, inv2 = moments(own2, rec2, peers, size)
     sums2, cross2 = totals(own5, rec5, peers)
     scale2, slant2, bias2 = back_coefs(g2, mean2, inv2, sums2, cross2, count)
     mean, inv = moments(own1, rec1, peers, size)
-    scale, bias = norm_coefs(g1, s1, mean, inv)
     clear_gaps(scr, cols)
     acts = []
     for at in range(0, half, cols):
@@ -399,7 +420,7 @@
             + scr[2 * i + 1, GAP - 2 : GAP - 2 + cols, :]
         )
         pre = pre1[at : at + cols, :]
-        grad = back * slope(pre * scale + bias)
+        grad = back * slope1[at : at + cols, :]
         e1[at : at + cols, :] = grad
         sums = sums + group(grad)
         cross = cross + group(grad * (pre - mean))
@@ -536,7 +557,7 @@
     return lax.ppermute(value, axis, [(i, (i + step) % count) for i in range(count)])
 
 
-def exchange(msg, peers):
+def exchanged(msg, peers):
     if peers == 0:
         return msg
     if peers == 1:
@@ -588,55 +609,64 @@
     w_rows = w_reduce.T
     gates = 2 * pixels * wide * chans
 
-    pre1, own1, im_held, w_held, wd_held = call(
+    pre1, own1, im_held, w_held = call(
         part(first_kernel, edge),
         [((half, wide), F32), ((WIDE_HEAD + edge, wide), BF16), ((pixels, chans), BF16)]
-        + [(w_rows.shape, BF16), (w_dilated.shape, BF16)],
-        im, w_rows, w_dilated, flops=gates, far=(0, 1, 2),
-        scratch=[pltpu.SemaphoreType.DMA((2 * chunks + 2,))],
-    )
-    fwd, we, prm = call(
+        + [(w_rows.shape, BF16)],
+        im, w_rows, flops=gates, far=(0, 1),
+        scratch=[pltpu.VMEM((pixels, chans), BF16), pltpu.VMEM(w_rows.shape, BF16)]
+        + [pltpu.SemaphoreType.DMA((2 * chunks + 1,))],
+    )
+    own1, cot = lax.optimization_barrier((own1, cot))
+    rec1 = exchanged(own1, peers)
+    we, fwd, bwd, prm = call(
         weights_kernel,
-        [((3 * wide, 3 * wide), BF16), ((mids, chans), BF16), ((8, chans), F32)],
-        wd_held, w_expand, row(gain_one), row(shift_one), row(gain_two), row(shift_two),
-        row(gain_three), row(shift_three), flops=10**6,
-    )
-    rec1 = exchange(own1, peers)
-    ext, pre2, own2, cot_held = call(
+        [(w_expand.shape, BF16)] + [((3 * wide, 3 * wide), BF16)] * 2 + [((8, chans), F32)],
+        w_dilated, row(gain_one), row(shift_one), row(gain_two), row(shift_two),
+        row(gain_three), row(shift_three), w_expand, flops=10**6, far=tuple(range(8)),
+        scratch=[pltpu.VMEM(w_dilated.shape, BF16)] + [pltpu.VMEM((1, mids), F32)] * 4
+        + [pltpu.VMEM((1, chans), F32)] * 2 + [pltpu.VMEM(w_expand.shape, BF16)]
+        + [pltpu.SemaphoreType.DMA((8,))],
+    )
+    ext, pre2, own2 = call(
         part(second_kernel, peers, edge),
-        [((ext_rows, wide), BF16), ((half, wide), F32), ((HEAD, wide), F32), ((pixels, chans), BF16)],
-        pre1, own1, rec1, prm, fwd, cot, far=(5,),
-        scratch=[gaps(2 * chunks), pltpu.SemaphoreType.DMA], flops=2 * half * 9 * wide * wide,
-    )
-    rec2 = exchange(own2, peers)
+        [((ext_rows, wide), BF16), ((half, wide), F32), ((HEAD, wide), F32)],
+        pre1, own1, rec1, prm, fwd, scratch=[gaps(2 * chunks)], flops=2 * half * 9 * wide * wide,
+    )
+    rec2 = exchanged(own2, peers)
+    im_half, cot_half = call(
+        part(halves_kernel, 64), [((pixels, chans), F32)] * 2, im_held, cot,
+        flops=4 * pixels * chans,
+    )
     act2, pre3, own3 = call(
         part(third_kernel, peers, cols),
         [((half, wide), BF16), ((pixels, chans), F32), ((HEAD, chans), F32)],
         pre2, own2, rec2, prm, we, flops=gates,
     )
-    rec3 = exchange(own3, peers)
+    rec3 = exchanged(own3, peers)
+    slope1, slope2 = call(
+        part(slopes_kernel, peers, cols), [((half, wide), F32)] * 2,
+        pre1, own1, rec1, pre2, own2, rec2, prm, flops=30 * half * wide,
+    )
     e3, own4 = call(
         part(fourth_kernel, peers, 64), [((pixels, chans), F32), ((HEAD, chans), F32)],
-        pre3, own3, rec3, prm, im_held, cot_held, flops=30 * pixels * chans,
-    )
-    rec4 = exchange(own4, peers)
+        pre3, own3, rec3, prm, im_half, cot_half, flops=30 * pixels * chans,
+    )
+    rec4 = exchanged(own4, peers)
     dh3, e2, own5 = call(
         part(fifth_kernel, peers, edge),
         [((pixels, chans), BF16), ((half, wide), F32), ((WIDE_HEAD + 2 * edge, wide), BF16)],
-        pre3, e3, own3, rec3, own4, rec4, prm, we, pre2, own2, rec2, flops=gates,
-    )
-    rec5 = exchange(own5, peers)
-    gwe, bwd = call(
-        expand_kernel, [((mids, chans), F32), ((3 * wide, 3 * wide), BF16)],
-        act2, dh3, wd_held, flops=gates,
-    )
+        pre3, e3, own3, rec3, own4, rec4, prm, we, pre2, own2, rec2, slope2, flops=gates,
+    )
+    rec5 = exchanged(own5, peers)
+    gwe = call(expand_kernel, [((mids, chans), F32)], act2, dh3, flops=gates)
     dext, e1, own6 = call(
         part(sixth_kernel, peers, edge),
         [((ext_rows, wide), BF16), ((half, wide), F32), ((HEAD, wide), F32)],
-        pre2, e2, own5, rec5, own2, rec2, pre1, own1, rec1, prm, bwd,
+        pre2, e2, own5, rec5, own2, rec2, pre1, own1, rec1, prm, bwd, slope1,
         scratch=[gaps(2 * chunks)], flops=2 * half * 9 * wide * wide,
     )
-    rec6 = exchange(own6, peers)
+    rec6 = exchanged(own6, peers)
     gwd = call(
         part(dilated_kernel, edge), [((5 * mids, wide), BF16)], ext, dext,
         scratch=[gaps(chunks), pltpu.VMEM((half, 3 * wide), BF16)],
@@ -661,7 +691,7 @@
     )
     result = call(
         part(result_kernel, peers, 64), [((pixels, chans), BF16)],
-        pre3, own3, rec3, prm, im_held, flops=10 * pixels * chans, final=True,
+        pre3, own3, rec3, prm, im_half, flops=10 * pixels * chans, final=True,
     )
     grads = call(
         part(unpack_kernel, peers, float(lax.axis_size("dp"))),

time: 43.8 us -> 42.4 us (0.968)
  waiting for transfers between devices: 14.7 us -> 13.3 us
  Pallas kernels: 14.6 us -> 15.3 us
  starting transfers between devices: 13.1 us -> 12.6 us
    ppermute x8, waiting for transfers between devices: 5.23 us -> 3.79 us  [swapped(): lax.ppermute(value, axis, [(i, (i + step) % count) for i in range(count)])]
    pallas_call x13 -> x15, Pallas kernels: 14.6 us -> 15.3 us  [call(): pl.pallas_call(kernel, out_shape=[kind_of(shape, kind) for shape, kind in...]
    ppermute x8, starting transfers between devices: 2.95 us -> 2.43 us  [swapped(): lax.ppermute(value, axis, [(i, (i + step) % count) for i in range(count)])]
  transfers between devices with their start and end apart: 12 -> 12, of which waited for: 10 -> 9; matrix products, arithmetic and copies ran while one was open for 0% -> 0% of each run, Pallas kernels for 11% -> 15%
where the time goes in v1:
time: 42.4 us; the launch traced here: 42 us
  Pallas kernels  15.3 us (36%)
  waiting for transfers between devices  13.3 us (31%)
  starting transfers between devices  12.6 us (30%)
  between operations  0.76 us (2%)
    pallas_call x15, Pallas kernels, call(): pl.pallas_call(kernel, out_shape=[kind_of(shape, kind) for shape, kind in...  15.3 us
    ppermute x4, starting transfers between devices, summed_over_dp(): got = lax.ppermute(part, ('dp', 'space'), pairs)  10.1 us
    ppermute x4, waiting for transfers between devices, summed_over_dp(): got = lax.ppermute(part, ('dp', 'space'), pairs)  9.51 us
    ppermute x8, waiting for transfers between devices, swapped(): lax.ppermute(value, axis, [(i, (i + step) % count) for i in range(count)])  3.79 us
    ppermute x8, starting transfers between devices, swapped(): lax.ppermute(value, axis, [(i, (i + step) % count) for i in range(count)])  2.43 us
  transfers between devices with their start and end apart: 12, of which 9 were waited for; matrix products, arithmetic and copies ran while one was open for 0% of the time, Pallas kernels for 15%

profile of v1, /device:TPU:0, one launch (start us, length us, event | category | flops | bytes accessed | tf_op | source)
XLA Modules:
  0.0 42.0 jit_solution(4337826713663386666)
XLA Ops:
  0.6 2.6 %shard_map.194 = (f32[1152,128]{1,0:T(8,128)S(1)}, bf16[592,128]{1,0:T(8,128)(2,1)S(1)}, bf16[2304,256]{1,0:T(8,128)(2,1)S(1)}, bf16[64,256]{1,0:T(8,128)(2,1)S(1)}) custom-call(bf16[2304,256]{1,0:T(8,128)(2,1)} %bitcast.20, bf16[64,256]{1,0:T(8,128)(2,1)} %bitcast.23), custom_call_target="tpu_custom_call" | custom-call | flops 150994944 | bytes 4530176 | tf_op jit(solution)/shard_map/pallas_call | solution.py:543
  3.2 0.0 copy-start
  3.2 0.6 %collective-permute-start = (bf16[592,128]{1,0:T(8,128)(2,1)S(1)}, bf16[592,128]{1,0:T(8,128)(2,1)S(1)}, u32[]{:S(2)}, u32[]{:S(2)}) collective-permute-start(bf16[592,128]{1,0:T(8,128)(2,1)S(1)} %get-tuple-element.53.own1), channel_id=1, source_target_pairs={{0,1},{1,0},{2,3},{3,2},{4,5},{5,4},{6,7},{7,6},{8,9},{9,8},{10,11... | collective-permute-start | bytes 454664 | tf_op jit(solution)/shard_map/ppermute | solution.py:557
  3.8 1.1 %shard_map.195 = (bf16[64,256]{1,0:T(8,128)(2,1)S(1)}, bf16[384,384]{1,0:T(8,128)(2,1)S(1)}, bf16[384,384]{1,0:T(8,128)(2,1)S(1)}, f32[8,256]{1,0:T(8,128)S(1)}) custom-call(bf16[3,3,64,64]{3,2,1,0:T(8,128)(2,1)} %refs_0_.1, f32[1,64]{1,0:T(1,128)} %bitcast.26, f32[1,64]{1,0:T(1,128)} %bitcast.27, f32[1,64]{1,0:T(1,128)} %bitcast.28, f32[1,64]{1,0:T(1,128)} %bitcast.29, ...), custom_call_target="tpu_custom_call" | custom-call | flops 1000000 | bytes 1362944 | tf_op jit(solution)/shard_map/pallas_call | solution.py:543
  4.9 0.0 collective-permute-done.rec1
  4.9 1.1 %shard_map.196 = (bf16[2304,128]{1,0:T(8,128)(2,1)S(1)}, f32[1152,128]{1,0:T(8,128)S(1)}, f32[8,128]{1,0:T(8,128)S(1)}) custom-call(f32[1152,128]{1,0:T(8,128)S(1)} %get-tuple-element.51.pre1, bf16[592,128]{1,0:T(8,128)(2,1)S(1)} %get-tuple-element.53.own1, bf16[592,128]{1,0:T(8,128)(2,1)S(1)} %collective-permute-done.rec1, ...), custom_call_target="tpu_custom_call" | custom-call | flops 339738624 | bytes 2969600 | tf_op jit(solution)/shard_map/pallas_call | solution.py:543
  6.1 0.3 collective-permute-start.1
  6.3 0.9 %collective-permute-done.1.rec2 = f32[8,128]{1,0:T(8,128)S(1)} collective-permute-done((f32[8,128]{1,0:T(8,128)S(1)}, f32[8,128]{1,0:T(8,128)S(1)}, u32[]{:S(2)}, u32[]{:S(2)}) %collective-permute-start.1) | collective-permute-done | bytes 4128 | tf_op jit(solution)/shard_map/ppermute | solution.py:557
  7.2 0.8 %shard_map.197 = (bf16[1152,128]{1,0:T(8,128)(2,1)S(1)}, f32[2304,256]{1,0:T(8,128)S(1)}, f32[8,256]{1,0:T(8,128)S(1)}) custom-call(f32[1152,128]{1,0:T(8,128)S(1)} %get-tuple-element.56.pre2, f32[8,128]{1,0:T(8,128)S(1)} %get-tuple-element.57.own2, f32[8,128]{1,0:T(8,128)S(1)} %collective-permute-done.1.rec2, f32[8,256]{1,0:T(8,128)S(1)} %get-tuple-element.54.prm, ...), custom_call_target="tpu_custom_call" | custom-call | flops 150994944 | bytes 3596288 | tf_op jit(solution)/shard_map/pallas_call | solution.py:543
  8.0 0.3 collective-permute-start.2
  8.3 0.0 copy-done
  8.4 0.5 %shard_map.198 = (f32[2304,256]{1,0:T(8,128)S(1)}, f32[2304,256]{1,0:T(8,128)S(1)}) custom-call(bf16[2304,256]{1,0:T(8,128)(2,1)S(1)} %get-tuple-element.61.im, bf16[2304,256]{1,0:T(8,128)(2,1)S(1)} %bitcast.19), custom_call_target="tpu_custom_call" | custom-call | flops 2359296 | bytes 7077888 | tf_op jit(solution)/shard_map/pallas_call | solution.py:543
  8.9 0.4 collective-permute-done.2.rec3
  9.3 1.2 %shard_map.200 = (f32[2304,256]{1,0:T(8,128)S(1)}, f32[8,256]{1,0:T(8,128)S(1)}) custom-call(f32[2304,256]{1,0:T(8,128)S(1)} %get-tuple-element.59.pre3, f32[8,256]{1,0:T(8,128)S(1)} %get-tuple-element.60.own3, f32[8,256]{1,0:T(8,128)S(1)} %collective-permute-done.2.rec3, f32[8,256]{1,0:T(8,128)S(1)} %get-tuple-element.54.prm, ...), custom_call_target="tpu_custom_call" | custom-call | flops 17694720 | bytes 9469952 | tf_op jit(solution)/shard_map/pallas_call | solution.py:543
  10.5 0.3 collective-permute-start.3
  10.8 0.4 %shard_map.201 = (f32[1152,128]{1,0:T(8,128)S(1)}, f32[1152,128]{1,0:T(8,128)S(1)}) custom-call(f32[1152,128]{1,0:T(8,128)S(1)} %get-tuple-element.51.pre1, bf16[592,128]{1,0:T(8,128)(2,1)S(1)} %get-tuple-element.53.own1, bf16[592,128]{1,0:T(8,128)(2,1)S(1)} %collective-permute-done.rec1, f32[1152,128]{1,0:T(8,128)S(1)} %get-tuple-element.56.pre2, ...), custom_call_target="tpu_custom_call" | custom-call | flops 4423680 | bytes 2678784 | tf_op jit(solution)/shard_map/pallas_call | solution.py:543
  11.3 0.5 %collective-permute-done.3.rec4 = f32[8,256]{1,0:T(8,128)S(1)} collective-permute-done((f32[8,256]{1,0:T(8,128)S(1)}, f32[8,256]{1,0:T(8,128)S(1)}, u32[]{:S(2)}, u32[]{:S(2)}) %collective-permute-start.3) | collective-permute-done | bytes 8224 | tf_op jit(solution)/shard_map/ppermute | solution.py:557
  11.8 0.7 %shard_map.202 = (bf16[2304,256]{1,0:T(8,128)(2,1)S(1)}, f32[1152,128]{1,0:T(8,128)S(1)}, bf16[1168,128]{1,0:T(8,128)(2,1)S(1)}) custom-call(f32[2304,256]{1,0:T(8,128)S(1)} %get-tuple-element.59.pre3, f32[2304,256]{1,0:T(8,128)S(1)} %get-tuple-element.65.e3, f32[8,256]{1,0:T(8,128)S(1)} %get-tuple-element.60.own3, ...), custom_call_target="tpu_custom_call" | custom-call | flops 150994944 | bytes 9527296 | tf_op jit(solution)/shard_map/pallas_call | solution.py:543
  12.5 0.3 collective-permute-start.4
  12.8 0.4 shard_map.205.gwe
  13.2 1.0 %collective-permute-done.4.rec5 = bf16[1168,128]{1,0:T(8,128)(2,1)S(1)} collective-permute-done((bf16[1168,128]{1,0:T(8,128)(2,1)S(1)}, bf16[1168,128]{1,0:T(8,128)(2,1)S(1)}, u32[]{:S(2)}, u32[]{:S(2)}) %collective-permute-start.4) | collective-permute-done | bytes 299040 | tf_op jit(solution)/shard_map/ppermute | solution.py:557
  14.1 1.1 %shard_map.203 = (bf16[2304,128]{1,0:T(8,128)(2,1)S(1)}, f32[1152,128]{1,0:T(8,128)S(1)}, f32[8,128]{1,0:T(8,128)S(1)}) custom-call(f32[1152,128]{1,0:T(8,128)S(1)} %get-tuple-element.56.pre2, f32[1152,128]{1,0:T(8,128)S(1)} %get-tuple-element.68.e2, bf16[1168,128]{1,0:T(8,128)(2,1)S(1)} %get-tuple-element.69.own5, ...), custom_call_target="tpu_custom_call" | custom-call | flops 339738624 | bytes 5345280 | tf_op jit(solution)/shard_map/pallas_call | solution.py:543
  15.2 0.3 collective-permute-start.5
  15.4 0.9 %shard_map.204.gwd = bf16[320,128]{1,0:T(8,128)(2,1)S(1)} custom-call(bf16[2304,128]{1,0:T(8,128)(2,1)S(1)} %get-tuple-element.74.ext, bf16[2304,128]{1,0:T(8,128)(2,1)S(1)} %get-tuple-element.75.dext), custom_call_target="tpu_custom_call" | custom-call | flops 339738624 | bytes 1343488 | tf_op jit(solution)/shard_map/pallas_call | solution.py:543
  16.3 0.0 collective-permute-done.5.rec6
  16.4 0.4 shard_map.206
  16.8 0.3 collective-permute-start.6
  17.1 1.0 %collective-permute-done.6 = bf16[304,128]{1,0:T(8,128)(2,1)S(1)} collective-permute-done((bf16[304,128]{1,0:T(8,128)(2,1)S(1)}, bf16[304,128]{1,0:T(8,128)(2,1)S(1)}, u32[]{:S(2)}, u32[]{:S(2)}) %collective-permute-start.6) | collective-permute-done | bytes 77856 | tf_op jit(solution)/shard_map/ppermute | solution.py:557
  18.1 2.8 %collective-permute-start.7 = (bf16[304,128]{1,0:T(8,128)(2,1)S(1)}, bf16[304,128]{1,0:T(8,128)(2,1)S(1)}, u32[]{:S(2)}, u32[]{:S(2)}) collective-permute-start(bf16[304,128]{1,0:T(8,128)(2,1)S(1)} %add_convert_fusion.4), channel_id=1, source_target_pairs={{0,2},{1,9},{2,0},{3,11},{4,6},{5,13},{6,4},{7,15},{8,10},{9,1},{1... | collective-permute-start | bytes 233480 | tf_op jit(solution)/shard_map/ppermute | solution.py:586
  20.9 2.4 %collective-permute-done.7 = bf16[304,128]{1,0:T(8,128)(2,1)S(1)} collective-permute-done((bf16[304,128]{1,0:T(8,128)(2,1)S(1)}, bf16[304,128]{1,0:T(8,128)(2,1)S(1)}, u32[]{:S(2)}, u32[]{:S(2)}) %collective-permute-start.7) | collective-permute-done | bytes 77856 | tf_op jit(solution)/shard_map/ppermute | solution.py:586
  23.3 2.1 %collective-permute-start.8 = (bf16[304,128]{1,0:T(8,128)(2,1)S(1)}, bf16[304,128]{1,0:T(8,128)(2,1)S(1)}, u32[]{:S(2)}, u32[]{:S(2)}) collective-permute-start(bf16[304,128]{1,0:T(8,128)(2,1)S(1)} %add_convert_fusion.3), channel_id=1, source_target_pairs={{0,4},{1,17},{2,6},{3,19},{4,0},{5,21},{6,2},{7,23},{8,12},{9,25},... | collective-permute-start | bytes 233480 | tf_op jit(solution)/shard_map/ppermute | solution.py:586
  25.4 2.4 %collective-permute-done.8 = bf16[304,128]{1,0:T(8,128)(2,1)S(1)} collective-permute-done((bf16[304,128]{1,0:T(8,128)(2,1)S(1)}, bf16[304,128]{1,0:T(8,128)(2,1)S(1)}, u32[]{:S(2)}, u32[]{:S(2)}) %collective-permute-start.8) | collective-permute-done | bytes 77856 | tf_op jit(solution)/shard_map/ppermute | solution.py:586
  27.9 2.1 %collective-permute-start.9 = (bf16[304,128]{1,0:T(8,128)(2,1)S(1)}, bf16[304,128]{1,0:T(8,128)(2,1)S(1)}, u32[]{:S(2)}, u32[]{:S(2)}) collective-permute-start(bf16[304,128]{1,0:T(8,128)(2,1)S(1)} %add_convert_fusion.2), channel_id=1, source_target_pairs={{0,8},{1,3},{2,10},{3,1},{4,12},{5,7},{6,14},{7,5},{8,0},{9,11},{1... | collective-permute-start | bytes 233480 | tf_op jit(solution)/shard_map/ppermute | solution.py:586
  30.0 2.4 %collective-permute-done.9 = bf16[304,128]{1,0:T(8,128)(2,1)S(1)} collective-permute-done((bf16[304,128]{1,0:T(8,128)(2,1)S(1)}, bf16[304,128]{1,0:T(8,128)(2,1)S(1)}, u32[]{:S(2)}, u32[]{:S(2)}) %collective-permute-start.9) | collective-permute-done | bytes 77856 | tf_op jit(solution)/shard_map/ppermute | solution.py:586
  32.4 3.1 %collective-permute-start.10 = (bf16[304,128]{1,0:T(8,128)(2,1)S(1)}, bf16[304,128]{1,0:T(8,128)(2,1)S(1)}, u32[]{:S(2)}, u32[]{:S(2)}) collective-permute-start(bf16[304,128]{1,0:T(8,128)(2,1)S(1)} %add_convert_fusion.1), channel_id=1, source_target_pairs={{0,16},{1,5},{2,18},{3,7},{4,20},{5,1},{6,22},{7,3},{8,24},{9,13},... | collective-permute-start | bytes 233480 | tf_op jit(solution)/shard_map/ppermute | solution.py:586
  35.5 2.4 %collective-permute-done.10 = bf16[304,128]{1,0:T(8,128)(2,1)S(1)} collective-permute-done((bf16[304,128]{1,0:T(8,128)(2,1)S(1)}, bf16[304,128]{1,0:T(8,128)(2,1)S(1)}, u32[]{:S(2)}, u32[]{:S(2)}) %collective-permute-start.10) | collective-permute-done | bytes 77856 | tf_op jit(solution)/shard_map/ppermute | solution.py:586
  37.9 0.1 collective-permute-start.11
  38.0 1.7 %shard_map.199 = bf16[2304,256]{1,0:T(8,128)(2,1)} custom-call(f32[2304,256]{1,0:T(8,128)S(1)} %get-tuple-element.59.pre3, f32[8,256]{1,0:T(8,128)S(1)} %get-tuple-element.60.own3, f32[8,256]{1,0:T(8,128)S(1)} %collective-permute-done.2.rec3, f32[8,256]{1,0:T(8,128)S(1)} %get-tuple-element.54.prm, f32[2304,256]{1,0:T(8,128)S(1)} %get-tuple-element.63.im_half), custom_call_target="tpu_custom_call" | custom-call | flops 5898240 | bytes 7102464 | tf_op jit(solution)/shard_map/pallas_call | solution.py:543
  39.7 1.5 %shard_map.207 = bf16[2304,256]{1,0:T(8,128)(2,1)} custom-call(bf16[1152,128]{1,0:T(8,128)(2,1)S(1)} %get-tuple-element.78.dh1, bf16[64,256]{1,0:T(8,128)(2,1)S(1)} %get-tuple-element.79.w, f32[2304,256]{1,0:T(8,128)S(1)} %get-tuple-element.65.e3), custom_call_target="tpu_custom_call" | custom-call | flops 150994944 | bytes 5046272 | tf_op jit(solution)/shard_map/pallas_call | solution.py:543
  41.2 0.0 collective-permute-done.11.refs_1_
  41.2 0.9 %shard_map.208 = (f32[64,256]{1,0:T(8,128)}, f32[9,64,64]{2,1,0:T(8,128)}, f32[64,256]{1,0:T(8,128)}, f32[1,64]{1,0:T(1,128)}, f32[1,64]{1,0:T(1,128)}, /*index=...) custom-call(bf16[304,128]{1,0:T(8,128)(2,1)S(1)} %add_convert_fusion.refs_0_, ...), custom_call_target="tpu_custom_call" | custom-call | bytes 437248 | tf_op jit(solution)/shard_map/pallas_call | solution.py:543
  (5 shorter events, 0.1 us)
Async XLA Ops:
  3.2 5.1 %copy-start = (bf16[1,8,288,256]{3,2,1,0:T(8,128)(2,1)S(1)}, bf16[1,8,288,256]{3,2,1,0:T(8,128)(2,1)}, u32[]{:S(2)}) copy-start(bf16[1,8,288,256]{3,2,1,0:T(8,128)(2,1)} %param.21) | copy-start | bytes 3538948
  3.2 1.7 %collective-permute-start = (bf16[592,128]{1,0:T(8,128)(2,1)S(1)}, bf16[592,128]{1,0:T(8,128)(2,1)S(1)}, u32[]{:S(2)}, u32[]{:S(2)}) collective-permute-start(bf16[592,128]{1,0:T(8,128)(2,1)S(1)} %get-tuple-element.53.own1), channel_id=1, source_target_pairs={{0,1},{1,0},{2,3},{3,2},{4,5},{5,4},{6,7},{7,6},{8,9},{9,8},{10,11... | collective-permute-start | bytes 454664 | tf_op jit(solution)/shard_map/ppermute | solution.py:557
  6.1 1.2 %collective-permute-start.1 = (f32[8,128]{1,0:T(8,128)S(1)}, f32[8,128]{1,0:T(8,128)S(1)}, u32[]{:S(2)}, u32[]{:S(2)}) collective-permute-start(f32[8,128]{1,0:T(8,128)S(1)} %get-tuple-element.57.own2), channel_id=1, source_target_pairs={{0,1},{1,0},{2,3},{3,2},{4,5},{5,4},{6,7},{7,6},{8,9},{9,8},{10,11... | collective-permute-start | bytes 12296 | tf_op jit(solution)/shard_map/ppermute | solution.py:557
  8.0 1.2 %collective-permute-start.2 = (f32[8,256]{1,0:T(8,128)S(1)}, f32[8,256]{1,0:T(8,128)S(1)}, u32[]{:S(2)}, u32[]{:S(2)}) collective-permute-start(f32[8,256]{1,0:T(8,128)S(1)} %get-tuple-element.60.own3), channel_id=1, source_target_pairs={{0,1},{1,0},{2,3},{3,2},{4,5},{5,4},{6,7},{7,6},{8,9},{9,8},{10,11... | collective-permute-start | bytes 24584 | tf_op jit(solution)/shard_map/ppermute | solution.py:557
  10.5 1.2 %collective-permute-start.3 = (f32[8,256]{1,0:T(8,128)S(1)}, f32[8,256]{1,0:T(8,128)S(1)}, u32[]{:S(2)}, u32[]{:S(2)}) collective-permute-start(f32[8,256]{1,0:T(8,128)S(1)} %get-tuple-element.66.own4), channel_id=1, source_target_pairs={{0,1},{1,0},{2,3},{3,2},{4,5},{5,4},{6,7},{7,6},{8,9},{9,8},{10,11... | collective-permute-start | bytes 24584 | tf_op jit(solution)/shard_map/ppermute | solution.py:557
  12.5 1.7 %collective-permute-start.4 = (bf16[1168,128]{1,0:T(8,128)(2,1)S(1)}, bf16[1168,128]{1,0:T(8,128)(2,1)S(1)}, u32[]{:S(2)}, u32[]{:S(2)}) collective-permute-start(bf16[1168,128]{1,0:T(8,128)(2,1)S(1)} %get-tuple-element.69.own5), channel_id=1, source_target_pairs={{0,1},{1,0},{2,3},{3,2},{4,5},{5,4},{6,7},{7,6},{8,9},{9,8},{10,11... | collective-permute-start | bytes 897032 | tf_op jit(solution)/shard_map/ppermute | solution.py:557
  15.2 1.2 %collective-permute-start.5 = (f32[8,128]{1,0:T(8,128)S(1)}, f32[8,128]{1,0:T(8,128)S(1)}, u32[]{:S(2)}, u32[]{:S(2)}) collective-permute-start(f32[8,128]{1,0:T(8,128)S(1)} %get-tuple-element.73.own6), channel_id=1, source_target_pairs={{0,1},{1,0},{2,3},{3,2},{4,5},{5,4},{6,7},{7,6},{8,9},{9,8},{10,11... | collective-permute-start | bytes 12296 | tf_op jit(solution)/shard_map/ppermute | solution.py:557
  16.8 1.3 %collective-permute-start.6 = (bf16[304,128]{1,0:T(8,128)(2,1)S(1)}, bf16[304,128]{1,0:T(8,128)(2,1)S(1)}, u32[]{:S(2)}, u32[]{:S(2)}) collective-permute-start(bf16[304,128]{1,0:T(8,128)(2,1)S(1)} %get-tuple-element.81), channel_id=1, source_target_pairs={{0,1},{1,0},{2,3},{3,2},{4,5},{5,4},{6,7},{7,6},{8,9},{9,8},{10,11... | collective-permute-start | bytes 233480 | tf_op jit(solution)/shard_map/ppermute | solution.py:557
  18.1 5.2 %collective-permute-start.7 = (bf16[304,128]{1,0:T(8,128)(2,1)S(1)}, bf16[304,128]{1,0:T(8,128)(2,1)S(1)}, u32[]{:S(2)}, u32[]{:S(2)}) collective-permute-start(bf16[304,128]{1,0:T(8,128)(2,1)S(1)} %add_convert_fusion.4), channel_id=1, source_target_pairs={{0,2},{1,9},{2,0},{3,11},{4,6},{5,13},{6,4},{7,15},{8,10},{9,1},{1... | collective-permute-start | bytes 233480 | tf_op jit(solution)/shard_map/ppermute | solution.py:586
  23.3 4.5 %collective-permute-start.8 = (bf16[304,128]{1,0:T(8,128)(2,1)S(1)}, bf16[304,128]{1,0:T(8,128)(2,1)S(1)}, u32[]{:S(2)}, u32[]{:S(2)}) collective-permute-start(bf16[304,128]{1,0:T(8,128)(2,1)S(1)} %add_convert_fusion.3), channel_id=1, source_target_pairs={{0,4},{1,17},{2,6},{3,19},{4,0},{5,21},{6,2},{7,23},{8,12},{9,25},... | collective-permute-start | bytes 233480 | tf_op jit(solution)/shard_map/ppermute | solution.py:586
  27.9 4.5 %collective-permute-start.9 = (bf16[304,128]{1,0:T(8,128)(2,1)S(1)}, bf16[304,128]{1,0:T(8,128)(2,1)S(1)}, u32[]{:S(2)}, u32[]{:S(2)}) collective-permute-start(bf16[304,128]{1,0:T(8,128)(2,1)S(1)} %add_convert_fusion.2), channel_id=1, source_target_pairs={{0,8},{1,3},{2,10},{3,1},{4,12},{5,7},{6,14},{7,5},{8,0},{9,11},{1... | collective-permute-start | bytes 233480 | tf_op jit(solution)/shard_map/ppermute | solution.py:586
  32.4 5.5 %collective-permute-start.10 = (bf16[304,128]{1,0:T(8,128)(2,1)S(1)}, bf16[304,128]{1,0:T(8,128)(2,1)S(1)}, u32[]{:S(2)}, u32[]{:S(2)}) collective-permute-start(bf16[304,128]{1,0:T(8,128)(2,1)S(1)} %add_convert_fusion.1), channel_id=1, source_target_pairs={{0,16},{1,5},{2,18},{3,7},{4,20},{5,1},{6,22},{7,3},{8,24},{9,13},... | collective-permute-start | bytes 233480 | tf_op jit(solution)/shard_map/ppermute | solution.py:586
  37.9 3.3 %collective-permute-start.11 = (bf16[304,128]{1,0:T(8,128)(2,1)S(1)}, bf16[304,128]{1,0:T(8,128)(2,1)S(1)}, u32[]{:S(2)}, u32[]{:S(2)}) collective-permute-start(bf16[304,128]{1,0:T(8,128)(2,1)S(1)} %add_convert_fusion.refs_0_), channel_id=1, source_target_pairs={{0,1},{1,0},{2,3},{3,2},{4,5},{5,4},{6,7},{7,6},{8,9},{9,8},{10,11... | collective-permute-start | bytes 233480 | tf_op jit(solution)/shard_map/ppermute | solution.py:557

commit v2 on v1

--- a/solution.py
+++ b/solution.py
@@ -130,24 +130,29 @@
     return rowsum(acc)
 
 
-def first_kernel(edge, im, w, pre, msg, im_held, w_held, im_near, w_near, sems):
-    half, cols = pre.shape[0], edge // 2
-    fetch_w = pltpu.make_async_copy(w, w_near, sems.at[0])
-    fetch_w.start()
+def first_kernel(edge, *refs):
+    im, far = refs[0], refs[1:10]
+    pre, msg, im_held, w_held, wd_held, we_held, prm = refs[10:17]
+    im_near, near, sems = refs[17], refs[18:27], refs[27]
+    half, cols, wide = pre.shape[0], edge // 2, pre.shape[1]
+    small = [pltpu.make_async_copy(a, b, sems.at[k]) for k, (a, b) in enumerate(zip(far, near))]
+    small[0].start()
     copies = []
     for at in range(0, half, cols):
         for base in (at, half + at):
             rows = pl.ds(base, cols)
-            sem = sems.at[1 + len(copies)]
+            sem = sems.at[len(small) + len(copies)]
             copies.append(pltpu.make_async_copy(im.at[rows, :], im_near.at[rows, :], sem))
             copies[-1].start()
-    fetch_w.wait()
-    weight = w_near[...]
+    for item in small[1:]:
+        item.start()
+    small[0].wait()
+    weight = near[0][...]
     w_held[...] = weight
     zero = jnp.zeros_like(weight)
     upper = jnp.concatenate([weight, zero], 0)
     lower = jnp.concatenate([zero, weight], 0)
-    acc = jnp.zeros((8, pre.shape[1]), F32)
+    acc = jnp.zeros((8, wide), F32)
     for k, at in enumerate(range(0, half, cols)):
         part = None
         for copy, base, side in ((2 * k, at, upper), (2 * k + 1, half + at, lower)):
@@ -161,6 +166,15 @@
     mean = both_halves(rowsum(acc)) / (2 * half)
     msg[0:WIDE_HEAD, :] = wide_head_rows(mean, both_halves(centred_squares(pre, mean, cols)))
     msg[WIDE_HEAD:, :] = edges(pre, edge, mean).astype(BF16)
+    for item in small[1:]:
+        item.wait()
+    wd_held[...] = near[1][...]
+    we_held[...] = near[2][...]
+    prm[...] = jnp.zeros(prm.shape, F32)
+    for k, ref in enumerate(near[3:7]):
+        prm[k : k + 1, 0:wide] = jnp.concatenate([ref[...], ref[...]], 1)
+    prm[4:5, :] = near[7][...]
+    prm[5:6, :] = near[8][...]
 
 
 def tap_blocks(w):
@@ -174,24 +188,20 @@
             )
 
 
-def weights_kernel(*refs):
-    far, (we_held, fwd, bwd, prm), near, sems = refs[:8], refs[8:12], refs[12:-1], refs[-1]
-    copies = [pltpu.make_async_copy(a, b, sems.at[k]) for k, (a, b) in enumerate(zip(far, near))]
-    for item in copies:
-        item.start()
-    for item in copies:
-        item.wait()
-    wide = 2 * near[0].shape[-1]
-    for a, b, both in tap_blocks(near[0]):
+def fetch_rows(far, near, sem, base):
+    return pltpu.make_async_copy(far.at[pl.ds(base, near.shape[0]), :], near, sem)
+
+
+def weights_kernel(wd, cot, fwd, bwd, cot_held, cot_near, sem):
+    fetch = fetch_rows(cot, cot_near, sem, 0)
+    fetch.start()
+    wide = 2 * wd.shape[-1]
+    for a, b, both in tap_blocks(wd):
         k = 2 - a
         fwd[a * wide : (a + 1) * wide, b * wide : (b + 1) * wide] = both
         bwd[b * wide : (b + 1) * wide, k * wide : (k + 1) * wide] = both
-    prm[...] = jnp.zeros(prm.shape, F32)
-    we_held[...] = near[7][...]
-    for k, ref in enumerate(near[1:5]):
-        prm[k : k + 1, 0:wide] = jnp.concatenate([ref[...], ref[...]], 1)
-    prm[4:5, :] = near[5][...]
-    prm[5:6, :] = near[6][...]
+    fetch.wait()
+    cot_held[...] = cot_near[...]
 
 
 def gain_shift(prm, norm, wide):
@@ -216,9 +226,11 @@
 
 
 def second_kernel(
-    peers, edge, pre1, own1, rec1, prm, w, ext, pre2, msg, scr
+    peers, edge, pre1, own1, rec1, prm, w, cot, ext, pre2, msg, cot_held, scr, cot_near, sem
 ):
     half, cols, wide = pre2.shape[0], edge // 2, pre2.shape[1]
+    fetch = fetch_rows(cot, cot_near, sem, cot.shape[0] - cot_near.shape[0])
+    fetch.start()
     g1, s1 = gain_shift(prm, 0, wide)
     mean, inv = moments(own1, rec1, peers, 2.0 * half)
     scale, bias = norm_coefs(g1, s1, mean, inv)
@@ -253,6 +265,8 @@
         acc = acc + group(part)
     mean = both_halves(rowsum(acc)) / (2 * half)
     msg[...] = head_rows(mean, both_halves(centred_squares(pre2, mean, cols)))
+    fetch.wait()
+    cot_held[...] = cot_near[...]
 
 
 def third_kernel(peers, cols, pre2, own2, rec2, prm, w, act2, pre3, msg):
@@ -278,14 +292,18 @@
     msg[...] = head_rows(mean, centred_squares(pre3, mean, cols))
 
 
-def halves_kernel(step, im, cot, im_half, cot_half):
-    def body(i, carry):
-        at = pl.ds(pl.multiple_of(i * step, step), step)
+def halves_kernel(step, im, cot_first, cot_last, im_half, cot_half):
+    split = cot_first.shape[0]
+
+    def body(base, cot, i, carry):
+        near = pl.ds(pl.multiple_of(i * step, step), step)
+        at = pl.ds(pl.multiple_of(base + i * step, step), step)
         im_half[at, :] = 0.5 * im[at, :].astype(F32)
-        cot_half[at, :] = 0.5 * cot[at, :].astype(F32)
+        cot_half[at, :] = 0.5 * cot[near, :].astype(F32)
         return carry
 
-    lax.fori_loop(0, im.shape[0] // step, body, 0, unroll=2)
+    for base, cot in ((0, cot_first), (split, cot_last)):
+        lax.fori_loop(0, cot.shape[0] // step, functools.partial(body, base, cot), 0)
 
 
 def slopes_kernel(peers, step, pre1, own1, rec1, pre2, own2, rec2, prm, slope1, slope2):
@@ -572,19 +590,29 @@
     return jnp.concatenate(heads, 0)
 
 
+def flipped_dp(part, masks):
+    count, sides = lax.axis_size("dp"), lax.axis_size("space")
+    pairs = []
+    for i in range(count * sides):
+        dp, side = divmod(i, sides)
+        pairs.append((i, (dp ^ masks[side % len(masks)]) * sides + side))
+    return lax.ppermute(part, ("dp", "space"), pairs).astype(F32)
+
+
 def summed_over_dp(part):
-    count, sides = lax.axis_size("dp"), lax.axis_size("space")
+    count = lax.axis_size("dp")
     if count & (count - 1):
         return lax.psum(part.astype(F32), "dp").astype(BF16)
     bits = [1 << k for k in range(count.bit_length() - 1)]
-    for k in range(len(bits)):
-        pairs = []
-        for i in range(count * sides):
-            dp, side = divmod(i, sides)
-            bit = bits[(k + side * (len(bits) // 2)) % len(bits)]
-            pairs.append((i, (dp ^ bit) * sides + side))
-        got = lax.ppermute(part, ("dp", "space"), pairs)
-        part = (part.astype(F32) + got.astype(F32)).astype(BF16)
+    twos = [bits[k : k + 2] for k in range(0, len(bits) - 1, 2)]
+    for k in range(len(twos)):
+        turn = [twos[(k + side * (len(twos) // 2)) % len(twos)] for side in range(2)]
+        low = flipped_dp(part, [pair[0] for pair in turn])
+        high = flipped_dp(part, [pair[1] for pair in turn])
+        both = flipped_dp(part, [pair[0] + pair[1] for pair in turn])
+        part = ((part.astype(F32) + low) + (high + both)).astype(BF16)
+    if len(bits) % 2:
+        part = (part.astype(F32) + flipped_dp(part, bits[-1:])).astype(BF16)
     return part
 
 
@@ -609,33 +637,38 @@
     w_rows = w_reduce.T
     gates = 2 * pixels * wide * chans
 
-    pre1, own1, im_held, w_held = call(
+    small = (w_rows, w_dilated, w_expand) + tuple(
+        row(item)
+        for item in (gain_one, shift_one, gain_two, shift_two, gain_three, shift_three)
+    )
+    pre1, own1, im_held, w_held, wd_held, we, prm = call(
         part(first_kernel, edge),
         [((half, wide), F32), ((WIDE_HEAD + edge, wide), BF16), ((pixels, chans), BF16)]
-        + [(w_rows.shape, BF16)],
-        im, w_rows, flops=gates, far=(0, 1),
-        scratch=[pltpu.VMEM((pixels, chans), BF16), pltpu.VMEM(w_rows.shape, BF16)]
-        + [pltpu.SemaphoreType.DMA((2 * chunks + 1,))],
-    )
-    own1, cot = lax.optimization_barrier((own1, cot))
+        + [(item.shape, BF16) for item in small[:3]] + [((8, chans), F32)],
+        im, *small, flops=gates, far=tuple(range(10)),
+        scratch=[pltpu.VMEM((pixels, chans), BF16)]
+        + [pltpu.VMEM(item.shape, item.dtype) for item in small]
+        + [pltpu.SemaphoreType.DMA((2 * chunks + len(small),))],
+    )
     rec1 = exchanged(own1, peers)
-    we, fwd, bwd, prm = call(
+    split = edge
+    held = lambda n: pltpu.VMEM((n, chans), BF16)
+    fwd, bwd, cot_first = call(
         weights_kernel,
-        [(w_expand.shape, BF16)] + [((3 * wide, 3 * wide), BF16)] * 2 + [((8, chans), F32)],
-        w_dilated, row(gain_one), row(shift_one), row(gain_two), row(shift_two),
-        row(gain_three), row(shift_three), w_expand, flops=10**6, far=tuple(range(8)),
-        scratch=[pltpu.VMEM(w_dilated.shape, BF16)] + [pltpu.VMEM((1, mids), F32)] * 4
-        + [pltpu.VMEM((1, chans), F32)] * 2 + [pltpu.VMEM(w_expand.shape, BF16)]
-        + [pltpu.SemaphoreType.DMA((8,))],
-    )
-    ext, pre2, own2 = call(
+        [((3 * wide, 3 * wide), BF16)] * 2 + [((split, chans), BF16)], wd_held, cot,
+        flops=10**6, far=(1,), scratch=[held(split), pltpu.SemaphoreType.DMA],
+    )
+    ext, pre2, own2, cot_last = call(
         part(second_kernel, peers, edge),
-        [((ext_rows, wide), BF16), ((half, wide), F32), ((HEAD, wide), F32)],
-        pre1, own1, rec1, prm, fwd, scratch=[gaps(2 * chunks)], flops=2 * half * 9 * wide * wide,
+        [((ext_rows, wide), BF16), ((half, wide), F32), ((HEAD, wide), F32)]
+        + [((pixels - split, chans), BF16)],
+        pre1, own1, rec1, prm, fwd, cot, far=(5,),
+        scratch=[gaps(2 * chunks), held(pixels - split), pltpu.SemaphoreType.DMA],
+        flops=2 * half * 9 * wide * wide,
     )
     rec2 = exchanged(own2, peers)
     im_half, cot_half = call(
-        part(halves_kernel, 64), [((pixels, chans), F32)] * 2, im_held, cot,
+        part(halves_kernel, 64), [((pixels, chans), F32)] * 2, im_held, cot_first, cot_last,
         flops=4 * pixels * chans,
     )
     act2, pre3, own3 = call(

time: 42.4 us -> 40.9 us (0.965)
  waiting for transfers between devices: 13.3 us -> 12.2 us
  starting transfers between devices: 12.6 us -> 11.8 us
    ppermute x4 -> x6, starting transfers between devices: 10.1 us -> 8.85 us  [flipped_dp(): return lax.ppermute(part, ('dp', 'space'), pairs).astype(F32)]
    ppermute x4 -> x6, waiting for transfers between devices: 9.51 us -> 8.77 us  [flipped_dp(): return lax.ppermute(part, ('dp', 'space'), pairs).astype(F32)]
    ppermute x8, starting transfers between devices: 2.43 us -> 2.95 us  [swapped(): lax.ppermute(value, axis, [(i, (i + step) % count) for i in range(count)])]
    pallas_call x15, Pallas kernels: 15.3 us -> 15.7 us  [call(): pl.pallas_call(kernel, out_shape=[kind_of(shape, kind) for shape, kind in...]
  transfers between devices with their start and end apart: 12 -> 14, of which waited for: 9 -> 10; matrix products, arithmetic and copies ran while one was open for 0% -> 0% of each run, Pallas kernels for 15% -> 16%
where the time goes in v2:
time: 40.9 us; the launch traced here: 40.6 us
  Pallas kernels  15.7 us (38%)
  waiting for transfers between devices  12.2 us (30%)
  starting transfers between devices  11.8 us (29%)
  between operations  0.76 us (2%)
    pallas_call x15, Pallas kernels, call(): pl.pallas_call(kernel, out_shape=[kind_of(shape, kind) for shape, kind in...  15.7 us
    ppermute x6, starting transfers between devices, flipped_dp(): return lax.ppermute(part, ('dp', 'space'), pairs).astype(F32)  8.85 us
    ppermute x6, waiting for transfers between devices, flipped_dp(): return lax.ppermute(part, ('dp', 'space'), pairs).astype(F32)  8.77 us
    ppermute x8, waiting for transfers between devices, swapped(): lax.ppermute(value, axis, [(i, (i + step) % count) for i in range(count)])  3.47 us
    ppermute x8, starting transfers between devices, swapped(): lax.ppermute(value, axis, [(i, (i + step) % count) for i in range(count)])  2.95 us
  transfers between devices with their start and end apart: 14, of which 10 were waited for; matrix products, arithmetic and copies ran while one was open for 0% of the time, Pallas kernels for 16%

profile of v2, /device:TPU:0, one launch (start us, length us, event | category | flops | bytes accessed | tf_op | source)
XLA Modules:
  0.0 40.6 jit_solution(3371494701831255561)
XLA Ops:
  0.6 2.8 %shard_map.194 = (f32[1152,128]{1,0:T(8,128)S(1)}, bf16[592,128]{1,0:T(8,128)(2,1)S(1)}, bf16[2304,256]{1,0:T(8,128)(2,1)S(1)}, bf16[64,256]{1,0:T(8,128)(2,1)S(...) custom-call(bf16[2304,256]{1,0:T(8,128)(2,1)} %bitcast.21, ...), custom_call_target="tpu_custom_call" | custom-call | flops 150994944 | bytes 4860928 | tf_op jit(solution)/shard_map/pallas_call | solution.py:561
  3.4 0.6 %collective-permute-start = (bf16[592,128]{1,0:T(8,128)(2,1)S(1)}, bf16[592,128]{1,0:T(8,128)(2,1)S(1)}, u32[]{:S(2)}, u32[]{:S(2)}) collective-permute-start(bf16[592,128]{1,0:T(8,128)(2,1)S(1)} %get-tuple-element.53.own1), channel_id=1, source_target_pairs={{0,1},{1,0},{2,3},{3,2},{4,5},{5,4},{6,7},{7,6},{8,9},{9,8},{10,11... | collective-permute-start | bytes 454664 | tf_op jit(solution)/shard_map/ppermute | solution.py:575
  4.0 1.0 %shard_map.195 = (bf16[384,384]{1,0:T(8,128)(2,1)S(1)}, bf16[384,384]{1,0:T(8,128)(2,1)S(1)}, bf16[576,256]{1,0:T(8,128)(2,1)S(1)}) custom-call(bf16[3,3,64,64]{3,2,1,0:T(8,128)(2,1)S(1)} %get-tuple-element.55.wd, bf16[2304,256]{1,0:T(8,128)(2,1)} %bitcast.19), custom_call_target="tpu_custom_call" | custom-call | flops 1000000 | bytes 3022848 | tf_op jit(solution)/shard_map/pallas_call | solution.py:561
  5.0 0.0 collective-permute-done.rec1
  5.0 1.6 %shard_map.196 = (bf16[2304,128]{1,0:T(8,128)(2,1)S(1)}, f32[1152,128]{1,0:T(8,128)S(1)}, f32[8,128]{1,0:T(8,128)S(1)}, bf16[1728,256]{1,0:T(8,128)(2,1)S(1)}) custom-call(f32[1152,128]{1,0:T(8,128)S(1)} %get-tuple-element.52.pre1, bf16[592,128]{1,0:T(8,128)(2,1)S(1)} %get-tuple-element.53.own1, bf16[592,128]{1,0:T(8,128)(2,1)S(1)} %collective-permute-done.rec1, ...), custom_call_target="tpu_custom_call" | custom-call | flops 339738624 | bytes 5918720 | tf_op jit(solution)/shard_map/pallas_call | solution.py:561
  6.6 0.4 %collective-permute-start.1 = (f32[8,128]{1,0:T(8,128)S(1)}, f32[8,128]{1,0:T(8,128)S(1)}, u32[]{:S(2)}, u32[]{:S(2)}) collective-permute-start(f32[8,128]{1,0:T(8,128)S(1)} %get-tuple-element.58.own2), channel_id=1, source_target_pairs={{0,1},{1,0},{2,3},{3,2},{4,5},{5,4},{6,7},{7,6},{8,9},{9,8},{10,11... | collective-permute-start | bytes 12296 | tf_op jit(solution)/shard_map/ppermute | solution.py:575
  7.0 0.8 %collective-permute-done.1.rec2 = f32[8,128]{1,0:T(8,128)S(1)} collective-permute-done((f32[8,128]{1,0:T(8,128)S(1)}, f32[8,128]{1,0:T(8,128)S(1)}, u32[]{:S(2)}, u32[]{:S(2)}) %collective-permute-start.1) | collective-permute-done | bytes 4128 | tf_op jit(solution)/shard_map/ppermute | solution.py:575
  7.8 0.8 %shard_map.197 = (bf16[1152,128]{1,0:T(8,128)(2,1)S(1)}, f32[2304,256]{1,0:T(8,128)S(1)}, f32[8,256]{1,0:T(8,128)S(1)}) custom-call(f32[1152,128]{1,0:T(8,128)S(1)} %get-tuple-element.57.pre2, f32[8,128]{1,0:T(8,128)S(1)} %get-tuple-element.58.own2, f32[8,128]{1,0:T(8,128)S(1)} %collective-permute-done.1.rec2, f32[8,256]{1,0:T(8,128)S(1)} %get-tuple-element.54.prm, ...), custom_call_target="tpu_custom_call" | custom-call | flops 150994944 | bytes 3596288 | tf_op jit(solution)/shard_map/pallas_call | solution.py:561
  8.6 0.4 collective-permute-start.2
  9.0 0.5 %shard_map.198 = (f32[2304,256]{1,0:T(8,128)S(1)}, f32[2304,256]{1,0:T(8,128)S(1)}) custom-call(bf16[2304,256]{1,0:T(8,128)(2,1)S(1)} %get-tuple-element.62.im, bf16[576,256]{1,0:T(8,128)(2,1)S(1)} %get-tuple-element.63.cot_first, bf16[1728,256]{1,0:T(8,128)(2,1)S(1)} %get-tuple-element.64.cot_last), custom_call_target="tpu_custom_call" | custom-call | flops 2359296 | bytes 7077888 | tf_op jit(solution)/shard_map/pallas_call | solution.py:561
  9.5 0.4 collective-permute-done.2.rec3
  9.8 1.2 %shard_map.200 = (f32[2304,256]{1,0:T(8,128)S(1)}, f32[8,256]{1,0:T(8,128)S(1)}) custom-call(f32[2304,256]{1,0:T(8,128)S(1)} %get-tuple-element.60.pre3, f32[8,256]{1,0:T(8,128)S(1)} %get-tuple-element.61.own3, f32[8,256]{1,0:T(8,128)S(1)} %collective-permute-done.2.rec3, f32[8,256]{1,0:T(8,128)S(1)} %get-tuple-element.54.prm, ...), custom_call_target="tpu_custom_call" | custom-call | flops 17694720 | bytes 9469952 | tf_op jit(solution)/shard_map/pallas_call | solution.py:561
  11.1 0.4 collective-permute-start.3
  11.5 0.4 %shard_map.201 = (f32[1152,128]{1,0:T(8,128)S(1)}, f32[1152,128]{1,0:T(8,128)S(1)}) custom-call(f32[1152,128]{1,0:T(8,128)S(1)} %get-tuple-element.52.pre1, bf16[592,128]{1,0:T(8,128)(2,1)S(1)} %get-tuple-element.53.own1, bf16[592,128]{1,0:T(8,128)(2,1)S(1)} %collective-permute-done.rec1, f32[1152,128]{1,0:T(8,128)S(1)} %get-tuple-element.57.pre2, ...), custom_call_target="tpu_custom_call" | custom-call | flops 4423680 | bytes 2678784 | tf_op jit(solution)/shard_map/pallas_call | solution.py:561
  11.9 0.4 collective-permute-done.3.rec4
  12.3 0.7 %shard_map.202 = (bf16[2304,256]{1,0:T(8,128)(2,1)S(1)}, f32[1152,128]{1,0:T(8,128)S(1)}, bf16[1168,128]{1,0:T(8,128)(2,1)S(1)}) custom-call(f32[2304,256]{1,0:T(8,128)S(1)} %get-tuple-element.60.pre3, f32[2304,256]{1,0:T(8,128)S(1)} %get-tuple-element.67.e3, f32[8,256]{1,0:T(8,128)S(1)} %get-tuple-element.61.own3, ...), custom_call_target="tpu_custom_call" | custom-call | flops 150994944 | bytes 9527296 | tf_op jit(solution)/shard_map/pallas_call | solution.py:561
  13.0 0.4 collective-permute-start.4
  13.4 0.4 shard_map.205.gwe
  13.8 0.9 %collective-permute-done.4.rec5 = bf16[1168,128]{1,0:T(8,128)(2,1)S(1)} collective-permute-done((bf16[1168,128]{1,0:T(8,128)(2,1)S(1)}, bf16[1168,128]{1,0:T(8,128)(2,1)S(1)}, u32[]{:S(2)}, u32[]{:S(2)}) %collective-permute-start.4) | collective-permute-done | bytes 299040 | tf_op jit(solution)/shard_map/ppermute | solution.py:575
  14.7 1.1 %shard_map.203 = (bf16[2304,128]{1,0:T(8,128)(2,1)S(1)}, f32[1152,128]{1,0:T(8,128)S(1)}, f32[8,128]{1,0:T(8,128)S(1)}) custom-call(f32[1152,128]{1,0:T(8,128)S(1)} %get-tuple-element.57.pre2, f32[1152,128]{1,0:T(8,128)S(1)} %get-tuple-element.70.e2, bf16[1168,128]{1,0:T(8,128)(2,1)S(1)} %get-tuple-element.71.own5, ...), custom_call_target="tpu_custom_call" | custom-call | flops 339738624 | bytes 5345280 | tf_op jit(solution)/shard_map/pallas_call | solution.py:561
  15.8 0.3 collective-permute-start.5
  16.1 0.9 %shard_map.204.gwd = bf16[320,128]{1,0:T(8,128)(2,1)S(1)} custom-call(bf16[2304,128]{1,0:T(8,128)(2,1)S(1)} %get-tuple-element.76.ext, bf16[2304,128]{1,0:T(8,128)(2,1)S(1)} %get-tuple-element.77.dext), custom_call_target="tpu_custom_call" | custom-call | flops 339738624 | bytes 1343488 | tf_op jit(solution)/shard_map/pallas_call | solution.py:561
  17.0 0.0 collective-permute-done.5.rec6
  17.0 0.4 %shard_map.206 = (bf16[1152,128]{1,0:T(8,128)(2,1)S(1)}, bf16[304,128]{1,0:T(8,128)(2,1)S(1)}, bf16[304,128]{1,0:T(8,128)(2,1)S(1)}) custom-call(f32[1152,128]{1,0:T(8,128)S(1)} %get-tuple-element.52.pre1, f32[1152,128]{1,0:T(8,128)S(1)} %get-tuple-element.74.e1, f32[8,128]{1,0:T(8,128)S(1)} %get-tuple-element.75.own6, ...), custom_call_target="tpu_custom_call" | custom-call | flops 150994944 | bytes 4034560 | tf_op jit(solution)/shard_map/pallas_call | solution.py:561
  17.4 0.3 collective-permute-start.6
  17.7 1.0 %collective-permute-done.6 = bf16[304,128]{1,0:T(8,128)(2,1)S(1)} collective-permute-done((bf16[304,128]{1,0:T(8,128)(2,1)S(1)}, bf16[304,128]{1,0:T(8,128)(2,1)S(1)}, u32[]{:S(2)}, u32[]{:S(2)}) %collective-permute-start.6) | collective-permute-done | bytes 77856 | tf_op jit(solution)/shard_map/ppermute | solution.py:575
  18.8 3.8 %collective-permute-start.9 = (bf16[304,128]{1,0:T(8,128)(2,1)S(1)}, bf16[304,128]{1,0:T(8,128)(2,1)S(1)}, u32[]{:S(2)}, u32[]{:S(2)}) collective-permute-start(bf16[304,128]{1,0:T(8,128)(2,1)S(1)} %add_convert_fusion.2), channel_id=1, source_target_pairs={{0,6},{1,25},{2,4},{3,27},{4,2},{5,29},{6,0},{7,31},{8,14},{9,17},... | collective-permute-start | bytes 233480 | tf_op jit(solution)/shard_map/ppermute | solution.py:599
  22.5 0.5 %collective-permute-start.8 = (bf16[304,128]{1,0:T(8,128)(2,1)S(1)}, bf16[304,128]{1,0:T(8,128)(2,1)S(1)}, u32[]{:S(2)}, u32[]{:S(2)}) collective-permute-start(bf16[304,128]{1,0:T(8,128)(2,1)S(1)} %add_convert_fusion.2), channel_id=1, source_target_pairs={{0,4},{1,17},{2,6},{3,19},{4,0},{5,21},{6,2},{7,23},{8,12},{9,25},... | collective-permute-start | bytes 233480 | tf_op jit(solution)/shard_map/ppermute | solution.py:599
  23.0 0.1 collective-permute-start.7
  23.2 1.7 %collective-permute-done.9 = bf16[304,128]{1,0:T(8,128)(2,1)S(1)} collective-permute-done((bf16[304,128]{1,0:T(8,128)(2,1)S(1)}, bf16[304,128]{1,0:T(8,128)(2,1)S(1)}, u32[]{:S(2)}, u32[]{:S(2)}) %collective-permute-start.9) | collective-permute-done | bytes 77856 | tf_op jit(solution)/shard_map/ppermute | solution.py:599
  24.9 2.0 %collective-permute-done.8 = bf16[304,128]{1,0:T(8,128)(2,1)S(1)} collective-permute-done((bf16[304,128]{1,0:T(8,128)(2,1)S(1)}, bf16[304,128]{1,0:T(8,128)(2,1)S(1)}, u32[]{:S(2)}, u32[]{:S(2)}) %collective-permute-start.8) | collective-permute-done | bytes 77856 | tf_op jit(solution)/shard_map/ppermute | solution.py:599
  26.9 0.5 %collective-permute-done.7 = bf16[304,128]{1,0:T(8,128)(2,1)S(1)} collective-permute-done((bf16[304,128]{1,0:T(8,128)(2,1)S(1)}, bf16[304,128]{1,0:T(8,128)(2,1)S(1)}, u32[]{:S(2)}, u32[]{:S(2)}) %collective-permute-start.7) | collective-permute-done | bytes 77856 | tf_op jit(solution)/shard_map/ppermute | solution.py:599
  27.5 3.7 %collective-permute-start.12 = (bf16[304,128]{1,0:T(8,128)(2,1)S(1)}, bf16[304,128]{1,0:T(8,128)(2,1)S(1)}, u32[]{:S(2)}, u32[]{:S(2)}) collective-permute-start(bf16[304,128]{1,0:T(8,128)(2,1)S(1)} %add_convert_fusion.1), channel_id=1, source_target_pairs={{0,24},{1,7},{2,26},{3,5},{4,28},{5,3},{6,30},{7,1},{8,16},{9,15},... | collective-permute-start | bytes 233480 | tf_op jit(solution)/shard_map/ppermute | solution.py:599
  31.2 0.0 collective-permute-start.11
  31.2 0.8 %collective-permute-start.10 = (bf16[304,128]{1,0:T(8,128)(2,1)S(1)}, bf16[304,128]{1,0:T(8,128)(2,1)S(1)}, u32[]{:S(2)}, u32[]{:S(2)}) collective-permute-start(bf16[304,128]{1,0:T(8,128)(2,1)S(1)} %add_convert_fusion.1), channel_id=1, source_target_pairs={{0,8},{1,3},{2,10},{3,1},{4,12},{5,7},{6,14},{7,5},{8,0},{9,11},{1... | collective-permute-start | bytes 233480 | tf_op jit(solution)/shard_map/ppermute | solution.py:599
  31.9 1.9 %collective-permute-done.12 = bf16[304,128]{1,0:T(8,128)(2,1)S(1)} collective-permute-done((bf16[304,128]{1,0:T(8,128)(2,1)S(1)}, bf16[304,128]{1,0:T(8,128)(2,1)S(1)}, u32[]{:S(2)}, u32[]{:S(2)}) %collective-permute-start.12) | collective-permute-done | bytes 77856 | tf_op jit(solution)/shard_map/ppermute | solution.py:599
  33.8 2.7 %collective-permute-done.11 = bf16[304,128]{1,0:T(8,128)(2,1)S(1)} collective-permute-done((bf16[304,128]{1,0:T(8,128)(2,1)S(1)}, bf16[304,128]{1,0:T(8,128)(2,1)S(1)}, u32[]{:S(2)}, u32[]{:S(2)}) %collective-permute-start.11) | collective-permute-done | bytes 77856 | tf_op jit(solution)/shard_map/ppermute | solution.py:599
  36.5 0.0 collective-permute-done.10
  36.5 0.1 collective-permute-start.13
  36.6 1.7 %shard_map.199 = bf16[2304,256]{1,0:T(8,128)(2,1)} custom-call(f32[2304,256]{1,0:T(8,128)S(1)} %get-tuple-element.60.pre3, f32[8,256]{1,0:T(8,128)S(1)} %get-tuple-element.61.own3, f32[8,256]{1,0:T(8,128)S(1)} %collective-permute-done.2.rec3, f32[8,256]{1,0:T(8,128)S(1)} %get-tuple-element.54.prm, f32[2304,256]{1,0:T(8,128)S(1)} %get-tuple-element.65.im_half), custom_call_target="tpu_custom_call" | custom-call | flops 5898240 | bytes 7102464 | tf_op jit(solution)/shard_map/pallas_call | solution.py:561
  38.3 1.5 %shard_map.207 = bf16[2304,256]{1,0:T(8,128)(2,1)} custom-call(bf16[1152,128]{1,0:T(8,128)(2,1)S(1)} %get-tuple-element.80.dh1, bf16[64,256]{1,0:T(8,128)(2,1)S(1)} %get-tuple-element.81.w, f32[2304,256]{1,0:T(8,128)S(1)} %get-tuple-element.67.e3), custom_call_target="tpu_custom_call" | custom-call | flops 150994944 | bytes 5046272 | tf_op jit(solution)/shard_map/pallas_call | solution.py:561
  39.8 0.0 collective-permute-done.13.refs_1_
  39.8 0.9 %shard_map.208 = (f32[64,256]{1,0:T(8,128)}, f32[9,64,64]{2,1,0:T(8,128)}, f32[64,256]{1,0:T(8,128)}, f32[1,64]{1,0:T(1,128)}, f32[1,64]{1,0:T(1,128)}, /*index=...) custom-call(bf16[304,128]{1,0:T(8,128)(2,1)S(1)} %add_convert_fusion.refs_0_, ...), custom_call_target="tpu_custom_call" | custom-call | bytes 437248 | tf_op jit(solution)/shard_map/pallas_call | solution.py:561
  (3 shorter events, 0.1 us)
Async XLA Ops:
  3.4 1.6 %collective-permute-start = (bf16[592,128]{1,0:T(8,128)(2,1)S(1)}, bf16[592,128]{1,0:T(8,128)(2,1)S(1)}, u32[]{:S(2)}, u32[]{:S(2)}) collective-permute-start(bf16[592,128]{1,0:T(8,128)(2,1)S(1)} %get-tuple-element.53.own1), channel_id=1, source_target_pairs={{0,1},{1,0},{2,3},{3,2},{4,5},{5,4},{6,7},{7,6},{8,9},{9,8},{10,11... | collective-permute-start | bytes 454664 | tf_op jit(solution)/shard_map/ppermute | solution.py:575
  6.6 1.3 %collective-permute-start.1 = (f32[8,128]{1,0:T(8,128)S(1)}, f32[8,128]{1,0:T(8,128)S(1)}, u32[]{:S(2)}, u32[]{:S(2)}) collective-permute-start(f32[8,128]{1,0:T(8,128)S(1)} %get-tuple-element.58.own2), channel_id=1, source_target_pairs={{0,1},{1,0},{2,3},{3,2},{4,5},{5,4},{6,7},{7,6},{8,9},{9,8},{10,11... | collective-permute-start | bytes 12296 | tf_op jit(solution)/shard_map/ppermute | solution.py:575
  8.6 1.2 %collective-permute-start.2 = (f32[8,256]{1,0:T(8,128)S(1)}, f32[8,256]{1,0:T(8,128)S(1)}, u32[]{:S(2)}, u32[]{:S(2)}) collective-permute-start(f32[8,256]{1,0:T(8,128)S(1)} %get-tuple-element.61.own3), channel_id=1, source_target_pairs={{0,1},{1,0},{2,3},{3,2},{4,5},{5,4},{6,7},{7,6},{8,9},{9,8},{10,11... | collective-permute-start | bytes 24584 | tf_op jit(solution)/shard_map/ppermute | solution.py:575
  11.1 1.2 %collective-permute-start.3 = (f32[8,256]{1,0:T(8,128)S(1)}, f32[8,256]{1,0:T(8,128)S(1)}, u32[]{:S(2)}, u32[]{:S(2)}) collective-permute-start(f32[8,256]{1,0:T(8,128)S(1)} %get-tuple-element.68.own4), channel_id=1, source_target_pairs={{0,1},{1,0},{2,3},{3,2},{4,5},{5,4},{6,7},{7,6},{8,9},{9,8},{10,11... | collective-permute-start | bytes 24584 | tf_op jit(solution)/shard_map/ppermute | solution.py:575
  13.0 1.7 %collective-permute-start.4 = (bf16[1168,128]{1,0:T(8,128)(2,1)S(1)}, bf16[1168,128]{1,0:T(8,128)(2,1)S(1)}, u32[]{:S(2)}, u32[]{:S(2)}) collective-permute-start(bf16[1168,128]{1,0:T(8,128)(2,1)S(1)} %get-tuple-element.71.own5), channel_id=1, source_target_pairs={{0,1},{1,0},{2,3},{3,2},{4,5},{5,4},{6,7},{7,6},{8,9},{9,8},{10,11... | collective-permute-start | bytes 897032 | tf_op jit(solution)/shard_map/ppermute | solution.py:575
  15.8 1.2 %collective-permute-start.5 = (f32[8,128]{1,0:T(8,128)S(1)}, f32[8,128]{1,0:T(8,128)S(1)}, u32[]{:S(2)}, u32[]{:S(2)}) collective-permute-start(f32[8,128]{1,0:T(8,128)S(1)} %get-tuple-element.75.own6), channel_id=1, source_target_pairs={{0,1},{1,0},{2,3},{3,2},{4,5},{5,4},{6,7},{7,6},{8,9},{9,8},{10,11... | collective-permute-start | bytes 12296 | tf_op jit(solution)/shard_map/ppermute | solution.py:575
  17.4 1.3 %collective-permute-start.6 = (bf16[304,128]{1,0:T(8,128)(2,1)S(1)}, bf16[304,128]{1,0:T(8,128)(2,1)S(1)}, u32[]{:S(2)}, u32[]{:S(2)}) collective-permute-start(bf16[304,128]{1,0:T(8,128)(2,1)S(1)} %get-tuple-element.83), channel_id=1, source_target_pairs={{0,1},{1,0},{2,3},{3,2},{4,5},{5,4},{6,7},{7,6},{8,9},{9,8},{10,11... | collective-permute-start | bytes 233480 | tf_op jit(solution)/shard_map/ppermute | solution.py:575
  18.8 6.1 %collective-permute-start.9 = (bf16[304,128]{1,0:T(8,128)(2,1)S(1)}, bf16[304,128]{1,0:T(8,128)(2,1)S(1)}, u32[]{:S(2)}, u32[]{:S(2)}) collective-permute-start(bf16[304,128]{1,0:T(8,128)(2,1)S(1)} %add_convert_fusion.2), channel_id=1, source_target_pairs={{0,6},{1,25},{2,4},{3,27},{4,2},{5,29},{6,0},{7,31},{8,14},{9,17},... | collective-permute-start | bytes 233480 | tf_op jit(solution)/shard_map/ppermute | solution.py:599
  22.5 4.4 %collective-permute-start.8 = (bf16[304,128]{1,0:T(8,128)(2,1)S(1)}, bf16[304,128]{1,0:T(8,128)(2,1)S(1)}, u32[]{:S(2)}, u32[]{:S(2)}) collective-permute-start(bf16[304,128]{1,0:T(8,128)(2,1)S(1)} %add_convert_fusion.2), channel_id=1, source_target_pairs={{0,4},{1,17},{2,6},{3,19},{4,0},{5,21},{6,2},{7,23},{8,12},{9,25},... | collective-permute-start | bytes 233480 | tf_op jit(solution)/shard_map/ppermute | solution.py:599
  23.0 4.4 %collective-permute-start.7 = (bf16[304,128]{1,0:T(8,128)(2,1)S(1)}, bf16[304,128]{1,0:T(8,128)(2,1)S(1)}, u32[]{:S(2)}, u32[]{:S(2)}) collective-permute-start(bf16[304,128]{1,0:T(8,128)(2,1)S(1)} %add_convert_fusion.2), channel_id=1, source_target_pairs={{0,2},{1,9},{2,0},{3,11},{4,6},{5,13},{6,4},{7,15},{8,10},{9,1},{1... | collective-permute-start | bytes 233480 | tf_op jit(solution)/shard_map/ppermute | solution.py:599
  27.5 6.3 %collective-permute-start.12 = (bf16[304,128]{1,0:T(8,128)(2,1)S(1)}, bf16[304,128]{1,0:T(8,128)(2,1)S(1)}, u32[]{:S(2)}, u32[]{:S(2)}) collective-permute-start(bf16[304,128]{1,0:T(8,128)(2,1)S(1)} %add_convert_fusion.1), channel_id=1, source_target_pairs={{0,24},{1,7},{2,26},{3,5},{4,28},{5,3},{6,30},{7,1},{8,16},{9,15},... | collective-permute-start | bytes 233480 | tf_op jit(solution)/shard_map/ppermute | solution.py:599
  31.2 5.3 %collective-permute-start.11 = (bf16[304,128]{1,0:T(8,128)(2,1)S(1)}, bf16[304,128]{1,0:T(8,128)(2,1)S(1)}, u32[]{:S(2)}, u32[]{:S(2)}) collective-permute-start(bf16[304,128]{1,0:T(8,128)(2,1)S(1)} %add_convert_fusion.1), channel_id=1, source_target_pairs={{0,16},{1,5},{2,18},{3,7},{4,20},{5,1},{6,22},{7,3},{8,24},{9,13},... | collective-permute-start | bytes 233480 | tf_op jit(solution)/shard_map/ppermute | solution.py:599
  31.2 5.3 %collective-permute-start.10 = (bf16[304,128]{1,0:T(8,128)(2,1)S(1)}, bf16[304,128]{1,0:T(8,128)(2,1)S(1)}, u32[]{:S(2)}, u32[]{:S(2)}) collective-permute-start(bf16[304,128]{1,0:T(8,128)(2,1)S(1)} %add_convert_fusion.1), channel_id=1, source_target_pairs={{0,8},{1,3},{2,10},{3,1},{4,12},{5,7},{6,14},{7,5},{8,0},{9,11},{1... | collective-permute-start | bytes 233480 | tf_op jit(solution)/shard_map/ppermute | solution.py:599
  36.5 3.3 %collective-permute-start.13 = (bf16[304,128]{1,0:T(8,128)(2,1)S(1)}, bf16[304,128]{1,0:T(8,128)(2,1)S(1)}, u32[]{:S(2)}, u32[]{:S(2)}) collective-permute-start(bf16[304,128]{1,0:T(8,128)(2,1)S(1)} %add_convert_fusion.refs_0_), channel_id=1, source_target_pairs={{0,1},{1,0},{2,3},{3,2},{4,5},{5,4},{6,7},{7,6},{8,9},{9,8},{10,11... | collective-permute-start | bytes 233480 | tf_op jit(solution)/shard_map/ppermute | solution.py:575

commit v3 on v1

--- a/solution.py
+++ b/solution.py
@@ -131,29 +131,30 @@
 
 
 def first_kernel(edge, im, w, pre, msg, im_held, w_held, im_near, w_near, sems):
-    half, cols = pre.shape[0], edge // 2
-    fetch_w = pltpu.make_async_copy(w, w_near, sems.at[0])
-    fetch_w.start()
+    half, cols, wide = pre.shape[0], edge // 2, pre.shape[1]
+    fetch = pltpu.make_async_copy(w, w_near, sems.at[0])
+    fetch.start()
+    cut = half // cols // 2 * cols
     copies = []
-    for at in range(0, half, cols):
-        for base in (at, half + at):
-            rows = pl.ds(base, cols)
-            sem = sems.at[1 + len(copies)]
-            copies.append(pltpu.make_async_copy(im.at[rows, :], im_near.at[rows, :], sem))
-            copies[-1].start()
-    fetch_w.wait()
+    for k, (base, size) in enumerate(((0, cut), (cut, half - cut))):
+        rows = pl.ds(base, size)
+        copies.append(
+            pltpu.make_async_copy(im.at[:, rows, :], im_near.at[:, rows, :], sems.at[k + 1])
+        )
+        copies[-1].start()
+    fetch.wait()
     weight = w_near[...]
     w_held[...] = weight
     zero = jnp.zeros_like(weight)
-    upper = jnp.concatenate([weight, zero], 0)
-    lower = jnp.concatenate([zero, weight], 0)
-    acc = jnp.zeros((8, pre.shape[1]), F32)
-    for k, at in enumerate(range(0, half, cols)):
+    sides = (jnp.concatenate([weight, zero], 0), jnp.concatenate([zero, weight], 0))
+    acc = jnp.zeros((8, wide), F32)
+    for at in range(0, half, cols):
+        if at in (0, cut):
+            copies[min(at, 1)].wait()
         part = None
-        for copy, base, side in ((2 * k, at, upper), (2 * k + 1, half + at, lower)):
-            copies[copy].wait()
-            block = im_near[base : base + cols, :]
-            im_held[base : base + cols, :] = block
+        for k, side in enumerate(sides):
+            block = im_near[k, at : at + cols, :]
+            im_held[k * half + at : k * half + at + cols, :] = block
             prod = nt(block, side)
             part = prod if part is None else part + prod
         pre[at : at + cols, :] = part
@@ -174,24 +175,21 @@
             )
 
 
-def weights_kernel(*refs):
-    far, (we_held, fwd, bwd, prm), near, sems = refs[:8], refs[8:12], refs[12:-1], refs[-1]
-    copies = [pltpu.make_async_copy(a, b, sems.at[k]) for k, (a, b) in enumerate(zip(far, near))]
-    for item in copies:
-        item.start()
-    for item in copies:
-        item.wait()
-    wide = 2 * near[0].shape[-1]
-    for a, b, both in tap_blocks(near[0]):
+def weights_kernel(wd, we, g1, s1, g2, s2, g3, s3, fwd, bwd, we_held, prm, wd_near, sem):
+    fetch = pltpu.make_async_copy(wd, wd_near, sem)
+    fetch.start()
+    wide = 2 * wd.shape[-1]
+    we_held[...] = we[...]
+    prm[...] = jnp.zeros(prm.shape, F32)
+    for k, ref in enumerate((g1, s1, g2, s2)):
+        prm[k : k + 1, 0:wide] = jnp.concatenate([ref[...], ref[...]], 1)
+    prm[4:5, :] = g3[...]
+    prm[5:6, :] = s3[...]
+    fetch.wait()
+    for a, b, both in tap_blocks(wd_near):
         k = 2 - a
         fwd[a * wide : (a + 1) * wide, b * wide : (b + 1) * wide] = both
         bwd[b * wide : (b + 1) * wide, k * wide : (k + 1) * wide] = both
-    prm[...] = jnp.zeros(prm.shape, F32)
-    we_held[...] = near[7][...]
-    for k, ref in enumerate(near[1:5]):
-        prm[k : k + 1, 0:wide] = jnp.concatenate([ref[...], ref[...]], 1)
-    prm[4:5, :] = near[5][...]
-    prm[5:6, :] = near[6][...]
 
 
 def gain_shift(prm, norm, wide):
@@ -572,19 +570,29 @@
     return jnp.concatenate(heads, 0)
 
 
+def flipped_dp(part, masks):
+    count, sides = lax.axis_size("dp"), lax.axis_size("space")
+    pairs = []
+    for i in range(count * sides):
+        dp, side = divmod(i, sides)
+        pairs.append((i, (dp ^ masks[side % len(masks)]) * sides + side))
+    return lax.ppermute(part, ("dp", "space"), pairs).astype(F32)
+
+
 def summed_over_dp(part):
-    count, sides = lax.axis_size("dp"), lax.axis_size("space")
+    count = lax.axis_size("dp")
     if count & (count - 1):
         return lax.psum(part.astype(F32), "dp").astype(BF16)
     bits = [1 << k for k in range(count.bit_length() - 1)]
-    for k in range(len(bits)):
-        pairs = []
-        for i in range(count * sides):
-            dp, side = divmod(i, sides)
-            bit = bits[(k + side * (len(bits) // 2)) % len(bits)]
-            pairs.append((i, (dp ^ bit) * sides + side))
-        got = lax.ppermute(part, ("dp", "space"), pairs)
-        part = (part.astype(F32) + got.astype(F32)).astype(BF16)
+    twos = [bits[k : k + 2] for k in range(0, len(bits) - 1, 2)]
+    for k in range(len(twos)):
+        turn = [twos[(k + side * (len(twos) // 2)) % len(twos)] for side in range(2)]
+        low = flipped_dp(part, [pair[0] for pair in turn])
+        high = flipped_dp(part, [pair[1] for pair in turn])
+        both = flipped_dp(part, [pair[0] + pair[1] for pair in turn])
+        part = ((part.astype(F32) + low) + (high + both)).astype(BF16)
+    if len(bits) % 2:
+        part = (part.astype(F32) + flipped_dp(part, bits[-1:])).astype(BF16)
     return part
 
 
@@ -613,20 +621,17 @@
         part(first_kernel, edge),
         [((half, wide), F32), ((WIDE_HEAD + edge, wide), BF16), ((pixels, chans), BF16)]
         + [(w_rows.shape, BF16)],
-        im, w_rows, flops=gates, far=(0, 1),
-        scratch=[pltpu.VMEM((pixels, chans), BF16), pltpu.VMEM(w_rows.shape, BF16)]
-        + [pltpu.SemaphoreType.DMA((2 * chunks + 1,))],
-    )
-    own1, cot = lax.optimization_barrier((own1, cot))
+        im.reshape(2, half, chans), w_rows, flops=gates, far=(0, 1),
+        scratch=[pltpu.VMEM((2, half, chans), BF16), pltpu.VMEM(w_rows.shape, BF16)]
+        + [pltpu.SemaphoreType.DMA((3,))],
+    )
     rec1 = exchanged(own1, peers)
-    we, fwd, bwd, prm = call(
+    fwd, bwd, we, prm = call(
         weights_kernel,
-        [(w_expand.shape, BF16)] + [((3 * wide, 3 * wide), BF16)] * 2 + [((8, chans), F32)],
-        w_dilated, row(gain_one), row(shift_one), row(gain_two), row(shift_two),
-        row(gain_three), row(shift_three), w_expand, flops=10**6, far=tuple(range(8)),
-        scratch=[pltpu.VMEM(w_dilated.shape, BF16)] + [pltpu.VMEM((1, mids), F32)] * 4
-        + [pltpu.VMEM((1, chans), F32)] * 2 + [pltpu.VMEM(w_expand.shape, BF16)]
-        + [pltpu.SemaphoreType.DMA((8,))],
+        [((3 * wide, 3 * wide), BF16)] * 2 + [(w_expand.shape, BF16), ((8, chans), F32)],
+        w_dilated, w_expand, row(gain_one), row(shift_one), row(gain_two), row(shift_two),
+        row(gain_three), row(shift_three), flops=10**10, far=(0,),
+        scratch=[pltpu.VMEM(w_dilated.shape, BF16), pltpu.SemaphoreType.DMA],
     )
     ext, pre2, own2 = call(
         part(second_kernel, peers, edge),

time: 42.4 us -> 39.7 us (0.936)
  starting transfers between devices: 12.6 us -> 11.4 us
  waiting for transfers between devices: 13.3 us -> 12.5 us
  Pallas kernels: 15.3 us -> 14.7 us
    ppermute x4 -> x6, starting transfers between devices: 10.1 us -> 8.86 us  [flipped_dp(): return lax.ppermute(part, ('dp', 'space'), pairs).astype(F32)]
    ppermute x4 -> x6, waiting for transfers between devices: 9.51 us -> 8.76 us  [flipped_dp(): return lax.ppermute(part, ('dp', 'space'), pairs).astype(F32)]
    pallas_call x15, Pallas kernels: 15.3 us -> 14.7 us  [call(): pl.pallas_call(kernel, out_shape=[kind_of(shape, kind) for shape, kind in...]
  transfers between devices with their start and end apart: 12 -> 14, of which waited for: 9 -> 10; matrix products, arithmetic and copies ran while one was open for 0% -> 0% of each run, Pallas kernels for 15% -> 16%
where the time goes in v3:
time: 39.7 us; the launch traced here: 39.5 us
  Pallas kernels  14.7 us (37%)
  waiting for transfers between devices  12.5 us (31%)
  starting transfers between devices  11.4 us (29%)
  between operations  0.85 us (2%)
    pallas_call x15, Pallas kernels, call(): pl.pallas_call(kernel, out_shape=[kind_of(shape, kind) for shape, kind in...  14.7 us
    ppermute x6, starting transfers between devices, flipped_dp(): return lax.ppermute(part, ('dp', 'space'), pairs).astype(F32)  8.86 us
    ppermute x6, waiting for transfers between devices, flipped_dp(): return lax.ppermute(part, ('dp', 'space'), pairs).astype(F32)  8.76 us
    ppermute x8, waiting for transfers between devices, swapped(): lax.ppermute(value, axis, [(i, (i + step) % count) for i in range(count)])  3.71 us
    ppermute x8, starting transfers between devices, swapped(): lax.ppermute(value, axis, [(i, (i + step) % count) for i in range(count)])  2.53 us
  transfers between devices with their start and end apart: 14, of which 10 were waited for; matrix products, arithmetic and copies ran while one was open for 0% of the time, Pallas kernels for 16%

profile of v3, /device:TPU:0, one launch (start us, length us, event | category | flops | bytes accessed | tf_op | source)
XLA Modules:
  0.0 39.5 jit_solution(7821989045022436144)
XLA Ops:
  0.7 2.0 %shard_map.194 = (f32[1152,128]{1,0:T(8,128)S(1)}, bf16[592,128]{1,0:T(8,128)(2,1)S(1)}, bf16[2304,256]{1,0:T(8,128)(2,1)S(1)}, bf16[64,256]{1,0:T(8,128)(2,1)S(1)}) custom-call(bf16[2,1152,256]{2,1,0:T(8,128)(2,1)} %bitcast.26, bf16[64,256]{1,0:T(8,128)(2,1)} %bitcast.29), custom_call_target="tpu_custom_call" | custom-call | flops 150994944 | bytes 4530176 | tf_op jit(solution)/shard_map/pallas_call | solution.py:541
  2.8 0.6 %collective-permute-start = (bf16[592,128]{1,0:T(8,128)(2,1)S(1)}, bf16[592,128]{1,0:T(8,128)(2,1)S(1)}, u32[]{:S(2)}, u32[]{:S(2)}) collective-permute-start(bf16[592,128]{1,0:T(8,128)(2,1)S(1)} %get-tuple-element.50.own1), channel_id=1, source_target_pairs={{0,1},{1,0},{2,3},{3,2},{4,5},{5,4},{6,7},{7,6},{8,9},{9,8},{10,11... | collective-permute-start | bytes 454664 | tf_op jit(solution)/shard_map/ppermute | solution.py:555
  3.3 0.0 copy-done.3
  3.3 0.0 copy-done.5
  3.3 0.0 copy-done.4
  3.3 0.0 copy-done.1
  3.4 1.0 %shard_map.195 = (bf16[384,384]{1,0:T(8,128)(2,1)S(1)}, bf16[384,384]{1,0:T(8,128)(2,1)S(1)}, bf16[64,256]{1,0:T(8,128)(2,1)S(1)}, f32[8,256]{1,0:T(8,128)S(1)}) custom-call(bf16[3,3,64,64]{3,2,1,0:T(8,128)(2,1)} %wd.1, bf16[64,256]{1,0:T(8,128)(2,1)S(1)} %copy-done.1, f32[1,64]{1,0:T(1,128)S(1)} %bitcast.22, f32[1,64]{1,0:T(1,128)S(1)} %bitcast.23, ...), custom_call_target="tpu_custom_call" | custom-call | flops 10000000000 | bytes 1362944 | tf_op jit(solution)/shard_map/pallas_call | solution.py:541
  4.4 0.0 copy-start
  4.4 0.0 collective-permute-done.rec1
  4.4 1.1 %shard_map.196 = (bf16[2304,128]{1,0:T(8,128)(2,1)S(1)}, f32[1152,128]{1,0:T(8,128)S(1)}, f32[8,128]{1,0:T(8,128)S(1)}) custom-call(f32[1152,128]{1,0:T(8,128)S(1)} %get-tuple-element.49.pre1, bf16[592,128]{1,0:T(8,128)(2,1)S(1)} %get-tuple-element.50.own1, bf16[592,128]{1,0:T(8,128)(2,1)S(1)} %collective-permute-done.rec1, ...), custom_call_target="tpu_custom_call" | custom-call | flops 339738624 | bytes 2969600 | tf_op jit(solution)/shard_map/pallas_call | solution.py:541
  5.6 0.3 collective-permute-start.1
  5.8 0.9 %collective-permute-done.1.rec2 = f32[8,128]{1,0:T(8,128)S(1)} collective-permute-done((f32[8,128]{1,0:T(8,128)S(1)}, f32[8,128]{1,0:T(8,128)S(1)}, u32[]{:S(2)}, u32[]{:S(2)}) %collective-permute-start.1) | collective-permute-done | bytes 4128 | tf_op jit(solution)/shard_map/ppermute | solution.py:555
  6.7 0.8 %shard_map.197 = (bf16[1152,128]{1,0:T(8,128)(2,1)S(1)}, f32[2304,256]{1,0:T(8,128)S(1)}, f32[8,256]{1,0:T(8,128)S(1)}) custom-call(f32[1152,128]{1,0:T(8,128)S(1)} %get-tuple-element.53.pre2, f32[8,128]{1,0:T(8,128)S(1)} %get-tuple-element.54.own2, f32[8,128]{1,0:T(8,128)S(1)} %collective-permute-done.1.rec2, f32[8,256]{1,0:T(8,128)S(1)} %get-tuple-element.51.prm, ...), custom_call_target="tpu_custom_call" | custom-call | flops 150994944 | bytes 3596288 | tf_op jit(solution)/shard_map/pallas_call | solution.py:541
  7.5 0.3 collective-permute-start.2
  7.9 0.5 %shard_map.198 = (f32[2304,256]{1,0:T(8,128)S(1)}, f32[2304,256]{1,0:T(8,128)S(1)}) custom-call(bf16[2304,256]{1,0:T(8,128)(2,1)S(1)} %get-tuple-element.58.im, bf16[2304,256]{1,0:T(8,128)(2,1)S(1)} %bitcast.19), custom_call_target="tpu_custom_call" | custom-call | flops 2359296 | bytes 7077888 | tf_op jit(solution)/shard_map/pallas_call | solution.py:541
  8.4 0.4 collective-permute-done.2.rec3
  8.8 1.2 %shard_map.200 = (f32[2304,256]{1,0:T(8,128)S(1)}, f32[8,256]{1,0:T(8,128)S(1)}) custom-call(f32[2304,256]{1,0:T(8,128)S(1)} %get-tuple-element.56.pre3, f32[8,256]{1,0:T(8,128)S(1)} %get-tuple-element.57.own3, f32[8,256]{1,0:T(8,128)S(1)} %collective-permute-done.2.rec3, f32[8,256]{1,0:T(8,128)S(1)} %get-tuple-element.51.prm, ...), custom_call_target="tpu_custom_call" | custom-call | flops 17694720 | bytes 9469952 | tf_op jit(solution)/shard_map/pallas_call | solution.py:541
  10.0 0.3 collective-permute-start.3
  10.3 0.4 %shard_map.201 = (f32[1152,128]{1,0:T(8,128)S(1)}, f32[1152,128]{1,0:T(8,128)S(1)}) custom-call(f32[1152,128]{1,0:T(8,128)S(1)} %get-tuple-element.49.pre1, bf16[592,128]{1,0:T(8,128)(2,1)S(1)} %get-tuple-element.50.own1, bf16[592,128]{1,0:T(8,128)(2,1)S(1)} %collective-permute-done.rec1, f32[1152,128]{1,0:T(8,128)S(1)} %get-tuple-element.53.pre2, ...), custom_call_target="tpu_custom_call" | custom-call | flops 4423680 | bytes 2678784 | tf_op jit(solution)/shard_map/pallas_call | solution.py:541
  10.8 0.5 %collective-permute-done.3.rec4 = f32[8,256]{1,0:T(8,128)S(1)} collective-permute-done((f32[8,256]{1,0:T(8,128)S(1)}, f32[8,256]{1,0:T(8,128)S(1)}, u32[]{:S(2)}, u32[]{:S(2)}) %collective-permute-start.3) | collective-permute-done | bytes 8224 | tf_op jit(solution)/shard_map/ppermute | solution.py:555
  11.2 0.7 %shard_map.202 = (bf16[2304,256]{1,0:T(8,128)(2,1)S(1)}, f32[1152,128]{1,0:T(8,128)S(1)}, bf16[1168,128]{1,0:T(8,128)(2,1)S(1)}) custom-call(f32[2304,256]{1,0:T(8,128)S(1)} %get-tuple-element.56.pre3, f32[2304,256]{1,0:T(8,128)S(1)} %get-tuple-element.61.e3, f32[8,256]{1,0:T(8,128)S(1)} %get-tuple-element.57.own3, ...), custom_call_target="tpu_custom_call" | custom-call | flops 150994944 | bytes 9527296 | tf_op jit(solution)/shard_map/pallas_call | solution.py:541
  12.0 0.3 collective-permute-start.4
  12.3 0.4 shard_map.205.gwe
  12.7 0.9 %collective-permute-done.4.rec5 = bf16[1168,128]{1,0:T(8,128)(2,1)S(1)} collective-permute-done((bf16[1168,128]{1,0:T(8,128)(2,1)S(1)}, bf16[1168,128]{1,0:T(8,128)(2,1)S(1)}, u32[]{:S(2)}, u32[]{:S(2)}) %collective-permute-start.4) | collective-permute-done | bytes 299040 | tf_op jit(solution)/shard_map/ppermute | solution.py:555
  13.6 1.0 %shard_map.203 = (bf16[2304,128]{1,0:T(8,128)(2,1)S(1)}, f32[1152,128]{1,0:T(8,128)S(1)}, f32[8,128]{1,0:T(8,128)S(1)}) custom-call(f32[1152,128]{1,0:T(8,128)S(1)} %get-tuple-element.53.pre2, f32[1152,128]{1,0:T(8,128)S(1)} %get-tuple-element.64.e2, bf16[1168,128]{1,0:T(8,128)(2,1)S(1)} %get-tuple-element.65.own5, ...), custom_call_target="tpu_custom_call" | custom-call | flops 339738624 | bytes 5345280 | tf_op jit(solution)/shard_map/pallas_call | solution.py:541
  14.7 0.3 collective-permute-start.5
  14.9 0.9 %shard_map.204.gwd = bf16[320,128]{1,0:T(8,128)(2,1)S(1)} custom-call(bf16[2304,128]{1,0:T(8,128)(2,1)S(1)} %get-tuple-element.70.ext, bf16[2304,128]{1,0:T(8,128)(2,1)S(1)} %get-tuple-element.71.dext), custom_call_target="tpu_custom_call" | custom-call | flops 339738624 | bytes 1343488 | tf_op jit(solution)/shard_map/pallas_call | solution.py:541
  15.8 0.0 collective-permute-done.5.rec6
  15.8 0.4 %shard_map.206 = (bf16[1152,128]{1,0:T(8,128)(2,1)S(1)}, bf16[304,128]{1,0:T(8,128)(2,1)S(1)}, bf16[304,128]{1,0:T(8,128)(2,1)S(1)}) custom-call(f32[1152,128]{1,0:T(8,128)S(1)} %get-tuple-element.49.pre1, f32[1152,128]{1,0:T(8,128)S(1)} %get-tuple-element.68.e1, f32[8,128]{1,0:T(8,128)S(1)} %get-tuple-element.69.own6, ...), custom_call_target="tpu_custom_call" | custom-call | flops 150994944 | bytes 4034560 | tf_op jit(solution)/shard_map/pallas_call | solution.py:541
  16.3 0.3 collective-permute-start.6
  16.6 1.0 %collective-permute-done.6 = bf16[304,128]{1,0:T(8,128)(2,1)S(1)} collective-permute-done((bf16[304,128]{1,0:T(8,128)(2,1)S(1)}, bf16[304,128]{1,0:T(8,128)(2,1)S(1)}, u32[]{:S(2)}, u32[]{:S(2)}) %collective-permute-start.6) | collective-permute-done | bytes 77856 | tf_op jit(solution)/shard_map/ppermute | solution.py:555
  17.6 3.8 %collective-permute-start.9 = (bf16[304,128]{1,0:T(8,128)(2,1)S(1)}, bf16[304,128]{1,0:T(8,128)(2,1)S(1)}, u32[]{:S(2)}, u32[]{:S(2)}) collective-permute-start(bf16[304,128]{1,0:T(8,128)(2,1)S(1)} %add_convert_fusion.2), channel_id=1, source_target_pairs={{0,6},{1,25},{2,4},{3,27},{4,2},{5,29},{6,0},{7,31},{8,14},{9,17},... | collective-permute-start | bytes 233480 | tf_op jit(solution)/shard_map/ppermute | solution.py:579
  21.4 0.5 %collective-permute-start.8 = (bf16[304,128]{1,0:T(8,128)(2,1)S(1)}, bf16[304,128]{1,0:T(8,128)(2,1)S(1)}, u32[]{:S(2)}, u32[]{:S(2)}) collective-permute-start(bf16[304,128]{1,0:T(8,128)(2,1)S(1)} %add_convert_fusion.2), channel_id=1, source_target_pairs={{0,4},{1,17},{2,6},{3,19},{4,0},{5,21},{6,2},{7,23},{8,12},{9,25},... | collective-permute-start | bytes 233480 | tf_op jit(solution)/shard_map/ppermute | solution.py:579
  21.9 0.1 collective-permute-start.7
  22.0 1.7 %collective-permute-done.9 = bf16[304,128]{1,0:T(8,128)(2,1)S(1)} collective-permute-done((bf16[304,128]{1,0:T(8,128)(2,1)S(1)}, bf16[304,128]{1,0:T(8,128)(2,1)S(1)}, u32[]{:S(2)}, u32[]{:S(2)}) %collective-permute-start.9) | collective-permute-done | bytes 77856 | tf_op jit(solution)/shard_map/ppermute | solution.py:579
  23.8 2.0 %collective-permute-done.8 = bf16[304,128]{1,0:T(8,128)(2,1)S(1)} collective-permute-done((bf16[304,128]{1,0:T(8,128)(2,1)S(1)}, bf16[304,128]{1,0:T(8,128)(2,1)S(1)}, u32[]{:S(2)}, u32[]{:S(2)}) %collective-permute-start.8) | collective-permute-done | bytes 77856 | tf_op jit(solution)/shard_map/ppermute | solution.py:579
  25.8 0.5 %collective-permute-done.7 = bf16[304,128]{1,0:T(8,128)(2,1)S(1)} collective-permute-done((bf16[304,128]{1,0:T(8,128)(2,1)S(1)}, bf16[304,128]{1,0:T(8,128)(2,1)S(1)}, u32[]{:S(2)}, u32[]{:S(2)}) %collective-permute-start.7) | collective-permute-done | bytes 77856 | tf_op jit(solution)/shard_map/ppermute | solution.py:579
  26.4 3.7 %collective-permute-start.12 = (bf16[304,128]{1,0:T(8,128)(2,1)S(1)}, bf16[304,128]{1,0:T(8,128)(2,1)S(1)}, u32[]{:S(2)}, u32[]{:S(2)}) collective-permute-start(bf16[304,128]{1,0:T(8,128)(2,1)S(1)} %add_convert_fusion.1), channel_id=1, source_target_pairs={{0,24},{1,7},{2,26},{3,5},{4,28},{5,3},{6,30},{7,1},{8,16},{9,15},... | collective-permute-start | bytes 233480 | tf_op jit(solution)/shard_map/ppermute | solution.py:579
  30.0 0.0 collective-permute-start.11
  30.0 0.8 %collective-permute-start.10 = (bf16[304,128]{1,0:T(8,128)(2,1)S(1)}, bf16[304,128]{1,0:T(8,128)(2,1)S(1)}, u32[]{:S(2)}, u32[]{:S(2)}) collective-permute-start(bf16[304,128]{1,0:T(8,128)(2,1)S(1)} %add_convert_fusion.1), channel_id=1, source_target_pairs={{0,8},{1,3},{2,10},{3,1},{4,12},{5,7},{6,14},{7,5},{8,0},{9,11},{1... | collective-permute-start | bytes 233480 | tf_op jit(solution)/shard_map/ppermute | solution.py:579
  30.8 1.9 %collective-permute-done.12 = bf16[304,128]{1,0:T(8,128)(2,1)S(1)} collective-permute-done((bf16[304,128]{1,0:T(8,128)(2,1)S(1)}, bf16[304,128]{1,0:T(8,128)(2,1)S(1)}, u32[]{:S(2)}, u32[]{:S(2)}) %collective-permute-start.12) | collective-permute-done | bytes 77856 | tf_op jit(solution)/shard_map/ppermute | solution.py:579
  32.7 2.6 %collective-permute-done.11 = bf16[304,128]{1,0:T(8,128)(2,1)S(1)} collective-permute-done((bf16[304,128]{1,0:T(8,128)(2,1)S(1)}, bf16[304,128]{1,0:T(8,128)(2,1)S(1)}, u32[]{:S(2)}, u32[]{:S(2)}) %collective-permute-start.11) | collective-permute-done | bytes 77856 | tf_op jit(solution)/shard_map/ppermute | solution.py:579
  35.3 0.0 collective-permute-done.10
  35.4 0.1 collective-permute-start.13
  35.4 1.7 %shard_map.199 = bf16[2304,256]{1,0:T(8,128)(2,1)} custom-call(f32[2304,256]{1,0:T(8,128)S(1)} %get-tuple-element.56.pre3, f32[8,256]{1,0:T(8,128)S(1)} %get-tuple-element.57.own3, f32[8,256]{1,0:T(8,128)S(1)} %collective-permute-done.2.rec3, f32[8,256]{1,0:T(8,128)S(1)} %get-tuple-element.51.prm, f32[2304,256]{1,0:T(8,128)S(1)} %get-tuple-element.59.im_half), custom_call_target="tpu_custom_call" | custom-call | flops 5898240 | bytes 7102464 | tf_op jit(solution)/shard_map/pallas_call | solution.py:541
  37.2 1.5 %shard_map.207 = bf16[2304,256]{1,0:T(8,128)(2,1)} custom-call(bf16[1152,128]{1,0:T(8,128)(2,1)S(1)} %get-tuple-element.74.dh1, bf16[64,256]{1,0:T(8,128)(2,1)S(1)} %get-tuple-element.75.w, f32[2304,256]{1,0:T(8,128)S(1)} %get-tuple-element.61.e3), custom_call_target="tpu_custom_call" | custom-call | flops 150994944 | bytes 5046272 | tf_op jit(solution)/shard_map/pallas_call | solution.py:541
  38.6 0.0 collective-permute-done.13.refs_1_
  38.6 0.9 %shard_map.208 = (f32[64,256]{1,0:T(8,128)}, f32[9,64,64]{2,1,0:T(8,128)}, f32[64,256]{1,0:T(8,128)}, f32[1,64]{1,0:T(1,128)}, f32[1,64]{1,0:T(1,128)}, /*index=...) custom-call(bf16[304,128]{1,0:T(8,128)(2,1)S(1)} %add_convert_fusion.refs_0_, ...), custom_call_target="tpu_custom_call" | custom-call | bytes 437248 | tf_op jit(solution)/shard_map/pallas_call | solution.py:541
  (14 shorter events, 0.1 us)
Async XLA Ops:
  0.6 2.7 %copy-start.3 = (f32[256]{0:T(256)S(1)}, f32[256]{0:T(256)}, u32[]{:S(2)}) copy-start(f32[256]{0:T(256)} %param.20) | copy-start | bytes 3076
  0.7 2.7 %copy-start.2 = (f32[256]{0:T(256)S(1)}, f32[256]{0:T(256)}, u32[]{:S(2)}) copy-start(f32[256]{0:T(256)} %param.19) | copy-start | bytes 3076
  0.7 2.7 %copy-start.7 = (f32[64]{0:T(128)S(1)}, f32[64]{0:T(128)}, u32[]{:S(2)}) copy-start(f32[64]{0:T(128)} %param.18) | copy-start | bytes 772
  0.7 2.6 %copy-start.6 = (f32[64]{0:T(128)S(1)}, f32[64]{0:T(128)}, u32[]{:S(2)}) copy-start(f32[64]{0:T(128)} %param.17) | copy-start | bytes 772
  0.7 2.6 %copy-start.5 = (f32[64]{0:T(128)S(1)}, f32[64]{0:T(128)}, u32[]{:S(2)}) copy-start(f32[64]{0:T(128)} %param.16) | copy-start | bytes 772
  0.7 2.6 %copy-start.4 = (f32[64]{0:T(128)S(1)}, f32[64]{0:T(128)}, u32[]{:S(2)}) copy-start(f32[64]{0:T(128)} %param.15) | copy-start | bytes 772
  0.7 2.6 %copy-start.1 = (bf16[64,256]{1,0:T(8,128)(2,1)S(1)}, bf16[64,256]{1,0:T(8,128)(2,1)}, u32[]{:S(2)}) copy-start(bf16[64,256]{1,0:T(8,128)(2,1)} %we.1) | copy-start | bytes 98308
  2.8 1.7 %collective-permute-start = (bf16[592,128]{1,0:T(8,128)(2,1)S(1)}, bf16[592,128]{1,0:T(8,128)(2,1)S(1)}, u32[]{:S(2)}, u32[]{:S(2)}) collective-permute-start(bf16[592,128]{1,0:T(8,128)(2,1)S(1)} %get-tuple-element.50.own1), channel_id=1, source_target_pairs={{0,1},{1,0},{2,3},{3,2},{4,5},{5,4},{6,7},{7,6},{8,9},{9,8},{10,11... | collective-permute-start | bytes 454664 | tf_op jit(solution)/shard_map/ppermute | solution.py:555
  4.4 3.5 %copy-start = (bf16[1,8,288,256]{3,2,1,0:T(8,128)(2,1)S(1)}, bf16[1,8,288,256]{3,2,1,0:T(8,128)(2,1)}, u32[]{:S(2)}) copy-start(bf16[1,8,288,256]{3,2,1,0:T(8,128)(2,1)} %param.21) | copy-start | bytes 3538948
  5.6 1.2 %collective-permute-start.1 = (f32[8,128]{1,0:T(8,128)S(1)}, f32[8,128]{1,0:T(8,128)S(1)}, u32[]{:S(2)}, u32[]{:S(2)}) collective-permute-start(f32[8,128]{1,0:T(8,128)S(1)} %get-tuple-element.54.own2), channel_id=1, source_target_pairs={{0,1},{1,0},{2,3},{3,2},{4,5},{5,4},{6,7},{7,6},{8,9},{9,8},{10,11... | collective-permute-start | bytes 12296 | tf_op jit(solution)/shard_map/ppermute | solution.py:555
  7.5 1.2 %collective-permute-start.2 = (f32[8,256]{1,0:T(8,128)S(1)}, f32[8,256]{1,0:T(8,128)S(1)}, u32[]{:S(2)}, u32[]{:S(2)}) collective-permute-start(f32[8,256]{1,0:T(8,128)S(1)} %get-tuple-element.57.own3), channel_id=1, source_target_pairs={{0,1},{1,0},{2,3},{3,2},{4,5},{5,4},{6,7},{7,6},{8,9},{9,8},{10,11... | collective-permute-start | bytes 24584 | tf_op jit(solution)/shard_map/ppermute | solution.py:555
  10.0 1.2 %collective-permute-start.3 = (f32[8,256]{1,0:T(8,128)S(1)}, f32[8,256]{1,0:T(8,128)S(1)}, u32[]{:S(2)}, u32[]{:S(2)}) collective-permute-start(f32[8,256]{1,0:T(8,128)S(1)} %get-tuple-element.62.own4), channel_id=1, source_target_pairs={{0,1},{1,0},{2,3},{3,2},{4,5},{5,4},{6,7},{7,6},{8,9},{9,8},{10,11... | collective-permute-start | bytes 24584 | tf_op jit(solution)/shard_map/ppermute | solution.py:555
  12.0 1.7 %collective-permute-start.4 = (bf16[1168,128]{1,0:T(8,128)(2,1)S(1)}, bf16[1168,128]{1,0:T(8,128)(2,1)S(1)}, u32[]{:S(2)}, u32[]{:S(2)}) collective-permute-start(bf16[1168,128]{1,0:T(8,128)(2,1)S(1)} %get-tuple-element.65.own5), channel_id=1, source_target_pairs={{0,1},{1,0},{2,3},{3,2},{4,5},{5,4},{6,7},{7,6},{8,9},{9,8},{10,11... | collective-permute-start | bytes 897032 | tf_op jit(solution)/shard_map/ppermute | solution.py:555
  14.7 1.2 %collective-permute-start.5 = (f32[8,128]{1,0:T(8,128)S(1)}, f32[8,128]{1,0:T(8,128)S(1)}, u32[]{:S(2)}, u32[]{:S(2)}) collective-permute-start(f32[8,128]{1,0:T(8,128)S(1)} %get-tuple-element.69.own6), channel_id=1, source_target_pairs={{0,1},{1,0},{2,3},{3,2},{4,5},{5,4},{6,7},{7,6},{8,9},{9,8},{10,11... | collective-permute-start | bytes 12296 | tf_op jit(solution)/shard_map/ppermute | solution.py:555
  16.3 1.3 %collective-permute-start.6 = (bf16[304,128]{1,0:T(8,128)(2,1)S(1)}, bf16[304,128]{1,0:T(8,128)(2,1)S(1)}, u32[]{:S(2)}, u32[]{:S(2)}) collective-permute-start(bf16[304,128]{1,0:T(8,128)(2,1)S(1)} %get-tuple-element.77), channel_id=1, source_target_pairs={{0,1},{1,0},{2,3},{3,2},{4,5},{5,4},{6,7},{7,6},{8,9},{9,8},{10,11... | collective-permute-start | bytes 233480 | tf_op jit(solution)/shard_map/ppermute | solution.py:555
  17.6 6.1 %collective-permute-start.9 = (bf16[304,128]{1,0:T(8,128)(2,1)S(1)}, bf16[304,128]{1,0:T(8,128)(2,1)S(1)}, u32[]{:S(2)}, u32[]{:S(2)}) collective-permute-start(bf16[304,128]{1,0:T(8,128)(2,1)S(1)} %add_convert_fusion.2), channel_id=1, source_target_pairs={{0,6},{1,25},{2,4},{3,27},{4,2},{5,29},{6,0},{7,31},{8,14},{9,17},... | collective-permute-start | bytes 233480 | tf_op jit(solution)/shard_map/ppermute | solution.py:579
  21.4 4.4 %collective-permute-start.8 = (bf16[304,128]{1,0:T(8,128)(2,1)S(1)}, bf16[304,128]{1,0:T(8,128)(2,1)S(1)}, u32[]{:S(2)}, u32[]{:S(2)}) collective-permute-start(bf16[304,128]{1,0:T(8,128)(2,1)S(1)} %add_convert_fusion.2), channel_id=1, source_target_pairs={{0,4},{1,17},{2,6},{3,19},{4,0},{5,21},{6,2},{7,23},{8,12},{9,25},... | collective-permute-start | bytes 233480 | tf_op jit(solution)/shard_map/ppermute | solution.py:579
  21.9 4.4 %collective-permute-start.7 = (bf16[304,128]{1,0:T(8,128)(2,1)S(1)}, bf16[304,128]{1,0:T(8,128)(2,1)S(1)}, u32[]{:S(2)}, u32[]{:S(2)}) collective-permute-start(bf16[304,128]{1,0:T(8,128)(2,1)S(1)} %add_convert_fusion.2), channel_id=1, source_target_pairs={{0,2},{1,9},{2,0},{3,11},{4,6},{5,13},{6,4},{7,15},{8,10},{9,1},{1... | collective-permute-start | bytes 233480 | tf_op jit(solution)/shard_map/ppermute | solution.py:579
  26.4 6.3 %collective-permute-start.12 = (bf16[304,128]{1,0:T(8,128)(2,1)S(1)}, bf16[304,128]{1,0:T(8,128)(2,1)S(1)}, u32[]{:S(2)}, u32[]{:S(2)}) collective-permute-start(bf16[304,128]{1,0:T(8,128)(2,1)S(1)} %add_convert_fusion.1), channel_id=1, source_target_pairs={{0,24},{1,7},{2,26},{3,5},{4,28},{5,3},{6,30},{7,1},{8,16},{9,15},... | collective-permute-start | bytes 233480 | tf_op jit(solution)/shard_map/ppermute | solution.py:579
  30.0 5.3 %collective-permute-start.11 = (bf16[304,128]{1,0:T(8,128)(2,1)S(1)}, bf16[304,128]{1,0:T(8,128)(2,1)S(1)}, u32[]{:S(2)}, u32[]{:S(2)}) collective-permute-start(bf16[304,128]{1,0:T(8,128)(2,1)S(1)} %add_convert_fusion.1), channel_id=1, source_target_pairs={{0,16},{1,5},{2,18},{3,7},{4,20},{5,1},{6,22},{7,3},{8,24},{9,13},... | collective-permute-start | bytes 233480 | tf_op jit(solution)/shard_map/ppermute | solution.py:579
  30.0 5.3 %collective-permute-start.10 = (bf16[304,128]{1,0:T(8,128)(2,1)S(1)}, bf16[304,128]{1,0:T(8,128)(2,1)S(1)}, u32[]{:S(2)}, u32[]{:S(2)}) collective-permute-start(bf16[304,128]{1,0:T(8,128)(2,1)S(1)} %add_convert_fusion.1), channel_id=1, source_target_pairs={{0,8},{1,3},{2,10},{3,1},{4,12},{5,7},{6,14},{7,5},{8,0},{9,11},{1... | collective-permute-start | bytes 233480 | tf_op jit(solution)/shard_map/ppermute | solution.py:579
  35.4 3.3 %collective-permute-start.13 = (bf16[304,128]{1,0:T(8,128)(2,1)S(1)}, bf16[304,128]{1,0:T(8,128)(2,1)S(1)}, u32[]{:S(2)}, u32[]{:S(2)}) collective-permute-start(bf16[304,128]{1,0:T(8,128)(2,1)S(1)} %add_convert_fusion.refs_0_), channel_id=1, source_target_pairs={{0,1},{1,0},{2,3},{3,2},{4,5},{5,4},{6,7},{7,6},{8,9},{9,8},{10,11... | collective-permute-start | bytes 233480 | tf_op jit(solution)/shard_map/ppermute | solution.py:555

commit v4 on v3

--- a/solution.py
+++ b/solution.py
@@ -130,7 +130,9 @@
     return rowsum(acc)
 
 
-def first_kernel(edge, im, w, pre, msg, im_held, w_held, im_near, w_near, sems):
+def first_kernel(
+    edge, im, w, wd, pre, msg, im_held, w_held, wd_held, im_near, w_near, wd_near, sems
+):
     half, cols, wide = pre.shape[0], edge // 2, pre.shape[1]
     fetch = pltpu.make_async_copy(w, w_near, sems.at[0])
     fetch.start()
@@ -142,6 +144,8 @@
             pltpu.make_async_copy(im.at[:, rows, :], im_near.at[:, rows, :], sems.at[k + 1])
         )
         copies[-1].start()
+    fetch_wd = pltpu.make_async_copy(wd, wd_near, sems.at[3])
+    fetch_wd.start()
     fetch.wait()
     weight = w_near[...]
     w_held[...] = weight
@@ -162,6 +166,8 @@
     mean = both_halves(rowsum(acc)) / (2 * half)
     msg[0:WIDE_HEAD, :] = wide_head_rows(mean, both_halves(centred_squares(pre, mean, cols)))
     msg[WIDE_HEAD:, :] = edges(pre, edge, mean).astype(BF16)
+    fetch_wd.wait()
+    wd_held[...] = wd_near[...]
 
 
 def tap_blocks(w):
@@ -175,9 +181,7 @@
             )
 
 
-def weights_kernel(wd, we, g1, s1, g2, s2, g3, s3, fwd, bwd, we_held, prm, wd_near, sem):
-    fetch = pltpu.make_async_copy(wd, wd_near, sem)
-    fetch.start()
+def weights_kernel(wd, we, g1, s1, g2, s2, g3, s3, fwd, bwd, we_held, prm):
     wide = 2 * wd.shape[-1]
     we_held[...] = we[...]
     prm[...] = jnp.zeros(prm.shape, F32)
@@ -185,8 +189,7 @@
         prm[k : k + 1, 0:wide] = jnp.concatenate([ref[...], ref[...]], 1)
     prm[4:5, :] = g3[...]
     prm[5:6, :] = s3[...]
-    fetch.wait()
-    for a, b, both in tap_blocks(wd_near):
+    for a, b, both in tap_blocks(wd):
         k = 2 - a
         fwd[a * wide : (a + 1) * wide, b * wide : (b + 1) * wide] = both
         bwd[b * wide : (b + 1) * wide, k * wide : (k + 1) * wide] = both
@@ -587,9 +590,9 @@
     twos = [bits[k : k + 2] for k in range(0, len(bits) - 1, 2)]
     for k in range(len(twos)):
         turn = [twos[(k + side * (len(twos) // 2)) % len(twos)] for side in range(2)]
+        both = flipped_dp(part, [pair[0] + pair[1] for pair in turn])
         low = flipped_dp(part, [pair[0] for pair in turn])
         high = flipped_dp(part, [pair[1] for pair in turn])
-        both = flipped_dp(part, [pair[0] + pair[1] for pair in turn])
         part = ((part.astype(F32) + low) + (high + both)).astype(BF16)
     if len(bits) % 2:
         part = (part.astype(F32) + flipped_dp(part, bits[-1:])).astype(BF16)
@@ -617,21 +620,20 @@
     w_rows = w_reduce.T
     gates = 2 * pixels * wide * chans
 
-    pre1, own1, im_held, w_held = call(
+    pre1, own1, im_held, w_held, wd_held = call(
         part(first_kernel, edge),
         [((half, wide), F32), ((WIDE_HEAD + edge, wide), BF16), ((pixels, chans), BF16)]
-        + [(w_rows.shape, BF16)],
-        im.reshape(2, half, chans), w_rows, flops=gates, far=(0, 1),
+        + [(w_rows.shape, BF16), (w_dilated.shape, BF16)],
+        im.reshape(2, half, chans), w_rows, w_dilated, flops=gates, far=(0, 1, 2),
         scratch=[pltpu.VMEM((2, half, chans), BF16), pltpu.VMEM(w_rows.shape, BF16)]
-        + [pltpu.SemaphoreType.DMA((3,))],
+        + [pltpu.VMEM(w_dilated.shape, BF16), pltpu.SemaphoreType.DMA((4,))],
     )
     rec1 = exchanged(own1, peers)
     fwd, bwd, we, prm = call(
         weights_kernel,
         [((3 * wide, 3 * wide), BF16)] * 2 + [(w_expand.shape, BF16), ((8, chans), F32)],
-        w_dilated, w_expand, row(gain_one), row(shift_one), row(gain_two), row(shift_two),
-        row(gain_three), row(shift_three), flops=10**10, far=(0,),
-        scratch=[pltpu.VMEM(w_dilated.shape, BF16), pltpu.SemaphoreType.DMA],
+        wd_held, w_expand, row(gain_one), row(shift_one), row(gain_two), row(shift_two),
+        row(gain_three), row(shift_three), flops=10**10,
     )
     ext, pre2, own2 = call(
         part(second_kernel, peers, edge),

time: 39.7 us -> 39.7 us (level)
  Pallas kernels: 14.7 us -> 13.8 us
  waiting for transfers between devices: 12.5 us -> 13 us
  starting transfers between devices: 11.4 us -> 11.8 us
    pallas_call x15, Pallas kernels: 14.7 us -> 13.8 us  [call(): pl.pallas_call(kernel, out_shape=[kind_of(shape, kind) for shape, kind in...]
    ppermute x8, waiting for transfers between devices: 3.71 us -> 4.25 us  [swapped(): lax.ppermute(value, axis, [(i, (i + step) % count) for i in range(count)])]
  transfers between devices with their start and end apart: 14 -> 14, of which waited for: 10 -> 11; matrix products, arithmetic and copies ran while one was open for 0% -> 0% of each run, Pallas kernels for 16% -> 14%
where the time goes in v4:
time: 39.7 us; the launch traced here: 39.5 us
  Pallas kernels  13.8 us (35%)
  waiting for transfers between devices  13 us (33%)
  starting transfers between devices  11.8 us (30%)
  between operations  0.84 us (2%)
    pallas_call x15, Pallas kernels, call(): pl.pallas_call(kernel, out_shape=[kind_of(shape, kind) for shape, kind in...  13.8 us
    ppermute x6, starting transfers between devices, flipped_dp(): return lax.ppermute(part, ('dp', 'space'), pairs).astype(F32)  8.86 us
    ppermute x6, waiting for transfers between devices, flipped_dp(): return lax.ppermute(part, ('dp', 'space'), pairs).astype(F32)  8.77 us
    ppermute x8, waiting for transfers between devices, swapped(): lax.ppermute(value, axis, [(i, (i + step) % count) for i in range(count)])  4.25 us
    ppermute x8, starting transfers between devices, swapped(): lax.ppermute(value, axis, [(i, (i + step) % count) for i in range(count)])  2.9 us
  transfers between devices with their start and end apart: 14, of which 11 were waited for; matrix products, arithmetic and copies ran while one was open for 0% of the time, Pallas kernels for 14%

profile of v4, /device:TPU:0, one launch (start us, length us, event | category | flops | bytes accessed | tf_op | source)
XLA Modules:
  0.0 39.5 jit_solution(12901342271822697097)
XLA Ops:
  0.6 0.0 copy-start.3
  0.7 0.0 copy-start.2
  0.7 0.0 copy-start.7
  0.7 0.0 copy-start.6
  0.7 2.1 %shard_map.194 = (f32[1152,128]{1,0:T(8,128)S(1)}, bf16[592,128]{1,0:T(8,128)(2,1)S(1)}, bf16[2304,256]{1,0:T(8,128)(2,1)S(1)}, bf16[64,256]{1,0:T(8,128)(2,1)S(1)}, bf16[3,3,64,64]{3,2,1,0:T(8,128)(2,1)S(1)}) custom-call(bf16[2,1152,256]{2,1,0:T(8,128)(2,1)} %bitcast.26, bf16[64,256]{1,0:T(8,128)(2,1)} %bitcast.29, bf16[3,3,64,64]{3,2,1,0:T(8,128)(2,1)} %wd.1), custom_call_target="tpu_custom_call" | custom-call | flops 150994944 | bytes 4751360 | tf_op jit(solution)/shard_map/pallas_call | solution.py:544
  2.8 0.6 %collective-permute-start = (bf16[592,128]{1,0:T(8,128)(2,1)S(1)}, bf16[592,128]{1,0:T(8,128)(2,1)S(1)}, u32[]{:S(2)}, u32[]{:S(2)}) collective-permute-start(bf16[592,128]{1,0:T(8,128)(2,1)S(1)} %get-tuple-element.51.own1), channel_id=1, source_target_pairs={{0,1},{1,0},{2,3},{3,2},{4,5},{5,4},{6,7},{7,6},{8,9},{9,8},{10,11... | collective-permute-start | bytes 454664 | tf_op jit(solution)/shard_map/ppermute | solution.py:558
  3.4 0.1 shard_map.195
  3.5 0.0 copy-start
  3.5 0.8 %collective-permute-done.rec1 = bf16[592,128]{1,0:T(8,128)(2,1)S(1)} collective-permute-done((bf16[592,128]{1,0:T(8,128)(2,1)S(1)}, bf16[592,128]{1,0:T(8,128)(2,1)S(1)}, u32[]{:S(2)}, u32[]{:S(2)}) %collective-permute-start) | collective-permute-done | bytes 151584 | tf_op jit(solution)/shard_map/ppermute | solution.py:558
  4.4 1.1 %shard_map.196 = (bf16[2304,128]{1,0:T(8,128)(2,1)S(1)}, f32[1152,128]{1,0:T(8,128)S(1)}, f32[8,128]{1,0:T(8,128)S(1)}) custom-call(f32[1152,128]{1,0:T(8,128)S(1)} %get-tuple-element.50.pre1, bf16[592,128]{1,0:T(8,128)(2,1)S(1)} %get-tuple-element.51.own1, bf16[592,128]{1,0:T(8,128)(2,1)S(1)} %collective-permute-done.rec1, ...), custom_call_target="tpu_custom_call" | custom-call | flops 339738624 | bytes 2969600 | tf_op jit(solution)/shard_map/pallas_call | solution.py:544
  5.5 0.4 collective-permute-start.1
  5.9 0.8 %collective-permute-done.1.rec2 = f32[8,128]{1,0:T(8,128)S(1)} collective-permute-done((f32[8,128]{1,0:T(8,128)S(1)}, f32[8,128]{1,0:T(8,128)S(1)}, u32[]{:S(2)}, u32[]{:S(2)}) %collective-permute-start.1) | collective-permute-done | bytes 4128 | tf_op jit(solution)/shard_map/ppermute | solution.py:558
  6.7 0.8 %shard_map.197 = (bf16[1152,128]{1,0:T(8,128)(2,1)S(1)}, f32[2304,256]{1,0:T(8,128)S(1)}, f32[8,256]{1,0:T(8,128)S(1)}) custom-call(f32[1152,128]{1,0:T(8,128)S(1)} %get-tuple-element.55.pre2, f32[8,128]{1,0:T(8,128)S(1)} %get-tuple-element.56.own2, f32[8,128]{1,0:T(8,128)S(1)} %collective-permute-done.1.rec2, f32[8,256]{1,0:T(8,128)S(1)} %get-tuple-element.53.prm, ...), custom_call_target="tpu_custom_call" | custom-call | flops 150994944 | bytes 3596288 | tf_op jit(solution)/shard_map/pallas_call | solution.py:544
  7.5 0.4 %collective-permute-start.2 = (f32[8,256]{1,0:T(8,128)S(1)}, f32[8,256]{1,0:T(8,128)S(1)}, u32[]{:S(2)}, u32[]{:S(2)}) collective-permute-start(f32[8,256]{1,0:T(8,128)S(1)} %get-tuple-element.59.own3), channel_id=1, source_target_pairs={{0,1},{1,0},{2,3},{3,2},{4,5},{5,4},{6,7},{7,6},{8,9},{9,8},{10,11... | collective-permute-start | bytes 24584 | tf_op jit(solution)/shard_map/ppermute | solution.py:558
  7.9 0.5 %shard_map.198 = (f32[2304,256]{1,0:T(8,128)S(1)}, f32[2304,256]{1,0:T(8,128)S(1)}) custom-call(bf16[2304,256]{1,0:T(8,128)(2,1)S(1)} %get-tuple-element.60.im, bf16[2304,256]{1,0:T(8,128)(2,1)S(1)} %bitcast.19), custom_call_target="tpu_custom_call" | custom-call | flops 2359296 | bytes 7077888 | tf_op jit(solution)/shard_map/pallas_call | solution.py:544
  8.4 0.3 collective-permute-done.2.rec3
  8.7 1.2 %shard_map.200 = (f32[2304,256]{1,0:T(8,128)S(1)}, f32[8,256]{1,0:T(8,128)S(1)}) custom-call(f32[2304,256]{1,0:T(8,128)S(1)} %get-tuple-element.58.pre3, f32[8,256]{1,0:T(8,128)S(1)} %get-tuple-element.59.own3, f32[8,256]{1,0:T(8,128)S(1)} %collective-permute-done.2.rec3, f32[8,256]{1,0:T(8,128)S(1)} %get-tuple-element.53.prm, ...), custom_call_target="tpu_custom_call" | custom-call | flops 17694720 | bytes 9469952 | tf_op jit(solution)/shard_map/pallas_call | solution.py:544
  10.0 0.4 %collective-permute-start.3 = (f32[8,256]{1,0:T(8,128)S(1)}, f32[8,256]{1,0:T(8,128)S(1)}, u32[]{:S(2)}, u32[]{:S(2)}) collective-permute-start(f32[8,256]{1,0:T(8,128)S(1)} %get-tuple-element.64.own4), channel_id=1, source_target_pairs={{0,1},{1,0},{2,3},{3,2},{4,5},{5,4},{6,7},{7,6},{8,9},{9,8},{10,11... | collective-permute-start | bytes 24584 | tf_op jit(solution)/shard_map/ppermute | solution.py:558
  10.4 0.4 %shard_map.201 = (f32[1152,128]{1,0:T(8,128)S(1)}, f32[1152,128]{1,0:T(8,128)S(1)}) custom-call(f32[1152,128]{1,0:T(8,128)S(1)} %get-tuple-element.50.pre1, bf16[592,128]{1,0:T(8,128)(2,1)S(1)} %get-tuple-element.51.own1, bf16[592,128]{1,0:T(8,128)(2,1)S(1)} %collective-permute-done.rec1, f32[1152,128]{1,0:T(8,128)S(1)} %get-tuple-element.55.pre2, ...), custom_call_target="tpu_custom_call" | custom-call | flops 4423680 | bytes 2678784 | tf_op jit(solution)/shard_map/pallas_call | solution.py:544
  10.8 0.4 %collective-permute-done.3.rec4 = f32[8,256]{1,0:T(8,128)S(1)} collective-permute-done((f32[8,256]{1,0:T(8,128)S(1)}, f32[8,256]{1,0:T(8,128)S(1)}, u32[]{:S(2)}, u32[]{:S(2)}) %collective-permute-start.3) | collective-permute-done | bytes 8224 | tf_op jit(solution)/shard_map/ppermute | solution.py:558
  11.2 0.7 %shard_map.202 = (bf16[2304,256]{1,0:T(8,128)(2,1)S(1)}, f32[1152,128]{1,0:T(8,128)S(1)}, bf16[1168,128]{1,0:T(8,128)(2,1)S(1)}) custom-call(f32[2304,256]{1,0:T(8,128)S(1)} %get-tuple-element.58.pre3, f32[2304,256]{1,0:T(8,128)S(1)} %get-tuple-element.63.e3, f32[8,256]{1,0:T(8,128)S(1)} %get-tuple-element.59.own3, ...), custom_call_target="tpu_custom_call" | custom-call | flops 150994944 | bytes 9527296 | tf_op jit(solution)/shard_map/pallas_call | solution.py:544
  11.9 0.4 %collective-permute-start.4 = (bf16[1168,128]{1,0:T(8,128)(2,1)S(1)}, bf16[1168,128]{1,0:T(8,128)(2,1)S(1)}, u32[]{:S(2)}, u32[]{:S(2)}) collective-permute-start(bf16[1168,128]{1,0:T(8,128)(2,1)S(1)} %get-tuple-element.67.own5), channel_id=1, source_target_pairs={{0,1},{1,0},{2,3},{3,2},{4,5},{5,4},{6,7},{7,6},{8,9},{9,8},{10,11... | collective-permute-start | bytes 897032 | tf_op jit(solution)/shard_map/ppermute | solution.py:558
  12.3 0.4 shard_map.205.gwe
  12.7 0.9 %collective-permute-done.4.rec5 = bf16[1168,128]{1,0:T(8,128)(2,1)S(1)} collective-permute-done((bf16[1168,128]{1,0:T(8,128)(2,1)S(1)}, bf16[1168,128]{1,0:T(8,128)(2,1)S(1)}, u32[]{:S(2)}, u32[]{:S(2)}) %collective-permute-start.4) | collective-permute-done | bytes 299040 | tf_op jit(solution)/shard_map/ppermute | solution.py:558
  13.6 1.1 %shard_map.203 = (bf16[2304,128]{1,0:T(8,128)(2,1)S(1)}, f32[1152,128]{1,0:T(8,128)S(1)}, f32[8,128]{1,0:T(8,128)S(1)}) custom-call(f32[1152,128]{1,0:T(8,128)S(1)} %get-tuple-element.55.pre2, f32[1152,128]{1,0:T(8,128)S(1)} %get-tuple-element.66.e2, bf16[1168,128]{1,0:T(8,128)(2,1)S(1)} %get-tuple-element.67.own5, ...), custom_call_target="tpu_custom_call" | custom-call | flops 339738624 | bytes 5345280 | tf_op jit(solution)/shard_map/pallas_call | solution.py:544
  14.6 0.3 collective-permute-start.5
  15.0 0.9 %shard_map.204.gwd = bf16[320,128]{1,0:T(8,128)(2,1)S(1)} custom-call(bf16[2304,128]{1,0:T(8,128)(2,1)S(1)} %get-tuple-element.72.ext, bf16[2304,128]{1,0:T(8,128)(2,1)S(1)} %get-tuple-element.73.dext), custom_call_target="tpu_custom_call" | custom-call | flops 339738624 | bytes 1343488 | tf_op jit(solution)/shard_map/pallas_call | solution.py:544
  15.9 0.0 collective-permute-done.5.rec6
  15.9 0.4 %shard_map.206 = (bf16[1152,128]{1,0:T(8,128)(2,1)S(1)}, bf16[304,128]{1,0:T(8,128)(2,1)S(1)}, bf16[304,128]{1,0:T(8,128)(2,1)S(1)}) custom-call(f32[1152,128]{1,0:T(8,128)S(1)} %get-tuple-element.50.pre1, f32[1152,128]{1,0:T(8,128)S(1)} %get-tuple-element.70.e1, f32[8,128]{1,0:T(8,128)S(1)} %get-tuple-element.71.own6, ...), custom_call_target="tpu_custom_call" | custom-call | flops 150994944 | bytes 4034560 | tf_op jit(solution)/shard_map/pallas_call | solution.py:544
  16.3 0.3 collective-permute-start.6
  16.6 1.0 %collective-permute-done.6 = bf16[304,128]{1,0:T(8,128)(2,1)S(1)} collective-permute-done((bf16[304,128]{1,0:T(8,128)(2,1)S(1)}, bf16[304,128]{1,0:T(8,128)(2,1)S(1)}, u32[]{:S(2)}, u32[]{:S(2)}) %collective-permute-start.6) | collective-permute-done | bytes 77856 | tf_op jit(solution)/shard_map/ppermute | solution.py:558
  17.7 3.8 %collective-permute-start.9 = (bf16[304,128]{1,0:T(8,128)(2,1)S(1)}, bf16[304,128]{1,0:T(8,128)(2,1)S(1)}, u32[]{:S(2)}, u32[]{:S(2)}) collective-permute-start(bf16[304,128]{1,0:T(8,128)(2,1)S(1)} %add_convert_fusion.2), channel_id=1, source_target_pairs={{0,6},{1,25},{2,4},{3,27},{4,2},{5,29},{6,0},{7,31},{8,14},{9,17},... | collective-permute-start | bytes 233480 | tf_op jit(solution)/shard_map/ppermute | solution.py:582
  21.4 0.5 %collective-permute-start.8 = (bf16[304,128]{1,0:T(8,128)(2,1)S(1)}, bf16[304,128]{1,0:T(8,128)(2,1)S(1)}, u32[]{:S(2)}, u32[]{:S(2)}) collective-permute-start(bf16[304,128]{1,0:T(8,128)(2,1)S(1)} %add_convert_fusion.2), channel_id=1, source_target_pairs={{0,4},{1,17},{2,6},{3,19},{4,0},{5,21},{6,2},{7,23},{8,12},{9,25},... | collective-permute-start | bytes 233480 | tf_op jit(solution)/shard_map/ppermute | solution.py:582
  22.0 0.1 collective-permute-start.7
  22.1 1.7 %collective-permute-done.9 = bf16[304,128]{1,0:T(8,128)(2,1)S(1)} collective-permute-done((bf16[304,128]{1,0:T(8,128)(2,1)S(1)}, bf16[304,128]{1,0:T(8,128)(2,1)S(1)}, u32[]{:S(2)}, u32[]{:S(2)}) %collective-permute-start.9) | collective-permute-done | bytes 77856 | tf_op jit(solution)/shard_map/ppermute | solution.py:582
  23.8 2.0 %collective-permute-done.8 = bf16[304,128]{1,0:T(8,128)(2,1)S(1)} collective-permute-done((bf16[304,128]{1,0:T(8,128)(2,1)S(1)}, bf16[304,128]{1,0:T(8,128)(2,1)S(1)}, u32[]{:S(2)}, u32[]{:S(2)}) %collective-permute-start.8) | collective-permute-done | bytes 77856 | tf_op jit(solution)/shard_map/ppermute | solution.py:582
  25.8 0.5 %collective-permute-done.7 = bf16[304,128]{1,0:T(8,128)(2,1)S(1)} collective-permute-done((bf16[304,128]{1,0:T(8,128)(2,1)S(1)}, bf16[304,128]{1,0:T(8,128)(2,1)S(1)}, u32[]{:S(2)}, u32[]{:S(2)}) %collective-permute-start.7) | collective-permute-done | bytes 77856 | tf_op jit(solution)/shard_map/ppermute | solution.py:582
  26.4 3.7 %collective-permute-start.12 = (bf16[304,128]{1,0:T(8,128)(2,1)S(1)}, bf16[304,128]{1,0:T(8,128)(2,1)S(1)}, u32[]{:S(2)}, u32[]{:S(2)}) collective-permute-start(bf16[304,128]{1,0:T(8,128)(2,1)S(1)} %add_convert_fusion.1), channel_id=1, source_target_pairs={{0,24},{1,7},{2,26},{3,5},{4,28},{5,3},{6,30},{7,1},{8,16},{9,15},... | collective-permute-start | bytes 233480 | tf_op jit(solution)/shard_map/ppermute | solution.py:582
  30.1 0.0 collective-permute-start.11
  30.1 0.8 %collective-permute-start.10 = (bf16[304,128]{1,0:T(8,128)(2,1)S(1)}, bf16[304,128]{1,0:T(8,128)(2,1)S(1)}, u32[]{:S(2)}, u32[]{:S(2)}) collective-permute-start(bf16[304,128]{1,0:T(8,128)(2,1)S(1)} %add_convert_fusion.1), channel_id=1, source_target_pairs={{0,8},{1,3},{2,10},{3,1},{4,12},{5,7},{6,14},{7,5},{8,0},{9,11},{1... | collective-permute-start | bytes 233480 | tf_op jit(solution)/shard_map/ppermute | solution.py:582
  30.9 1.9 %collective-permute-done.12 = bf16[304,128]{1,0:T(8,128)(2,1)S(1)} collective-permute-done((bf16[304,128]{1,0:T(8,128)(2,1)S(1)}, bf16[304,128]{1,0:T(8,128)(2,1)S(1)}, u32[]{:S(2)}, u32[]{:S(2)}) %collective-permute-start.12) | collective-permute-done | bytes 77856 | tf_op jit(solution)/shard_map/ppermute | solution.py:582
  32.7 2.6 %collective-permute-done.11 = bf16[304,128]{1,0:T(8,128)(2,1)S(1)} collective-permute-done((bf16[304,128]{1,0:T(8,128)(2,1)S(1)}, bf16[304,128]{1,0:T(8,128)(2,1)S(1)}, u32[]{:S(2)}, u32[]{:S(2)}) %collective-permute-start.11) | collective-permute-done | bytes 77856 | tf_op jit(solution)/shard_map/ppermute | solution.py:582
  35.4 0.0 collective-permute-done.10
  35.4 0.1 collective-permute-start.13
  35.5 1.7 %shard_map.199 = bf16[2304,256]{1,0:T(8,128)(2,1)} custom-call(f32[2304,256]{1,0:T(8,128)S(1)} %get-tuple-element.58.pre3, f32[8,256]{1,0:T(8,128)S(1)} %get-tuple-element.59.own3, f32[8,256]{1,0:T(8,128)S(1)} %collective-permute-done.2.rec3, f32[8,256]{1,0:T(8,128)S(1)} %get-tuple-element.53.prm, f32[2304,256]{1,0:T(8,128)S(1)} %get-tuple-element.61.im_half), custom_call_target="tpu_custom_call" | custom-call | flops 5898240 | bytes 7102464 | tf_op jit(solution)/shard_map/pallas_call | solution.py:544
  37.2 1.5 %shard_map.207 = bf16[2304,256]{1,0:T(8,128)(2,1)} custom-call(bf16[1152,128]{1,0:T(8,128)(2,1)S(1)} %get-tuple-element.76.dh1, bf16[64,256]{1,0:T(8,128)(2,1)S(1)} %get-tuple-element.77.w, f32[2304,256]{1,0:T(8,128)S(1)} %get-tuple-element.63.e3), custom_call_target="tpu_custom_call" | custom-call | flops 150994944 | bytes 5046272 | tf_op jit(solution)/shard_map/pallas_call | solution.py:544
  38.7 0.0 collective-permute-done.13.refs_1_
  38.7 0.9 %shard_map.208 = (f32[64,256]{1,0:T(8,128)}, f32[9,64,64]{2,1,0:T(8,128)}, f32[64,256]{1,0:T(8,128)}, f32[1,64]{1,0:T(1,128)}, f32[1,64]{1,0:T(1,128)}, /*index=...) custom-call(bf16[304,128]{1,0:T(8,128)(2,1)S(1)} %add_convert_fusion.refs_0_, ...), custom_call_target="tpu_custom_call" | custom-call | bytes 437248 | tf_op jit(solution)/shard_map/pallas_call | solution.py:544
  (14 shorter events, 0.1 us)
Async XLA Ops:
  0.6 2.7 %copy-start.3 = (f32[256]{0:T(256)S(1)}, f32[256]{0:T(256)}, u32[]{:S(2)}) copy-start(f32[256]{0:T(256)} %param.20) | copy-start | bytes 3076
  0.7 2.7 %copy-start.2 = (f32[256]{0:T(256)S(1)}, f32[256]{0:T(256)}, u32[]{:S(2)}) copy-start(f32[256]{0:T(256)} %param.19) | copy-start | bytes 3076
  0.7 2.7 %copy-start.7 = (f32[64]{0:T(128)S(1)}, f32[64]{0:T(128)}, u32[]{:S(2)}) copy-start(f32[64]{0:T(128)} %param.18) | copy-start | bytes 772
  0.7 2.7 %copy-start.6 = (f32[64]{0:T(128)S(1)}, f32[64]{0:T(128)}, u32[]{:S(2)}) copy-start(f32[64]{0:T(128)} %param.17) | copy-start | bytes 772
  0.7 2.7 %copy-start.5 = (f32[64]{0:T(128)S(1)}, f32[64]{0:T(128)}, u32[]{:S(2)}) copy-start(f32[64]{0:T(128)} %param.16) | copy-start | bytes 772
  0.7 2.7 %copy-start.4 = (f32[64]{0:T(128)S(1)}, f32[64]{0:T(128)}, u32[]{:S(2)}) copy-start(f32[64]{0:T(128)} %param.15) | copy-start | bytes 772
  0.7 2.7 %copy-start.1 = (bf16[64,256]{1,0:T(8,128)(2,1)S(1)}, bf16[64,256]{1,0:T(8,128)(2,1)}, u32[]{:S(2)}) copy-start(bf16[64,256]{1,0:T(8,128)(2,1)} %we.1) | copy-start | bytes 98308
  2.8 1.6 %collective-permute-start = (bf16[592,128]{1,0:T(8,128)(2,1)S(1)}, bf16[592,128]{1,0:T(8,128)(2,1)S(1)}, u32[]{:S(2)}, u32[]{:S(2)}) collective-permute-start(bf16[592,128]{1,0:T(8,128)(2,1)S(1)} %get-tuple-element.51.own1), channel_id=1, source_target_pairs={{0,1},{1,0},{2,3},{3,2},{4,5},{5,4},{6,7},{7,6},{8,9},{9,8},{10,11... | collective-permute-start | bytes 454664 | tf_op jit(solution)/shard_map/ppermute | solution.py:558
  3.5 4.4 %copy-start = (bf16[1,8,288,256]{3,2,1,0:T(8,128)(2,1)S(1)}, bf16[1,8,288,256]{3,2,1,0:T(8,128)(2,1)}, u32[]{:S(2)}) copy-start(bf16[1,8,288,256]{3,2,1,0:T(8,128)(2,1)} %param.21) | copy-start | bytes 3538948
  5.5 1.2 %collective-permute-start.1 = (f32[8,128]{1,0:T(8,128)S(1)}, f32[8,128]{1,0:T(8,128)S(1)}, u32[]{:S(2)}, u32[]{:S(2)}) collective-permute-start(f32[8,128]{1,0:T(8,128)S(1)} %get-tuple-element.56.own2), channel_id=1, source_target_pairs={{0,1},{1,0},{2,3},{3,2},{4,5},{5,4},{6,7},{7,6},{8,9},{9,8},{10,11... | collective-permute-start | bytes 12296 | tf_op jit(solution)/shard_map/ppermute | solution.py:558
  7.5 1.2 %collective-permute-start.2 = (f32[8,256]{1,0:T(8,128)S(1)}, f32[8,256]{1,0:T(8,128)S(1)}, u32[]{:S(2)}, u32[]{:S(2)}) collective-permute-start(f32[8,256]{1,0:T(8,128)S(1)} %get-tuple-element.59.own3), channel_id=1, source_target_pairs={{0,1},{1,0},{2,3},{3,2},{4,5},{5,4},{6,7},{7,6},{8,9},{9,8},{10,11... | collective-permute-start | bytes 24584 | tf_op jit(solution)/shard_map/ppermute | solution.py:558
  10.0 1.2 %collective-permute-start.3 = (f32[8,256]{1,0:T(8,128)S(1)}, f32[8,256]{1,0:T(8,128)S(1)}, u32[]{:S(2)}, u32[]{:S(2)}) collective-permute-start(f32[8,256]{1,0:T(8,128)S(1)} %get-tuple-element.64.own4), channel_id=1, source_target_pairs={{0,1},{1,0},{2,3},{3,2},{4,5},{5,4},{6,7},{7,6},{8,9},{9,8},{10,11... | collective-permute-start | bytes 24584 | tf_op jit(solution)/shard_map/ppermute | solution.py:558
  11.9 1.7 %collective-permute-start.4 = (bf16[1168,128]{1,0:T(8,128)(2,1)S(1)}, bf16[1168,128]{1,0:T(8,128)(2,1)S(1)}, u32[]{:S(2)}, u32[]{:S(2)}) collective-permute-start(bf16[1168,128]{1,0:T(8,128)(2,1)S(1)} %get-tuple-element.67.own5), channel_id=1, source_target_pairs={{0,1},{1,0},{2,3},{3,2},{4,5},{5,4},{6,7},{7,6},{8,9},{9,8},{10,11... | collective-permute-start | bytes 897032 | tf_op jit(solution)/shard_map/ppermute | solution.py:558
  14.6 1.2 %collective-permute-start.5 = (f32[8,128]{1,0:T(8,128)S(1)}, f32[8,128]{1,0:T(8,128)S(1)}, u32[]{:S(2)}, u32[]{:S(2)}) collective-permute-start(f32[8,128]{1,0:T(8,128)S(1)} %get-tuple-element.71.own6), channel_id=1, source_target_pairs={{0,1},{1,0},{2,3},{3,2},{4,5},{5,4},{6,7},{7,6},{8,9},{9,8},{10,11... | collective-permute-start | bytes 12296 | tf_op jit(solution)/shard_map/ppermute | solution.py:558
  16.3 1.3 %collective-permute-start.6 = (bf16[304,128]{1,0:T(8,128)(2,1)S(1)}, bf16[304,128]{1,0:T(8,128)(2,1)S(1)}, u32[]{:S(2)}, u32[]{:S(2)}) collective-permute-start(bf16[304,128]{1,0:T(8,128)(2,1)S(1)} %get-tuple-element.79), channel_id=1, source_target_pairs={{0,1},{1,0},{2,3},{3,2},{4,5},{5,4},{6,7},{7,6},{8,9},{9,8},{10,11... | collective-permute-start | bytes 233480 | tf_op jit(solution)/shard_map/ppermute | solution.py:558
  17.7 6.1 %collective-permute-start.9 = (bf16[304,128]{1,0:T(8,128)(2,1)S(1)}, bf16[304,128]{1,0:T(8,128)(2,1)S(1)}, u32[]{:S(2)}, u32[]{:S(2)}) collective-permute-start(bf16[304,128]{1,0:T(8,128)(2,1)S(1)} %add_convert_fusion.2), channel_id=1, source_target_pairs={{0,6},{1,25},{2,4},{3,27},{4,2},{5,29},{6,0},{7,31},{8,14},{9,17},... | collective-permute-start | bytes 233480 | tf_op jit(solution)/shard_map/ppermute | solution.py:582
  21.4 4.4 %collective-permute-start.8 = (bf16[304,128]{1,0:T(8,128)(2,1)S(1)}, bf16[304,128]{1,0:T(8,128)(2,1)S(1)}, u32[]{:S(2)}, u32[]{:S(2)}) collective-permute-start(bf16[304,128]{1,0:T(8,128)(2,1)S(1)} %add_convert_fusion.2), channel_id=1, source_target_pairs={{0,4},{1,17},{2,6},{3,19},{4,0},{5,21},{6,2},{7,23},{8,12},{9,25},... | collective-permute-start | bytes 233480 | tf_op jit(solution)/shard_map/ppermute | solution.py:582
  22.0 4.4 %collective-permute-start.7 = (bf16[304,128]{1,0:T(8,128)(2,1)S(1)}, bf16[304,128]{1,0:T(8,128)(2,1)S(1)}, u32[]{:S(2)}, u32[]{:S(2)}) collective-permute-start(bf16[304,128]{1,0:T(8,128)(2,1)S(1)} %add_convert_fusion.2), channel_id=1, source_target_pairs={{0,2},{1,9},{2,0},{3,11},{4,6},{5,13},{6,4},{7,15},{8,10},{9,1},{1... | collective-permute-start | bytes 233480 | tf_op jit(solution)/shard_map/ppermute | solution.py:582
  26.4 6.3 %collective-permute-start.12 = (bf16[304,128]{1,0:T(8,128)(2,1)S(1)}, bf16[304,128]{1,0:T(8,128)(2,1)S(1)}, u32[]{:S(2)}, u32[]{:S(2)}) collective-permute-start(bf16[304,128]{1,0:T(8,128)(2,1)S(1)} %add_convert_fusion.1), channel_id=1, source_target_pairs={{0,24},{1,7},{2,26},{3,5},{4,28},{5,3},{6,30},{7,1},{8,16},{9,15},... | collective-permute-start | bytes 233480 | tf_op jit(solution)/shard_map/ppermute | solution.py:582
  30.1 5.3 %collective-permute-start.11 = (bf16[304,128]{1,0:T(8,128)(2,1)S(1)}, bf16[304,128]{1,0:T(8,128)(2,1)S(1)}, u32[]{:S(2)}, u32[]{:S(2)}) collective-permute-start(bf16[304,128]{1,0:T(8,128)(2,1)S(1)} %add_convert_fusion.1), channel_id=1, source_target_pairs={{0,16},{1,5},{2,18},{3,7},{4,20},{5,1},{6,22},{7,3},{8,24},{9,13},... | collective-permute-start | bytes 233480 | tf_op jit(solution)/shard_map/ppermute | solution.py:582
  30.1 5.3 %collective-permute-start.10 = (bf16[304,128]{1,0:T(8,128)(2,1)S(1)}, bf16[304,128]{1,0:T(8,128)(2,1)S(1)}, u32[]{:S(2)}, u32[]{:S(2)}) collective-permute-start(bf16[304,128]{1,0:T(8,128)(2,1)S(1)} %add_convert_fusion.1), channel_id=1, source_target_pairs={{0,8},{1,3},{2,10},{3,1},{4,12},{5,7},{6,14},{7,5},{8,0},{9,11},{1... | collective-permute-start | bytes 233480 | tf_op jit(solution)/shard_map/ppermute | solution.py:582
  35.4 3.3 %collective-permute-start.13 = (bf16[304,128]{1,0:T(8,128)(2,1)S(1)}, bf16[304,128]{1,0:T(8,128)(2,1)S(1)}, u32[]{:S(2)}, u32[]{:S(2)}) collective-permute-start(bf16[304,128]{1,0:T(8,128)(2,1)S(1)} %add_convert_fusion.refs_0_), channel_id=1, source_target_pairs={{0,1},{1,0},{2,3},{3,2},{4,5},{5,4},{6,7},{7,6},{8,9},{9,8},{10,11... | collective-permute-start | bytes 233480 | tf_op jit(solution)/shard_map/ppermute | solution.py:558

commit v5 on v4

--- a/solution.py
+++ b/solution.py
@@ -97,10 +97,36 @@
     return jnp.concatenate(three_terms(first) + three_terms(second) + [rest], 0).astype(BF16)
 
 
-def edges(ref, edge, centre=0.0):
-    size = ref.shape[0]
-    top = ref[0:edge, :]
-    return swap_halves(jnp.where(lower_half(top.shape), top, ref[size - edge : size, :]) - centre)
+def halo_rows(edge, peers):
+    return edge // 2 if peers == 1 else edge
+
+
+def edges(ref, edge, peers, centre=0.0):
+    size, cols = ref.shape[0], edge // 2
+    top, low = ref[0:edge, :], ref[size - edge : size, :]
+    if peers != 1:
+        return swap_halves(jnp.where(lower_half(top.shape), top, low) - centre)
+    first = lax.axis_index("space") == 0
+    turned = swap_halves(jnp.where(first, low[0:cols, :], top[cols:, :]) - centre)
+    straight = jnp.where(first, low[cols:, :], top[0:cols, :]) - centre
+    lanes = lower_half(turned.shape)
+    return jnp.where(first, jnp.where(lanes, turned, straight), jnp.where(lanes, straight, turned))
+
+
+def received(rec, base, edge, peers):
+    part = rec[base : base + halo_rows(edge, peers), :].astype(F32)
+    if peers != 1:
+        return part
+    turned = swap_halves(part)
+    lanes = lower_half(part.shape)
+    return jnp.concatenate(
+        [jnp.where(lanes, part, turned), jnp.where(lanes, turned, part)], 0
+    )
+
+
+def sender_row(rec, peers, which):
+    above, below = head_row(rec, 0, which), head_row(rec, peers - 1, which)
+    return jnp.where(lower_half(above.shape), above, below)
 
 
 def fill_edges(ext, first, last, halo, edge):
@@ -131,7 +157,7 @@
 
 
 def first_kernel(
-    edge, im, w, wd, pre, msg, im_held, w_held, wd_held, im_near, w_near, wd_near, sems
+    peers, edge, im, w, wd, pre, msg, im_held, w_held, wd_held, im_near, w_near, wd_near, sems
 ):
     half, cols, wide = pre.shape[0], edge // 2, pre.shape[1]
     fetch = pltpu.make_async_copy(w, w_near, sems.at[0])
@@ -165,7 +191,7 @@
         acc = acc + group(part)
     mean = both_halves(rowsum(acc)) / (2 * half)
     msg[0:WIDE_HEAD, :] = wide_head_rows(mean, both_halves(centred_squares(pre, mean, cols)))
-    msg[WIDE_HEAD:, :] = edges(pre, edge, mean).astype(BF16)
+    msg[WIDE_HEAD:, :] = edges(pre, edge, peers, mean).astype(BF16)
     fetch_wd.wait()
     wd_held[...] = wd_near[...]
 
@@ -234,9 +260,8 @@
     first = jnp.concatenate([act for at, act in acts if at < edge], 0)
     last = jnp.concatenate([act for at, act in acts if at >= half - edge], 0)
     if peers:
-        above, below = head_row(rec1, 0, 0), head_row(rec1, peers - 1, 0)
-        centre = jnp.where(lower_half(above.shape), above, below)
-        halo = silu((rec1[WIDE_HEAD * peers :, :].astype(F32) + centre) * scale + bias)
+        centre = sender_row(rec1, peers, 0)
+        halo = silu((received(rec1, WIDE_HEAD * peers, edge, peers) + centre) * scale + bias)
     else:
         halo = jnp.zeros((edge, wide), F32)
     fill_edges(ext, first, last, halo, edge)
@@ -367,9 +392,11 @@
         e2[at : at + cols, :] = grad
         sums = sums + group(grad)
         cross = cross + group(grad * (pre - mean))
-    msg[0:WIDE_HEAD, :] = wide_head_rows(both_halves(rowsum(sums)), both_halves(rowsum(cross) * inv))
-    msg[WIDE_HEAD : WIDE_HEAD + edge, :] = edges(e2, edge).astype(BF16)
-    msg[WIDE_HEAD + edge :, :] = edges(pre2, edge, mean).astype(BF16)
+    sums = both_halves(rowsum(sums))
+    msg[0:WIDE_HEAD, :] = wide_head_rows(sums, both_halves(rowsum(cross) * inv))
+    base = WIDE_HEAD + halo_rows(edge, peers)
+    msg[WIDE_HEAD:base, :] = edges(e2, edge, peers, sums / size).astype(BF16)
+    msg[base:, :] = edges(pre2, edge, peers, mean).astype(BF16)
 
 
 def expand_kernel(act2, dh3, out):
@@ -401,11 +428,9 @@
     last = jnp.concatenate([act for at, act in acts if at >= half - edge], 0)
     if peers:
         base = WIDE_HEAD * peers
-        halo = (
-            rec5[base : base + edge, :].astype(F32) * scale2
-            + rec5[base + edge :, :].astype(F32) * slant2
-            + (bias2 + slant2 * mean2)
-        )
+        grad = received(rec5, base, edge, peers) + sender_row(rec5, peers, 0) / size
+        pre = received(rec5, base + halo_rows(edge, peers), edge, peers) + mean2
+        halo = grad * scale2 + pre * slant2 + bias2
     else:
         halo = jnp.zeros((edge, wide), F32)
     fill_edges(dext, first, last, halo, edge)
@@ -621,8 +646,8 @@
     gates = 2 * pixels * wide * chans
 
     pre1, own1, im_held, w_held, wd_held = call(
-        part(first_kernel, edge),
-        [((half, wide), F32), ((WIDE_HEAD + edge, wide), BF16), ((pixels, chans), BF16)]
+        part(first_kernel, peers, edge),
+        [((half, wide), F32), ((WIDE_HEAD + halo_rows(edge, peers), wide), BF16), ((pixels, chans), BF16)]
         + [(w_rows.shape, BF16), (w_dilated.shape, BF16)],
         im.reshape(2, half, chans), w_rows, w_dilated, flops=gates, far=(0, 1, 2),
         scratch=[pltpu.VMEM((2, half, chans), BF16), pltpu.VMEM(w_rows.shape, BF16)]
@@ -662,7 +687,7 @@
     rec4 = exchanged(own4, peers)
     dh3, e2, own5 = call(
         part(fifth_kernel, peers, edge),
-        [((pixels, chans), BF16), ((half, wide), F32), ((WIDE_HEAD + 2 * edge, wide), BF16)],
+        [((pixels, chans), BF16), ((half, wide), F32), ((WIDE_HEAD + 2 * halo_rows(edge, peers), wide), BF16)],
         pre3, e3, own3, rec3, own4, rec4, prm, we, pre2, own2, rec2, slope2, flops=gates,
     )
     rec5 = exchanged(own5, peers)

time: 39.7 us -> 39.6 us (level)
  no operation moved by 1% of the time
where the time goes in v5:
time: 39.6 us; the launch traced here: 39.5 us
  Pallas kernels  14 us (35%)
  waiting for transfers between devices  12.7 us (32%)
  starting transfers between devices  11.7 us (30%)
  between operations  0.84 us (2%)
    pallas_call x15, Pallas kernels, call(): pl.pallas_call(kernel, out_shape=[kind_of(shape, kind) for shape, kind in...  14 us
    ppermute x6, starting transfers between devices, flipped_dp(): return lax.ppermute(part, ('dp', 'space'), pairs).astype(F32)  8.84 us
    ppermute x6, waiting for transfers between devices, flipped_dp(): return lax.ppermute(part, ('dp', 'space'), pairs).astype(F32)  8.77 us
    ppermute x8, waiting for transfers between devices, swapped(): lax.ppermute(value, axis, [(i, (i + step) % count) for i in range(count)])  3.97 us
    ppermute x8, starting transfers between devices, swapped(): lax.ppermute(value, axis, [(i, (i + step) % count) for i in range(count)])  2.87 us
  transfers between devices with their start and end apart: 14, of which 11 were waited for; matrix products, arithmetic and copies ran while one was open for 0% of the time, Pallas kernels for 14%

profile of v5, /device:TPU:0, one launch (start us, length us, event | category | flops | bytes accessed | tf_op | source)
XLA Modules:
  0.0 39.5 jit_solution(8842498978771740012)
XLA Ops:
  0.6 0.0 copy-start.3
  0.7 0.0 copy-start.2
  0.7 0.0 copy-start.7
  0.7 0.0 copy-start.6
  0.7 2.1 %shard_map.194 = (f32[1152,128]{1,0:T(8,128)S(1)}, bf16[304,128]{1,0:T(8,128)(2,1)S(1)}, bf16[2304,256]{1,0:T(8,128)(2,1)S(1)}, bf16[64,256]{1,0:T(8,128)(2,1)S(1)}, bf16[3,3,64,64]{3,2,1,0:T(8,128)(2,1)S(1)}) custom-call(bf16[2,1152,256]{2,1,0:T(8,128)(2,1)} %bitcast.26, bf16[64,256]{1,0:T(8,128)(2,1)} %bitcast.29, bf16[3,3,64,64]{3,2,1,0:T(8,128)(2,1)} %wd.1), custom_call_target="tpu_custom_call" | custom-call | flops 150994944 | bytes 4603904 | tf_op jit(solution)/shard_map/pallas_call | solution.py:569
  2.8 0.6 %collective-permute-start = (bf16[304,128]{1,0:T(8,128)(2,1)S(1)}, bf16[304,128]{1,0:T(8,128)(2,1)S(1)}, u32[]{:S(2)}, u32[]{:S(2)}) collective-permute-start(bf16[304,128]{1,0:T(8,128)(2,1)S(1)} %get-tuple-element.51.own1), channel_id=1, source_target_pairs={{0,1},{1,0},{2,3},{3,2},{4,5},{5,4},{6,7},{7,6},{8,9},{9,8},{10,11... | collective-permute-start | bytes 233480 | tf_op jit(solution)/shard_map/ppermute | solution.py:583
  3.4 0.1 shard_map.195
  3.5 0.0 copy-start
  3.5 0.7 %collective-permute-done.rec1 = bf16[304,128]{1,0:T(8,128)(2,1)S(1)} collective-permute-done((bf16[304,128]{1,0:T(8,128)(2,1)S(1)}, bf16[304,128]{1,0:T(8,128)(2,1)S(1)}, u32[]{:S(2)}, u32[]{:S(2)}) %collective-permute-start) | collective-permute-done | bytes 77856 | tf_op jit(solution)/shard_map/ppermute | solution.py:583
  4.3 1.2 %shard_map.196 = (bf16[2304,128]{1,0:T(8,128)(2,1)S(1)}, f32[1152,128]{1,0:T(8,128)S(1)}, f32[8,128]{1,0:T(8,128)S(1)}) custom-call(f32[1152,128]{1,0:T(8,128)S(1)} %get-tuple-element.50.pre1, bf16[304,128]{1,0:T(8,128)(2,1)S(1)} %get-tuple-element.51.own1, bf16[304,128]{1,0:T(8,128)(2,1)S(1)} %collective-permute-done.rec1, ...), custom_call_target="tpu_custom_call" | custom-call | flops 339738624 | bytes 2822144 | tf_op jit(solution)/shard_map/pallas_call | solution.py:569
  5.5 0.4 collective-permute-start.1
  5.9 0.8 %collective-permute-done.1.rec2 = f32[8,128]{1,0:T(8,128)S(1)} collective-permute-done((f32[8,128]{1,0:T(8,128)S(1)}, f32[8,128]{1,0:T(8,128)S(1)}, u32[]{:S(2)}, u32[]{:S(2)}) %collective-permute-start.1) | collective-permute-done | bytes 4128 | tf_op jit(solution)/shard_map/ppermute | solution.py:583
  6.7 0.8 %shard_map.197 = (bf16[1152,128]{1,0:T(8,128)(2,1)S(1)}, f32[2304,256]{1,0:T(8,128)S(1)}, f32[8,256]{1,0:T(8,128)S(1)}) custom-call(f32[1152,128]{1,0:T(8,128)S(1)} %get-tuple-element.55.pre2, f32[8,128]{1,0:T(8,128)S(1)} %get-tuple-element.56.own2, f32[8,128]{1,0:T(8,128)S(1)} %collective-permute-done.1.rec2, f32[8,256]{1,0:T(8,128)S(1)} %get-tuple-element.53.prm, ...), custom_call_target="tpu_custom_call" | custom-call | flops 150994944 | bytes 3596288 | tf_op jit(solution)/shard_map/pallas_call | solution.py:569
  7.5 0.4 %collective-permute-start.2 = (f32[8,256]{1,0:T(8,128)S(1)}, f32[8,256]{1,0:T(8,128)S(1)}, u32[]{:S(2)}, u32[]{:S(2)}) collective-permute-start(f32[8,256]{1,0:T(8,128)S(1)} %get-tuple-element.59.own3), channel_id=1, source_target_pairs={{0,1},{1,0},{2,3},{3,2},{4,5},{5,4},{6,7},{7,6},{8,9},{9,8},{10,11... | collective-permute-start | bytes 24584 | tf_op jit(solution)/shard_map/ppermute | solution.py:583
  7.9 0.5 %shard_map.198 = (f32[2304,256]{1,0:T(8,128)S(1)}, f32[2304,256]{1,0:T(8,128)S(1)}) custom-call(bf16[2304,256]{1,0:T(8,128)(2,1)S(1)} %get-tuple-element.60.im, bf16[2304,256]{1,0:T(8,128)(2,1)S(1)} %bitcast.19), custom_call_target="tpu_custom_call" | custom-call | flops 2359296 | bytes 7077888 | tf_op jit(solution)/shard_map/pallas_call | solution.py:569
  8.4 0.3 collective-permute-done.2.rec3
  8.7 1.2 %shard_map.200 = (f32[2304,256]{1,0:T(8,128)S(1)}, f32[8,256]{1,0:T(8,128)S(1)}) custom-call(f32[2304,256]{1,0:T(8,128)S(1)} %get-tuple-element.58.pre3, f32[8,256]{1,0:T(8,128)S(1)} %get-tuple-element.59.own3, f32[8,256]{1,0:T(8,128)S(1)} %collective-permute-done.2.rec3, f32[8,256]{1,0:T(8,128)S(1)} %get-tuple-element.53.prm, ...), custom_call_target="tpu_custom_call" | custom-call | flops 17694720 | bytes 9469952 | tf_op jit(solution)/shard_map/pallas_call | solution.py:569
  10.0 0.4 %collective-permute-start.3 = (f32[8,256]{1,0:T(8,128)S(1)}, f32[8,256]{1,0:T(8,128)S(1)}, u32[]{:S(2)}, u32[]{:S(2)}) collective-permute-start(f32[8,256]{1,0:T(8,128)S(1)} %get-tuple-element.64.own4), channel_id=1, source_target_pairs={{0,1},{1,0},{2,3},{3,2},{4,5},{5,4},{6,7},{7,6},{8,9},{9,8},{10,11... | collective-permute-start | bytes 24584 | tf_op jit(solution)/shard_map/ppermute | solution.py:583
  10.4 0.4 %shard_map.201 = (f32[1152,128]{1,0:T(8,128)S(1)}, f32[1152,128]{1,0:T(8,128)S(1)}) custom-call(f32[1152,128]{1,0:T(8,128)S(1)} %get-tuple-element.50.pre1, bf16[304,128]{1,0:T(8,128)(2,1)S(1)} %get-tuple-element.51.own1, bf16[304,128]{1,0:T(8,128)(2,1)S(1)} %collective-permute-done.rec1, f32[1152,128]{1,0:T(8,128)S(1)} %get-tuple-element.55.pre2, ...), custom_call_target="tpu_custom_call" | custom-call | flops 4423680 | bytes 2531328 | tf_op jit(solution)/shard_map/pallas_call | solution.py:569
  10.8 0.4 %collective-permute-done.3.rec4 = f32[8,256]{1,0:T(8,128)S(1)} collective-permute-done((f32[8,256]{1,0:T(8,128)S(1)}, f32[8,256]{1,0:T(8,128)S(1)}, u32[]{:S(2)}, u32[]{:S(2)}) %collective-permute-start.3) | collective-permute-done | bytes 8224 | tf_op jit(solution)/shard_map/ppermute | solution.py:583
  11.2 0.8 %shard_map.202 = (bf16[2304,256]{1,0:T(8,128)(2,1)S(1)}, f32[1152,128]{1,0:T(8,128)S(1)}, bf16[592,128]{1,0:T(8,128)(2,1)S(1)}) custom-call(f32[2304,256]{1,0:T(8,128)S(1)} %get-tuple-element.58.pre3, f32[2304,256]{1,0:T(8,128)S(1)} %get-tuple-element.63.e3, f32[8,256]{1,0:T(8,128)S(1)} %get-tuple-element.59.own3, f32[8,256]{1,0:T(8,128)S(1)} %collective-permute-done.2.rec3, ...), custom_call_target="tpu_custom_call" | custom-call | flops 150994944 | bytes 9232384 | tf_op jit(solution)/shard_map/pallas_call | solution.py:569
  12.0 0.4 %collective-permute-start.4 = (bf16[592,128]{1,0:T(8,128)(2,1)S(1)}, bf16[592,128]{1,0:T(8,128)(2,1)S(1)}, u32[]{:S(2)}, u32[]{:S(2)}) collective-permute-start(bf16[592,128]{1,0:T(8,128)(2,1)S(1)} %get-tuple-element.67.own5), channel_id=1, source_target_pairs={{0,1},{1,0},{2,3},{3,2},{4,5},{5,4},{6,7},{7,6},{8,9},{9,8},{10,11... | collective-permute-start | bytes 454664 | tf_op jit(solution)/shard_map/ppermute | solution.py:583
  12.4 0.4 shard_map.205.gwe
  12.8 0.7 %collective-permute-done.4.rec5 = bf16[592,128]{1,0:T(8,128)(2,1)S(1)} collective-permute-done((bf16[592,128]{1,0:T(8,128)(2,1)S(1)}, bf16[592,128]{1,0:T(8,128)(2,1)S(1)}, u32[]{:S(2)}, u32[]{:S(2)}) %collective-permute-start.4) | collective-permute-done | bytes 151584 | tf_op jit(solution)/shard_map/ppermute | solution.py:583
  13.4 1.1 %shard_map.203 = (bf16[2304,128]{1,0:T(8,128)(2,1)S(1)}, f32[1152,128]{1,0:T(8,128)S(1)}, f32[8,128]{1,0:T(8,128)S(1)}) custom-call(f32[1152,128]{1,0:T(8,128)S(1)} %get-tuple-element.55.pre2, f32[1152,128]{1,0:T(8,128)S(1)} %get-tuple-element.66.e2, bf16[592,128]{1,0:T(8,128)(2,1)S(1)} %get-tuple-element.67.own5, ...), custom_call_target="tpu_custom_call" | custom-call | flops 339738624 | bytes 4902912 | tf_op jit(solution)/shard_map/pallas_call | solution.py:569
  14.6 0.3 collective-permute-start.5
  14.9 0.9 %shard_map.204.gwd = bf16[320,128]{1,0:T(8,128)(2,1)S(1)} custom-call(bf16[2304,128]{1,0:T(8,128)(2,1)S(1)} %get-tuple-element.72.ext, bf16[2304,128]{1,0:T(8,128)(2,1)S(1)} %get-tuple-element.73.dext), custom_call_target="tpu_custom_call" | custom-call | flops 339738624 | bytes 1343488 | tf_op jit(solution)/shard_map/pallas_call | solution.py:569
  15.8 0.0 collective-permute-done.5.rec6
  15.8 0.4 %shard_map.206 = (bf16[1152,128]{1,0:T(8,128)(2,1)S(1)}, bf16[304,128]{1,0:T(8,128)(2,1)S(1)}, bf16[304,128]{1,0:T(8,128)(2,1)S(1)}) custom-call(f32[1152,128]{1,0:T(8,128)S(1)} %get-tuple-element.50.pre1, f32[1152,128]{1,0:T(8,128)S(1)} %get-tuple-element.70.e1, f32[8,128]{1,0:T(8,128)S(1)} %get-tuple-element.71.own6, ...), custom_call_target="tpu_custom_call" | custom-call | flops 150994944 | bytes 3739648 | tf_op jit(solution)/shard_map/pallas_call | solution.py:569
  16.3 0.3 collective-permute-start.6
  16.6 1.0 %collective-permute-done.6 = bf16[304,128]{1,0:T(8,128)(2,1)S(1)} collective-permute-done((bf16[304,128]{1,0:T(8,128)(2,1)S(1)}, bf16[304,128]{1,0:T(8,128)(2,1)S(1)}, u32[]{:S(2)}, u32[]{:S(2)}) %collective-permute-start.6) | collective-permute-done | bytes 77856 | tf_op jit(solution)/shard_map/ppermute | solution.py:583
  17.6 3.7 %collective-permute-start.9 = (bf16[304,128]{1,0:T(8,128)(2,1)S(1)}, bf16[304,128]{1,0:T(8,128)(2,1)S(1)}, u32[]{:S(2)}, u32[]{:S(2)}) collective-permute-start(bf16[304,128]{1,0:T(8,128)(2,1)S(1)} %add_convert_fusion.2), channel_id=1, source_target_pairs={{0,6},{1,25},{2,4},{3,27},{4,2},{5,29},{6,0},{7,31},{8,14},{9,17},... | collective-permute-start | bytes 233480 | tf_op jit(solution)/shard_map/ppermute | solution.py:607
  21.4 0.5 %collective-permute-start.8 = (bf16[304,128]{1,0:T(8,128)(2,1)S(1)}, bf16[304,128]{1,0:T(8,128)(2,1)S(1)}, u32[]{:S(2)}, u32[]{:S(2)}) collective-permute-start(bf16[304,128]{1,0:T(8,128)(2,1)S(1)} %add_convert_fusion.2), channel_id=1, source_target_pairs={{0,4},{1,17},{2,6},{3,19},{4,0},{5,21},{6,2},{7,23},{8,12},{9,25},... | collective-permute-start | bytes 233480 | tf_op jit(solution)/shard_map/ppermute | solution.py:607
  21.9 0.1 collective-permute-start.7
  22.0 1.7 %collective-permute-done.9 = bf16[304,128]{1,0:T(8,128)(2,1)S(1)} collective-permute-done((bf16[304,128]{1,0:T(8,128)(2,1)S(1)}, bf16[304,128]{1,0:T(8,128)(2,1)S(1)}, u32[]{:S(2)}, u32[]{:S(2)}) %collective-permute-start.9) | collective-permute-done | bytes 77856 | tf_op jit(solution)/shard_map/ppermute | solution.py:607
  23.7 2.0 %collective-permute-done.8 = bf16[304,128]{1,0:T(8,128)(2,1)S(1)} collective-permute-done((bf16[304,128]{1,0:T(8,128)(2,1)S(1)}, bf16[304,128]{1,0:T(8,128)(2,1)S(1)}, u32[]{:S(2)}, u32[]{:S(2)}) %collective-permute-start.8) | collective-permute-done | bytes 77856 | tf_op jit(solution)/shard_map/ppermute | solution.py:607
  25.8 0.5 %collective-permute-done.7 = bf16[304,128]{1,0:T(8,128)(2,1)S(1)} collective-permute-done((bf16[304,128]{1,0:T(8,128)(2,1)S(1)}, bf16[304,128]{1,0:T(8,128)(2,1)S(1)}, u32[]{:S(2)}, u32[]{:S(2)}) %collective-permute-start.7) | collective-permute-done | bytes 77856 | tf_op jit(solution)/shard_map/ppermute | solution.py:607
  26.3 3.7 %collective-permute-start.12 = (bf16[304,128]{1,0:T(8,128)(2,1)S(1)}, bf16[304,128]{1,0:T(8,128)(2,1)S(1)}, u32[]{:S(2)}, u32[]{:S(2)}) collective-permute-start(bf16[304,128]{1,0:T(8,128)(2,1)S(1)} %add_convert_fusion.1), channel_id=1, source_target_pairs={{0,24},{1,7},{2,26},{3,5},{4,28},{5,3},{6,30},{7,1},{8,16},{9,15},... | collective-permute-start | bytes 233480 | tf_op jit(solution)/shard_map/ppermute | solution.py:607
  30.0 0.0 collective-permute-start.11
  30.0 0.8 %collective-permute-start.10 = (bf16[304,128]{1,0:T(8,128)(2,1)S(1)}, bf16[304,128]{1,0:T(8,128)(2,1)S(1)}, u32[]{:S(2)}, u32[]{:S(2)}) collective-permute-start(bf16[304,128]{1,0:T(8,128)(2,1)S(1)} %add_convert_fusion.1), channel_id=1, source_target_pairs={{0,8},{1,3},{2,10},{3,1},{4,12},{5,7},{6,14},{7,5},{8,0},{9,11},{1... | collective-permute-start | bytes 233480 | tf_op jit(solution)/shard_map/ppermute | solution.py:607
  30.8 1.9 %collective-permute-done.12 = bf16[304,128]{1,0:T(8,128)(2,1)S(1)} collective-permute-done((bf16[304,128]{1,0:T(8,128)(2,1)S(1)}, bf16[304,128]{1,0:T(8,128)(2,1)S(1)}, u32[]{:S(2)}, u32[]{:S(2)}) %collective-permute-start.12) | collective-permute-done | bytes 77856 | tf_op jit(solution)/shard_map/ppermute | solution.py:607
  32.6 2.6 %collective-permute-done.11 = bf16[304,128]{1,0:T(8,128)(2,1)S(1)} collective-permute-done((bf16[304,128]{1,0:T(8,128)(2,1)S(1)}, bf16[304,128]{1,0:T(8,128)(2,1)S(1)}, u32[]{:S(2)}, u32[]{:S(2)}) %collective-permute-start.11) | collective-permute-done | bytes 77856 | tf_op jit(solution)/shard_map/ppermute | solution.py:607
  35.3 0.0 collective-permute-done.10
  35.3 0.1 collective-permute-start.13
  35.4 1.7 %shard_map.199 = bf16[2304,256]{1,0:T(8,128)(2,1)} custom-call(f32[2304,256]{1,0:T(8,128)S(1)} %get-tuple-element.58.pre3, f32[8,256]{1,0:T(8,128)S(1)} %get-tuple-element.59.own3, f32[8,256]{1,0:T(8,128)S(1)} %collective-permute-done.2.rec3, f32[8,256]{1,0:T(8,128)S(1)} %get-tuple-element.53.prm, f32[2304,256]{1,0:T(8,128)S(1)} %get-tuple-element.61.im_half), custom_call_target="tpu_custom_call" | custom-call | flops 5898240 | bytes 7102464 | tf_op jit(solution)/shard_map/pallas_call | solution.py:569
  37.1 1.5 %shard_map.207 = bf16[2304,256]{1,0:T(8,128)(2,1)} custom-call(bf16[1152,128]{1,0:T(8,128)(2,1)S(1)} %get-tuple-element.76.dh1, bf16[64,256]{1,0:T(8,128)(2,1)S(1)} %get-tuple-element.77.w, f32[2304,256]{1,0:T(8,128)S(1)} %get-tuple-element.63.e3), custom_call_target="tpu_custom_call" | custom-call | flops 150994944 | bytes 5046272 | tf_op jit(solution)/shard_map/pallas_call | solution.py:569
  38.6 0.0 collective-permute-done.13.refs_1_
  38.6 0.9 %shard_map.208 = (f32[64,256]{1,0:T(8,128)}, f32[9,64,64]{2,1,0:T(8,128)}, f32[64,256]{1,0:T(8,128)}, f32[1,64]{1,0:T(1,128)}, f32[1,64]{1,0:T(1,128)}, /*index=...) custom-call(bf16[304,128]{1,0:T(8,128)(2,1)S(1)} %add_convert_fusion.refs_0_, ...), custom_call_target="tpu_custom_call" | custom-call | bytes 437248 | tf_op jit(solution)/shard_map/pallas_call | solution.py:569
  (14 shorter events, 0.1 us)
Async XLA Ops:
  0.6 2.7 %copy-start.3 = (f32[256]{0:T(256)S(1)}, f32[256]{0:T(256)}, u32[]{:S(2)}) copy-start(f32[256]{0:T(256)} %param.20) | copy-start | bytes 3076
  0.7 2.7 %copy-start.2 = (f32[256]{0:T(256)S(1)}, f32[256]{0:T(256)}, u32[]{:S(2)}) copy-start(f32[256]{0:T(256)} %param.19) | copy-start | bytes 3076
  0.7 2.7 %copy-start.7 = (f32[64]{0:T(128)S(1)}, f32[64]{0:T(128)}, u32[]{:S(2)}) copy-start(f32[64]{0:T(128)} %param.18) | copy-start | bytes 772
  0.7 2.7 %copy-start.6 = (f32[64]{0:T(128)S(1)}, f32[64]{0:T(128)}, u32[]{:S(2)}) copy-start(f32[64]{0:T(128)} %param.17) | copy-start | bytes 772
  0.7 2.7 %copy-start.5 = (f32[64]{0:T(128)S(1)}, f32[64]{0:T(128)}, u32[]{:S(2)}) copy-start(f32[64]{0:T(128)} %param.16) | copy-start | bytes 772
  0.7 2.7 %copy-start.4 = (f32[64]{0:T(128)S(1)}, f32[64]{0:T(128)}, u32[]{:S(2)}) copy-start(f32[64]{0:T(128)} %param.15) | copy-start | bytes 772
  0.7 2.7 %copy-start.1 = (bf16[64,256]{1,0:T(8,128)(2,1)S(1)}, bf16[64,256]{1,0:T(8,128)(2,1)}, u32[]{:S(2)}) copy-start(bf16[64,256]{1,0:T(8,128)(2,1)} %we.1) | copy-start | bytes 98308
  2.8 1.5 %collective-permute-start = (bf16[304,128]{1,0:T(8,128)(2,1)S(1)}, bf16[304,128]{1,0:T(8,128)(2,1)S(1)}, u32[]{:S(2)}, u32[]{:S(2)}) collective-permute-start(bf16[304,128]{1,0:T(8,128)(2,1)S(1)} %get-tuple-element.51.own1), channel_id=1, source_target_pairs={{0,1},{1,0},{2,3},{3,2},{4,5},{5,4},{6,7},{7,6},{8,9},{9,8},{10,11... | collective-permute-start | bytes 233480 | tf_op jit(solution)/shard_map/ppermute | solution.py:583
  3.5 4.4 %copy-start = (bf16[1,8,288,256]{3,2,1,0:T(8,128)(2,1)S(1)}, bf16[1,8,288,256]{3,2,1,0:T(8,128)(2,1)}, u32[]{:S(2)}) copy-start(bf16[1,8,288,256]{3,2,1,0:T(8,128)(2,1)} %param.21) | copy-start | bytes 3538948
  5.5 1.2 %collective-permute-start.1 = (f32[8,128]{1,0:T(8,128)S(1)}, f32[8,128]{1,0:T(8,128)S(1)}, u32[]{:S(2)}, u32[]{:S(2)}) collective-permute-start(f32[8,128]{1,0:T(8,128)S(1)} %get-tuple-element.56.own2), channel_id=1, source_target_pairs={{0,1},{1,0},{2,3},{3,2},{4,5},{5,4},{6,7},{7,6},{8,9},{9,8},{10,11... | collective-permute-start | bytes 12296 | tf_op jit(solution)/shard_map/ppermute | solution.py:583
  7.5 1.2 %collective-permute-start.2 = (f32[8,256]{1,0:T(8,128)S(1)}, f32[8,256]{1,0:T(8,128)S(1)}, u32[]{:S(2)}, u32[]{:S(2)}) collective-permute-start(f32[8,256]{1,0:T(8,128)S(1)} %get-tuple-element.59.own3), channel_id=1, source_target_pairs={{0,1},{1,0},{2,3},{3,2},{4,5},{5,4},{6,7},{7,6},{8,9},{9,8},{10,11... | collective-permute-start | bytes 24584 | tf_op jit(solution)/shard_map/ppermute | solution.py:583
  10.0 1.2 %collective-permute-start.3 = (f32[8,256]{1,0:T(8,128)S(1)}, f32[8,256]{1,0:T(8,128)S(1)}, u32[]{:S(2)}, u32[]{:S(2)}) collective-permute-start(f32[8,256]{1,0:T(8,128)S(1)} %get-tuple-element.64.own4), channel_id=1, source_target_pairs={{0,1},{1,0},{2,3},{3,2},{4,5},{5,4},{6,7},{7,6},{8,9},{9,8},{10,11... | collective-permute-start | bytes 24584 | tf_op jit(solution)/shard_map/ppermute | solution.py:583
  12.0 1.4 %collective-permute-start.4 = (bf16[592,128]{1,0:T(8,128)(2,1)S(1)}, bf16[592,128]{1,0:T(8,128)(2,1)S(1)}, u32[]{:S(2)}, u32[]{:S(2)}) collective-permute-start(bf16[592,128]{1,0:T(8,128)(2,1)S(1)} %get-tuple-element.67.own5), channel_id=1, source_target_pairs={{0,1},{1,0},{2,3},{3,2},{4,5},{5,4},{6,7},{7,6},{8,9},{9,8},{10,11... | collective-permute-start | bytes 454664 | tf_op jit(solution)/shard_map/ppermute | solution.py:583
  14.6 1.3 %collective-permute-start.5 = (f32[8,128]{1,0:T(8,128)S(1)}, f32[8,128]{1,0:T(8,128)S(1)}, u32[]{:S(2)}, u32[]{:S(2)}) collective-permute-start(f32[8,128]{1,0:T(8,128)S(1)} %get-tuple-element.71.own6), channel_id=1, source_target_pairs={{0,1},{1,0},{2,3},{3,2},{4,5},{5,4},{6,7},{7,6},{8,9},{9,8},{10,11... | collective-permute-start | bytes 12296 | tf_op jit(solution)/shard_map/ppermute | solution.py:583
  16.3 1.3 %collective-permute-start.6 = (bf16[304,128]{1,0:T(8,128)(2,1)S(1)}, bf16[304,128]{1,0:T(8,128)(2,1)S(1)}, u32[]{:S(2)}, u32[]{:S(2)}) collective-permute-start(bf16[304,128]{1,0:T(8,128)(2,1)S(1)} %get-tuple-element.79), channel_id=1, source_target_pairs={{0,1},{1,0},{2,3},{3,2},{4,5},{5,4},{6,7},{7,6},{8,9},{9,8},{10,11... | collective-permute-start | bytes 233480 | tf_op jit(solution)/shard_map/ppermute | solution.py:583
  17.6 6.1 %collective-permute-start.9 = (bf16[304,128]{1,0:T(8,128)(2,1)S(1)}, bf16[304,128]{1,0:T(8,128)(2,1)S(1)}, u32[]{:S(2)}, u32[]{:S(2)}) collective-permute-start(bf16[304,128]{1,0:T(8,128)(2,1)S(1)} %add_convert_fusion.2), channel_id=1, source_target_pairs={{0,6},{1,25},{2,4},{3,27},{4,2},{5,29},{6,0},{7,31},{8,14},{9,17},... | collective-permute-start | bytes 233480 | tf_op jit(solution)/shard_map/ppermute | solution.py:607
  21.4 4.4 %collective-permute-start.8 = (bf16[304,128]{1,0:T(8,128)(2,1)S(1)}, bf16[304,128]{1,0:T(8,128)(2,1)S(1)}, u32[]{:S(2)}, u32[]{:S(2)}) collective-permute-start(bf16[304,128]{1,0:T(8,128)(2,1)S(1)} %add_convert_fusion.2), channel_id=1, source_target_pairs={{0,4},{1,17},{2,6},{3,19},{4,0},{5,21},{6,2},{7,23},{8,12},{9,25},... | collective-permute-start | bytes 233480 | tf_op jit(solution)/shard_map/ppermute | solution.py:607
  21.9 4.4 %collective-permute-start.7 = (bf16[304,128]{1,0:T(8,128)(2,1)S(1)}, bf16[304,128]{1,0:T(8,128)(2,1)S(1)}, u32[]{:S(2)}, u32[]{:S(2)}) collective-permute-start(bf16[304,128]{1,0:T(8,128)(2,1)S(1)} %add_convert_fusion.2), channel_id=1, source_target_pairs={{0,2},{1,9},{2,0},{3,11},{4,6},{5,13},{6,4},{7,15},{8,10},{9,1},{1... | collective-permute-start | bytes 233480 | tf_op jit(solution)/shard_map/ppermute | solution.py:607
  26.3 6.3 %collective-permute-start.12 = (bf16[304,128]{1,0:T(8,128)(2,1)S(1)}, bf16[304,128]{1,0:T(8,128)(2,1)S(1)}, u32[]{:S(2)}, u32[]{:S(2)}) collective-permute-start(bf16[304,128]{1,0:T(8,128)(2,1)S(1)} %add_convert_fusion.1), channel_id=1, source_target_pairs={{0,24},{1,7},{2,26},{3,5},{4,28},{5,3},{6,30},{7,1},{8,16},{9,15},... | collective-permute-start | bytes 233480 | tf_op jit(solution)/shard_map/ppermute | solution.py:607
  30.0 5.3 %collective-permute-start.11 = (bf16[304,128]{1,0:T(8,128)(2,1)S(1)}, bf16[304,128]{1,0:T(8,128)(2,1)S(1)}, u32[]{:S(2)}, u32[]{:S(2)}) collective-permute-start(bf16[304,128]{1,0:T(8,128)(2,1)S(1)} %add_convert_fusion.1), channel_id=1, source_target_pairs={{0,16},{1,5},{2,18},{3,7},{4,20},{5,1},{6,22},{7,3},{8,24},{9,13},... | collective-permute-start | bytes 233480 | tf_op jit(solution)/shard_map/ppermute | solution.py:607
  30.0 5.3 %collective-permute-start.10 = (bf16[304,128]{1,0:T(8,128)(2,1)S(1)}, bf16[304,128]{1,0:T(8,128)(2,1)S(1)}, u32[]{:S(2)}, u32[]{:S(2)}) collective-permute-start(bf16[304,128]{1,0:T(8,128)(2,1)S(1)} %add_convert_fusion.1), channel_id=1, source_target_pairs={{0,8},{1,3},{2,10},{3,1},{4,12},{5,7},{6,14},{7,5},{8,0},{9,11},{1... | collective-permute-start | bytes 233480 | tf_op jit(solution)/shard_map/ppermute | solution.py:607
  35.3 3.3 %collective-permute-start.13 = (bf16[304,128]{1,0:T(8,128)(2,1)S(1)}, bf16[304,128]{1,0:T(8,128)(2,1)S(1)}, u32[]{:S(2)}, u32[]{:S(2)}) collective-permute-start(bf16[304,128]{1,0:T(8,128)(2,1)S(1)} %add_convert_fusion.refs_0_), channel_id=1, source_target_pairs={{0,1},{1,0},{2,3},{3,2},{4,5},{5,4},{6,7},{7,6},{8,9},{9,8},{10,11... | collective-permute-start | bytes 233480 | tf_op jit(solution)/shard_map/ppermute | solution.py:583
